TPU v7x, 256 devices: a whole 4x4x8 slice. The times are simulated.
256 devices in a mesh: mem: 8 (over y, x_lo), grid: 32 (over z, x_hi, core).
Axes of the slice: x: 4 (x_hi: 2, x_lo: 2; x = x_hi * 2 + x_lo), y: 4, z: 8, core: 2. Of those that a mesh axis runs over, the one named last changes fastest.
Arguments:
- ens_state: bfloat16 [80, 512, 512], P('mem', 'grid'), may hold values from -6 to 6
- obs_prior: bfloat16 [80, 12288, 128], P('mem', 'grid'), may hold values from -6 to 6
- obs_value: float32 [12288, 128], P('grid'), may hold values from -6 to 6
- obs_prec: float32 [12288, 128], P('grid'), may hold values from 0.01 to 0.2
- obs_len: int32 [12288], P('grid'), may hold values from 1 to 128, as said below
- pair_block: int32 [512, 256], P('grid'), may hold values from 0 to 12287, as said below
- obs_pos: float32 [12288, 128], P('grid'), may hold values from 0 to 512, as said below
Outputs:
- analysis: bfloat16 [80, 512, 512], P('mem', 'grid')
Inputs may be any that keep to these rules, and one draw needn't show every extreme that they name: `obs_len`: count of valid slots of each observation block; slots at or past it are padding. Row b lists 256 distinct observation blocks; for each, pair_block[b,p] // 384 - b // 16 is -1, 0 or 1 modulo 12288 // 384. `obs_pos`: positions along the cyclic band of 512 state blocks.
All inputs are finite; a program needn't handle non-finite values. Where the computation divides by a largest or mean magnitude, that divisor is 1e-20 or more.
Results may differ from a plain program's by a relative error of at most 0.0058.
Values may be sent and summed in bfloat16 or wider, within the bound.
No kernel may reach another device: no remote copies, remote signals or barrier semaphores. Data moves between devices by JAX's collectives and lax.ppermute only.
A program may use at most 128 MiB of HBM per device.

v0:
```python
import math

import jax
import jax.numpy as jnp
from jax import lax
from jax.sharding import PartitionSpec as P

NSIT = 3
LOCR = 8


inflation = 1.1


def extended(block, sides, width):
    for axis, dim in sides:
        count = lax.axis_size(axis)
        forward = [(i, i + 1) for i in range(count - 1)]
        forward.append((count - 1, 0))
        backward = [(target, source) for source, target in forward]
        low = lax.ppermute(
            lax.slice_in_dim(block, block.shape[dim] - width, None, axis=dim), axis, forward
        )
        high = lax.ppermute(lax.slice_in_dim(block, 0, width, axis=dim), axis, backward)
        block = jnp.concatenate([low, block, high], axis=dim)
    return block


def finish(gram_matrix, forcing):
    members = gram_matrix.shape[0]
    highest = lax.Precision.HIGHEST
    identity = jnp.eye(members, dtype=jnp.float32)
    system = gram_matrix + (members - 1) / inflation * identity
    bound_sum = jnp.max(jnp.sum(jnp.abs(system), axis=1))
    y_iter = system / bound_sum
    z_iter = identity
    for sweep in range(NSIT):
        factor = 1.5 * identity - 0.5 * jnp.dot(z_iter, y_iter, precision=highest)
        y_iter = jnp.dot(y_iter, factor, precision=highest)
        z_iter = jnp.dot(factor, z_iter, precision=highest)
    root_inv = z_iter / jnp.sqrt(bound_sum)
    mean_weight = jnp.dot(
        root_inv, jnp.dot(root_inv, forcing, precision=highest), precision=highest
    )
    return (math.sqrt(members - 1) * root_inv + mean_weight[:, None]).astype(jnp.bfloat16)


def block_terms(window, aux_window, block_ids, center, nb_total):
    chosen = jnp.take(window, block_ids, axis=1)
    departure = jnp.take(aux_window[0], block_ids, axis=0)
    precision_obs = jnp.take(aux_window[1], block_ids, axis=0)
    position = jnp.take(aux_window[2], block_ids, axis=0)
    distance = jnp.abs(position - center)
    distance = jnp.minimum(distance, nb_total - distance)
    relative = distance / LOCR
    weight = precision_obs * jnp.exp(-0.5 * relative * relative)
    scaled = (chosen.astype(jnp.float32) * weight).astype(jnp.bfloat16)
    gram_matrix = lax.dot_general(
        scaled, chosen, (((1, 2), (1, 2)), ((), ())), preferred_element_type=jnp.float32
    )
    forcing = jnp.einsum(
        "ipk,pk->i", scaled.astype(jnp.float32), departure, precision=lax.Precision.HIGHEST
    )
    return (gram_matrix, forcing)


def run_groups(func, items, count):
    group = math.gcd(count, 2)
    shaped = jax.tree.map(lambda arr: arr.reshape((count // group, group) + arr.shape[1:]), items)
    result = lax.map(lambda part_items: jax.vmap(func)(*part_items), shaped)
    return result.reshape((count,) + result.shape[2:])


def per_device(ens_state, obs_prior, obs_value, obs_prec, obs_len, pair_block, obs_pos):
    mem_count = lax.axis_size("mem")
    grid_count = lax.axis_size("grid")
    members = mem_count * ens_state.shape[0]
    blocks_dev = ens_state.shape[1]
    obs_blocks = obs_prior.shape[1]
    owned = blocks_dev // mem_count
    obs_sums, state_sums = lax.psum(
        (
            jnp.sum(obs_prior, axis=0, dtype=jnp.float32),
            jnp.sum(ens_state, axis=0, dtype=jnp.float32),
        ),
        "mem",
    )
    obs_mean = obs_sums / members
    state_mean = state_sums / members
    valid = lax.broadcasted_iota(jnp.int32, obs_mean.shape, 1) < obs_len[:, None]
    perturb = jnp.where(valid, obs_prior.astype(jnp.float32) - obs_mean, 0.0).astype(jnp.bfloat16)
    departure = jnp.where(valid, obs_value - obs_mean, 0.0)
    aux_window = extended(jnp.stack([departure, obs_prec, obs_pos]), (("grid", 1),), obs_blocks)
    first = lax.axis_index("mem") * owned
    grid_pos = lax.axis_index("grid")
    total_obs = obs_blocks * grid_count
    nb_total = blocks_dev * grid_count
    all_members = lax.all_gather(perturb, "mem", axis=0, tiled=True)
    window = extended(all_members, (("grid", 1),), obs_blocks)
    my_pairs = lax.dynamic_slice_in_dim(pair_block, first, owned, 0)
    local_ids = (my_pairs - (grid_pos - 1) * obs_blocks) % total_obs
    centers = (grid_pos * blocks_dev + first + jnp.arange(owned, dtype=jnp.int32)).astype(
        jnp.float32
    ) + 0.5

    def solve_one(block_ids, center):
        gram_matrix, forcing = block_terms(window, aux_window, block_ids, center, nb_total)
        return finish(gram_matrix, forcing)

    transforms = run_groups(solve_one, (local_ids, centers), owned)
    deviation = (ens_state.astype(jnp.float32) - state_mean).astype(jnp.bfloat16)
    rows_back = lax.all_to_all(transforms, "mem", split_axis=1, concat_axis=0, tiled=True)
    product = lax.dot_general(
        rows_back, deviation, (((1,), (0,)), ((0,), (1,))), preferred_element_type=jnp.float32
    )
    summed = lax.psum_scatter(
        jnp.transpose(product, (1, 0, 2)), "mem", scatter_dimension=0, tiled=True
    )
    return (state_mean[None, :, :] + summed).astype(jnp.bfloat16)


def solution(mesh):
    placed = (
        P("mem", "grid", None),
        P("mem", "grid", None),
        P("grid", None),
        P("grid", None),
        P("grid"),
        P("grid", None),
        P("grid", None),
    )
    return jax.shard_map(
        per_device, mesh=mesh, in_specs=placed, out_specs=P("mem", "grid", None), check_vma=False
    )
```

profile of v0, /device:TPU:101, one launch (start us, length us, event | category | flops | bytes accessed | tf_op | source)
XLA Modules:
  0.0 632.8 jit_solution(14787413260775118740)
XLA Ops:
  6.5 2.1 convert_reduce_fusion
  8.6 0.0 all-reduce.2.cloned.1.call-update
  8.7 0.0 all-gather.2.cloned.1.call-start
  8.7 0.8 iota_compare_fusion
  9.5 76.3 %all-reduce.2.cloned.1.call-done = f32[384,128]{1,0:T(8,128)} async-done(((f32[384,128]{1,0:T(8,128)}), f32[384,128]{1,0:T(8,128)}) %all-reduce.2.cloned.1.call-update) | async-done | bytes 196624 | tf_op jit(solution)/shard_map/psum | solution.py:81
  85.9 1.2 select_bitcast_fusion
  87.0 2.6 fusion.9
  89.6 0.0 all-gather.2.cloned.1.call-update
  89.6 165.2 %all-gather.2.cloned.1.call-done = bf16[80,384,128]{2,1,0:T(8,128)(2,1)} async-done(((bf16[10,384,128]{2,1,0:T(8,128)(2,1)}), bf16[80,384,128]{2,1,0:T(8,128)(2,1)}) %all-gather.2.cloned.1.call-update) | async-done | bytes 7864336 | tf_op jit(solution)/shard_map/all_gather | solution.py:98
  254.7 11.5 %copy.33 = bf16[80,384,128]{2,0,1:T(8,128)(2,1)} copy(bf16[80,384,128]{2,1,0:T(8,128)(2,1)} %all-gather.2.cloned.1.call-done) | data formatting | bytes 15728640 | tf_op jit(solution)/shard_map/all_gather | solution.py:98
  266.2 0.8 collective-permute-start.1
  267.0 4.5 collective-permute-start
  271.6 0.1 copy.36
  271.7 0.7 compare_and_fusion
  272.5 0.1 collective-permute-start.3
  272.6 5.3 collective-permute-start.2
  278.0 107.7 %psum.14 = f32[16,512]{1,0:T(8,128)S(1)} all-reduce(f32[16,512]{1,0:T(8,128)S(1)} %convert_reduce_fusion.1), channel_id=1, replica_groups=mesh['mem'=8,'grid'=32] {'mem'}, use_global_device_ids=true, to_apply=%region_1.0 | all-reduce | flops 8192 | bytes 65536 | tf_op jit(solution)/shard_map/psum | solution.py:81
  385.8 0.1 pad_maximum_fusion.1
  385.9 0.1 slice_bitcast_fusion
  386.0 1.0 gather_fusion.3
  387.1 1.0 gather_fusion.2
  388.1 1.0 gather_fusion.1
  389.1 0.2 broadcast_select_fusion.3
  389.4 17.2 %pad_maximum_fusion = bf16[80,1152,128]{2,0,1:T(8,128)(2,1)} fusion(bf16[80,384,128]{2,0,1:T(8,128)(2,1)} %collective-permute-done.1, bf16[80,384,128]{2,0,1:T(8,128)(2,1)} %copy.33, bf16[80,384,128]{2,0,1:T(8,128)(2,1)} %collective-permute-done), kind=kLoop, calls=%fused_computation.4 | loop fusion | flops 23592960 | bytes 47185920 | tf_op jit(solution)/shard_map/concatenate | solution.py:25
  406.5 22.3 %gather_fusion = bf16[512,80,128]{2,1,0:T(8,128)(2,1)} fusion(bf16[80,1152,128]{2,0,1:T(8,128)(2,1)} %pad_maximum_fusion, s32[1024]{0:T(1024)S(1)} %pad_clamp_fusion), kind=kCustom, calls=%fused_computation.3 | custom fusion | bytes 20973568 | tf_op jit(solution)/shard_map/while/body/eval_jaxpr/vmap(jit(_take))/gather | solution.py:49
  428.9 11.8 %abs_reduce_fusion = (f32[2,80]{1,0:T(2,128)S(1)}, f32[2,80,80]{1,2,0:T(8,128)S(1)}) fusion(f32[80,80]{0,1:T(8,128)S(1)} %copy.36, bf16[2,256,80,128]{3,2,1,0:T(8,128)(2,1)} %bitcast.93, pred[2,256]{1,0:T(4,128)(4,1)S(1)} %get-tuple-element.16, f32[2,256,128]{2,1,0:T(8,128)S(1)} %get-tuple-element.32), kind=kOutput, calls=%fused_computation.51 | convolution fusion | flops 865113472 | bytes 10825856 | tf_op jit(solution)/shard_map/while/body/eval_jaxpr/vmap()/dot_general | solution.py:58
  440.7 0.1 reduce_max.10
  440.8 0.3 fusion.19
  441.2 0.2 fusion.27
  441.3 0.4 fusion.30
  441.7 0.2 fusion.17
  442.0 0.2 fusion.33
  442.2 0.2 fusion.34
  442.4 11.3 %fusion.20 = f32[2,80,1]{1,2,0:T(1,128)S(1)} fusion(f32[2,256,128,1]{2,3,1,0:T(1,128)S(1)} %bitcast.103, f32[2,256,128]{2,1,0:T(8,128)S(1)} %get-tuple-element.32, bf16[2,256,80,128]{3,2,1,0:T(8,128)(2,1)} %bitcast.94, pred[2,256]{1,0:T(4,128)(4,1)S(1)} %get-tuple-element.16), kind=kOutput, calls=%fused_computation.31 | convolution fusion | flops 83886080 | bytes 11011200 | tf_op jit(solution)/shard_map/while/body/eval_jaxpr/vmap(ipk,pk->i)/dot_general | solution.py:61
  453.7 0.2 fusion.16
  454.0 0.2 convolution_divide_fusion
  454.2 0.2 convolution_bitcast_fusion.1
  454.4 0.2 fusion.35
  454.7 0.1 add_convert_fusion.1
  454.8 0.6 copy.39
  455.4 3.3 all-to-all-start
  458.8 0.0 reduce-scatter.2.cloned.1.call-start
  458.9 5.0 all-to-all-done
  463.9 0.5 convolution_bitcast_fusion
  464.4 3.0 copy.42
  467.4 0.0 reduce-scatter.2.cloned.1.call-update
  467.5 157.2 %reduce-scatter.2.cloned.1.call-done = f32[10,16,512]{2,1,0:T(8,128)} async-done(((f32[80,16,512]{2,1,0:T(8,128)}), f32[10,16,512]{2,1,0:T(8,128)}) %reduce-scatter.2.cloned.1.call-update) | async-done | bytes 327696 | tf_op jit(solution)/shard_map/reduce_scatter | solution.py:116
  624.6 1.7 add_convert_fusion
  (22 shorter events, 0.2 us)
Async XLA Ops:
  6.5 265.9 %copy-start.2 = (bf16[10,16,512]{2,1,0:T(8,128)(2,1)S(1)}, bf16[10,16,512]{2,1,0:T(8,128)(2,1)}, u32[]{:S(2)}) copy-start(bf16[10,16,512]{2,1,0:T(8,128)(2,1)} %param.9) | copy-start | bytes 491524
  6.5 265.9 %copy-start = (f32[384,128]{1,0:T(8,128)S(1)}, f32[384,128]{1,0:T(8,128)}, u32[]{:S(2)}) copy-start(f32[384,128]{1,0:T(8,128)} %param.15) | copy-start | bytes 589828
  6.5 265.9 %copy-start.1 = (f32[384,128]{1,0:T(8,128)S(1)}, f32[384,128]{1,0:T(8,128)}, u32[]{:S(2)}) copy-start(f32[384,128]{1,0:T(8,128)} %param.12) | copy-start | bytes 589828
  6.5 79.3 %all-reduce.2.cloned.1.call-start = ((), (), s32[]{:S(2)}) async-start(), calls=%async_computation.2 | async-start | bytes 393216 | tf_op jit(solution)/shard_map/psum | solution.py:81
  8.7 246.1 %all-gather.2.cloned.1.call-start = ((), (), s32[]{:S(2)}) async-start(), calls=%async_computation.3 | async-start | bytes 8847360 | tf_op jit(solution)/shard_map/all_gather | solution.py:98
  266.2 123.1 %collective-permute-start.1 = (bf16[80,384,128]{2,0,1:T(8,128)(2,1)}, bf16[80,384,128]{2,0,1:T(8,128)(2,1)}, u32[]{:S(2)}, u32[]{:S(2)}) collective-permute-start(bf16[80,384,128]{2,0,1:T(8,128)(2,1)} %copy.33), channel_id=1, source_target_pairs={{1,0},{2,1},{3,2},{4,3},{5,4},{6,5},{7,6},{8,7},{9,8},{10,9},{11,1... | collective-permute-start | bytes 23592968 | tf_op jit(solution)/shard_map/ppermute | solution.py:24
  267.0 122.3 %collective-permute-start = (bf16[80,384,128]{2,0,1:T(8,128)(2,1)}, bf16[80,384,128]{2,0,1:T(8,128)(2,1)}, u32[]{:S(2)}, u32[]{:S(2)}) collective-permute-start(bf16[80,384,128]{2,0,1:T(8,128)(2,1)} %copy.33), channel_id=1, source_target_pairs={{0,1},{1,2},{2,3},{3,4},{4,5},{5,6},{6,7},{7,8},{8,9},{9,10},{10,1... | collective-permute-start | bytes 23592968 | tf_op jit(solution)/shard_map/ppermute | solution.py:21
  272.5 113.2 %collective-permute-start.3 = (f32[3,384,128]{2,1,0:T(8,128)S(1)}, f32[3,384,128]{2,1,0:T(8,128)S(1)}, u32[]{:S(2)}, u32[]{:S(2)}) collective-permute-start(f32[3,384,128]{2,1,0:T(8,128)S(1)} %pad_maximum_fusion.2), channel_id=1, source_target_pairs={{1,0},{2,1},{3,2},{4,3},{5,4},{6,5},{7,6},{8,7},{9,8},{10,9},{11,1... | collective-permute-start | bytes 1769480 | tf_op jit(solution)/shard_map/ppermute | solution.py:24
  272.6 113.1 %collective-permute-start.2 = (f32[3,384,128]{2,1,0:T(8,128)S(1)}, f32[3,384,128]{2,1,0:T(8,128)S(1)}, u32[]{:S(2)}, u32[]{:S(2)}) collective-permute-start(f32[3,384,128]{2,1,0:T(8,128)S(1)} %pad_maximum_fusion.2), channel_id=1, source_target_pairs={{0,1},{1,2},{2,3},{3,4},{4,5},{5,6},{6,7},{7,8},{8,9},{9,10},{10,1... | collective-permute-start | bytes 1769480 | tf_op jit(solution)/shard_map/ppermute | solution.py:21
  455.4 8.4 %all-to-all-start = ((bf16[2,80,80]{2,0,1:T(2,128)(2,1)}), bf16[2,80,80]{2,0,1:T(2,128)(2,1)S(1)}, u32[]{:S(2)}, u32[]{:S(2)}) async-start(bf16[2,80,80]{2,0,1:T(2,128)(2,1)} %copy.39), calls=%async_computation | async-start | bytes 81920 | tf_op jit(solution)/shard_map/all_to_all | solution.py:112
  458.8 165.8 %reduce-scatter.2.cloned.1.call-start = ((), (), s32[]{:S(2)}) async-start(), calls=%async_computation.4 | async-start | bytes 2949120 | tf_op jit(solution)/shard_map/reduce_scatter | solution.py:116
Sparse Core Ops, SparseCore 0:
  9.9 75.8 all-reduce.1
  89.7 164.9 all-gather.1
  467.6 157.0 reduce-scatter.1
where the time goes:
time: 636 us; the launch traced here: 633 us
  waiting for transfers between devices  404 us (64%)
  blocking collectives  108 us (17%)
  local copies, waits for them, and re-layouts  40.8 us (6%)
  other arithmetic  26.8 us (4%)
  matrix products  26.1 us (4%)
  starting transfers between devices  14.2 us (2%)
  between operations  13.4 us (2%)
    all_gather x1, waiting for transfers between devices, per_device(): all_members = lax.all_gather(perturb, 'mem', axis=0, tiled=True)  165 us
    reduce_scatter x1, waiting for transfers between devices, per_device(): lax.psum_scatter(jnp.transpose(product, (1, 0, 2)), 'mem', scatter_dimens...  157 us
    psum x1, blocking collectives, per_device(): lax.psum((jnp.sum(obs_prior, axis=0, dtype=jnp.float32), jnp.sum(ens_stat...  108 us
    psum x1, waiting for transfers between devices, per_device(): lax.psum((jnp.sum(obs_prior, axis=0, dtype=jnp.float32), jnp.sum(ens_stat...  76.3 us
    gather x1, local copies, waits for them, and re-layouts, block_terms(): chosen = jnp.take(window, block_ids, axis=1)  22.3 us
    concatenate x2, other arithmetic, extended(): block = jnp.concatenate([low, block, high], axis=dim)  17.3 us
  transfers between devices with their start and end apart: 8, of which 4 were waited for; matrix products, arithmetic and copies ran while one was open for 1% of the time, Pallas kernels for 0%

commit v1 on v0

v1 whole, which is shorter than its diff:
```python
import functools
import math

import jax
import jax.numpy as jnp
from jax import lax
from jax.experimental import pallas as pl
from jax.experimental.pallas import tpu as pltpu
from jax.sharding import PartitionSpec as P

NSIT = 3
LOCR = 8
LANES = 128

inflation = 1.1


def shift(value, axis, step):
    count = lax.axis_size(axis)
    return lax.ppermute(value, axis, [(i, (i + step) % count) for i in range(count)])


def weight_kernel(nb_total, obs, base_ref, pairs_ref, centers_ref, prec_ref, pos_ref, out_ref):
    pairs = pairs_ref[...] - base_ref[0]
    centers = centers_ref[...]
    for o in range(obs):
        hit = jnp.max(jnp.where(pairs == o, 1.0, 0.0), axis=1, keepdims=True)
        gap = jnp.abs(pos_ref[o : o + 1, :] - centers)
        distance = jnp.minimum(gap, nb_total - gap)
        relative = distance * (1.0 / LOCR)
        weight = prec_ref[o : o + 1, :] * jnp.exp(-0.5 * relative * relative)
        out_ref[:, o * LANES : (o + 1) * LANES] = jnp.where(hit > 0.0, weight, 0.0)


def gram_kernel(members, obs, rows, blocks, chunk, batch, prior_ref, len_ref, value_ref, w_ref, out_ref, dev_ref, d_ref, acc_ref):
    total = prior_ref[0].astype(jnp.float32)
    for i in range(1, members):
        total = total + prior_ref[i].astype(jnp.float32)
    mean = total / members
    valid = lax.broadcasted_iota(jnp.int32, mean.shape, 1) < len_ref[...]
    for i in range(members):
        dev_ref[i * obs : (i + 1) * obs, :] = jnp.where(
            valid, prior_ref[i].astype(jnp.float32) - mean, 0.0
        )
    departure = jnp.where(valid, value_ref[...] - mean, 0.0)
    high = departure.astype(jnp.bfloat16).astype(jnp.float32)
    dev_ref[members * obs : (members + 1) * obs, :] = high
    dev_ref[(members + 1) * obs : (members + 2) * obs, :] = departure - high
    dev_ref[(members + 2) * obs : rows * obs, :] = jnp.zeros(((rows - members - 2) * obs, LANES), jnp.float32)
    for o in range(obs):
        d_ref[:, o * LANES : (o + 1) * LANES] = dev_ref[pl.ds(o, rows, stride=obs), :].astype(jnp.bfloat16)
    acc_ref[...] = jnp.zeros(acc_ref.shape, jnp.float32)
    width = chunk * LANES

    def step(c, carry):
        start = pl.multiple_of(c * width, width)
        full = d_ref[:, pl.ds(start, width)]
        d = full[:members]
        for b0 in range(0, blocks, batch):
            parts = []
            for b in range(b0, b0 + batch):
                w = jnp.broadcast_to(w_ref[b : b + 1, pl.ds(start, width)], (16, width)).astype(jnp.bfloat16)
                parts.append((d.reshape(members // 16, 16, width) * w[None]).reshape(members, width))
            scaled = jnp.concatenate(parts, axis=0)
            got = lax.dot_general(scaled, full, (((1,), (1,)), ((), ())), preferred_element_type=jnp.float32)
            acc_ref[b0 * members : (b0 + batch) * members, :] += got
        return carry

    lax.fori_loop(0, obs // chunk, step, 0)
    got = acc_ref[...]
    force = got[:, members : members + 1] + got[:, members + 1 : members + 2]
    high = force.astype(jnp.bfloat16).astype(jnp.float32)
    lane = lax.broadcasted_iota(jnp.int32, got.shape, 1)
    got = jnp.where(lane == members, high, jnp.where(lane == members + 1, force - high, got))
    out_ref[...] = got.astype(jnp.bfloat16)


def finish(gram_matrix, forcing):
    members = gram_matrix.shape[0]
    highest = lax.Precision.HIGHEST
    identity = jnp.eye(members, dtype=jnp.float32)
    system = gram_matrix + (members - 1) / inflation * identity
    bound_sum = jnp.max(jnp.sum(jnp.abs(system), axis=1))
    y_iter = system / bound_sum
    z_iter = identity
    for sweep in range(NSIT):
        factor = 1.5 * identity - 0.5 * jnp.dot(z_iter, y_iter, precision=highest)
        y_iter = jnp.dot(y_iter, factor, precision=highest)
        z_iter = jnp.dot(factor, z_iter, precision=highest)
    root_inv = z_iter / jnp.sqrt(bound_sum)
    mean_weight = jnp.dot(
        root_inv, jnp.dot(root_inv, forcing, precision=highest), precision=highest
    )
    return (math.sqrt(members - 1) * root_inv + mean_weight[:, None]).astype(jnp.bfloat16)


def per_device(ens_state, obs_prior, obs_value, obs_prec, obs_len, pair_block, obs_pos):
    mem_count = lax.axis_size("mem")
    grid_count = lax.axis_size("grid")
    local = ens_state.shape[0]
    members = mem_count * local
    blocks_dev = ens_state.shape[1]
    obs_blocks = obs_prior.shape[1]
    owned = blocks_dev // mem_count
    obs = obs_blocks // mem_count
    nb_total = blocks_dev * grid_count
    mem_pos = lax.axis_index("mem")
    grid_pos = lax.axis_index("grid")

    prior = lax.all_to_all(obs_prior, "mem", split_axis=1, concat_axis=0, tiled=True)
    state = lax.all_to_all(ens_state, "mem", split_axis=1, concat_axis=0, tiled=True)
    from_low = shift(pair_block, "grid", 1)
    from_high = shift(pair_block, "grid", -1)

    blocks = 3 * blocks_dev
    pairs = jnp.stack([from_low, pair_block, from_high])
    pairs = pairs.reshape(3, mem_count, owned, -1).transpose(1, 0, 2, 3).reshape(blocks, -1)
    places = (grid_pos + jnp.arange(-1, 2, dtype=jnp.int32)) % grid_count
    ids = places[None, :, None] * blocks_dev + (
        jnp.arange(mem_count, dtype=jnp.int32)[:, None, None] * owned
        + jnp.arange(owned, dtype=jnp.int32)[None, None, :]
    )
    centers = ids.reshape(blocks, 1).astype(jnp.float32) + 0.5

    def mine(value):
        return lax.dynamic_slice_in_dim(value, mem_pos * obs, obs, 0)

    base = (grid_pos * obs_blocks + mem_pos * obs).reshape(1)
    vmem = pl.BlockSpec(memory_space=pltpu.VMEM)
    weights = pl.pallas_call(
        functools.partial(weight_kernel, float(nb_total), obs),
        out_shape=jax.ShapeDtypeStruct((blocks, obs * LANES), jnp.float32),
        in_specs=[pl.BlockSpec(memory_space=pltpu.SMEM), vmem, vmem, vmem, vmem],
        out_specs=vmem,
        name="weights",
    )(base, pairs, centers, mine(obs_prec), mine(obs_pos))

    rows = -(-(members + 2) // 16) * 16
    partial = pl.pallas_call(
        functools.partial(gram_kernel, members, obs, rows, blocks, 2, 8),
        out_shape=jax.ShapeDtypeStruct((blocks * members, rows), jnp.bfloat16),
        in_specs=[vmem, vmem, vmem, vmem],
        out_specs=vmem,
        scratch_shapes=[
            pltpu.VMEM((rows * obs, LANES), jnp.float32),
            pltpu.VMEM((rows, obs * LANES), jnp.bfloat16),
            pltpu.VMEM((blocks * members, rows), jnp.float32),
        ],
        name="gram",
    )(prior, mine(obs_len)[:, None], mine(obs_value), weights)

    partial = partial.reshape(mem_count, 3 * owned, members, rows)
    swapped = lax.all_to_all(partial, "mem", split_axis=0, concat_axis=0, tiled=True)
    summed = jnp.sum(swapped.reshape(mem_count, 3, owned, members, rows), axis=0, dtype=jnp.float32)
    total = summed[1] + shift(summed[0], "grid", -1) + shift(summed[2], "grid", 1)
    forcing = total[:, :, members] + total[:, :, members + 1]
    transforms = jax.vmap(finish)(total[:, :, :members], forcing)

    state = state.astype(jnp.float32)
    state_mean = jnp.sum(state, axis=0) / members
    deviation = (state - state_mean).astype(jnp.bfloat16)
    product = lax.dot_general(
        transforms, deviation, (((1,), (0,)), ((0,), (1,))), preferred_element_type=jnp.float32
    )
    analysis = (state_mean[:, None, :] + product).astype(jnp.bfloat16)
    return lax.all_to_all(
        jnp.transpose(analysis, (1, 0, 2)), "mem", split_axis=0, concat_axis=1, tiled=True
    )


def solution(mesh):
    placed = (
        P("mem", "grid", None),
        P("mem", "grid", None),
        P("grid", None),
        P("grid", None),
        P("grid"),
        P("grid", None),
        P("grid", None),
    )
    return jax.shard_map(
        per_device, mesh=mesh, in_specs=placed, out_specs=P("mem", "grid", None), check_vma=False
    )
```

time: 636 us -> 108 us (0.17)
  waiting for transfers between devices: 404 us -> 38.1 us
  blocking collectives: 108 us -> 8.49 us
  local copies, waits for them, and re-layouts: 40.8 us -> 11.2 us
  other arithmetic: 26.8 us -> 1.09 us
  matrix products: 26.1 us -> 2.58 us
  Pallas kernels: 0 us -> 23.5 us
  between operations: 13.4 us -> 0.22 us
  starting transfers between devices: 14.2 us -> 22.5 us
    all_gather x1 -> x0, waiting for transfers between devices: 165 us -> none  [per_device(): all_members = lax.all_gather(perturb, 'mem', axis=0, tiled=True)]
    reduce_scatter x1 -> x0, waiting for transfers between devices: 157 us -> none  [per_device(): lax.psum_scatter(jnp.transpose(product, (1, 0, 2)), 'mem', scatter_dimens...]
    psum x1 -> x0, blocking collectives: 108 us -> none  [per_device(): lax.psum((jnp.sum(obs_prior, axis=0, dtype=jnp.float32), jnp.sum(ens_stat...]
    psum x1 -> x0, waiting for transfers between devices: 76.3 us -> none  [per_device(): lax.psum((jnp.sum(obs_prior, axis=0, dtype=jnp.float32), jnp.sum(ens_stat...]
    all_to_all x1 -> x3, waiting for transfers between devices: 4.97 us -> 30.7 us  [the longest x1 15.5 us: per_device(): lax.all_to_all(obs_prior, 'mem', split_axis=1, concat_axis=0, tiled=True)]
    gather x4 -> x0, local copies, waits for them, and re-layouts: 25.5 us -> none  [the longest x1 22.3 us: block_terms(): chosen = jnp.take(window, block_ids, axis=1)]
    pallas_call x0 -> x2, Pallas kernels: none -> 23.5 us  [the longest x1 21 us: per_device(): pl.pallas_call(functools.partial(gram_kernel, members, obs, rows, blocks,...]
    dot_general x3 -> x1, matrix products: 23.7 us -> 0.34 us  [per_device(): lax.dot_general(transforms, deviation, (((1,), (0,)), ((0,), (1,))), pref...]
  transfers between devices with their start and end apart: 8 -> 7, of which waited for: 4 -> 4; matrix products, arithmetic and copies ran while one was open for 1% -> 10% of each run, Pallas kernels for 0% -> 22%
where the time goes in v1:
time: 108 us
  waiting for transfers between devices  38.1 us (35%)
  Pallas kernels  23.5 us (22%)
  starting transfers between devices  22.5 us (21%)
  local copies, waits for them, and re-layouts  11.2 us (10%)
  blocking collectives  8.49 us (8%)
  matrix products  2.58 us (2%)
  other arithmetic  1.09 us (1%)
    pallas_call x1, Pallas kernels, per_device(): pl.pallas_call(functools.partial(gram_kernel, members, obs, rows, blocks,...  21 us
    all_to_all x1, waiting for transfers between devices, per_device(): lax.all_to_all(obs_prior, 'mem', split_axis=1, concat_axis=0, tiled=True)  15.5 us
    all_to_all x1, waiting for transfers between devices, per_device(): lax.all_to_all(partial, 'mem', split_axis=0, concat_axis=0, tiled=True)  15.2 us
    ppermute x4, starting transfers between devices, shift(): lax.ppermute(value, axis, [(i, (i + step) % count) for i in range(count)])  9.12 us
    all_to_all x1, blocking collectives, per_device(): lax.all_to_all(jnp.transpose(analysis, (1, 0, 2)), 'mem', split_axis=0, c...  8.49 us
    ppermute x4, waiting for transfers between devices, shift(): lax.ppermute(value, axis, [(i, (i + step) % count) for i in range(count)])  7.34 us
    all_to_all x1, starting transfers between devices, per_device(): lax.all_to_all(partial, 'mem', split_axis=0, concat_axis=0, tiled=True)  5 us
    all_to_all x1, starting transfers between devices, per_device(): lax.all_to_all(obs_prior, 'mem', split_axis=1, concat_axis=0, tiled=True)  4.96 us
  transfers between devices with their start and end apart: 7, of which 4 were waited for; matrix products, arithmetic and copies ran while one was open for 10% of the time, Pallas kernels for 22%

profile of v1, /device:TPU:101, one launch (start us, length us, event | category | flops | bytes accessed | tf_op | source)
XLA Modules:
  0.0 107.5 jit_solution(13841883885307271097)
XLA Ops:
  0.0 0.7 collective-permute-start.1
  0.7 4.7 %collective-permute-start = (s32[16,256]{1,0:T(8,128)}, s32[16,256]{1,0:T(8,128)S(1)}, u32[]{:S(2)}, u32[]{:S(2)}) collective-permute-start(s32[16,256]{1,0:T(8,128)} %param.12), channel_id=1, source_target_pairs={{0,1},{1,2},{2,3},{3,4},{4,5},{5,6},{6,7},{7,8},{8,9},{9,10},{10,1... | collective-permute-start | bytes 49160 | tf_op jit(solution)/shard_map/ppermute | solution.py:20
  5.4 3.1 %copy.72 = bf16[10,384,128]{2,0,1:T(8,128)(2,1)} copy(bf16[10,384,128]{2,1,0:T(8,128)(2,1)} %param.8) | data formatting | bytes 1966080 | tf_op args[1]
  8.4 5.0 %all-to-all-start.1 = ((bf16[10,384,128]{2,0,1:T(8,128)(2,1)}), bf16[10,384,128]{2,0,1:T(8,128)(2,1)S(1)}, u32[]{:S(2)}, u32[]{:S(2)}) async-start(bf16[10,384,128]{2,0,1:T(8,128)(2,1)} %copy.72), calls=%async_computation.1 | async-start | bytes 3145728 | tf_op jit(solution)/shard_map/all_to_all | solution.py:110
  13.4 0.8 copy.70
  14.2 0.6 constant_dynamic-slice_fusion.2.value_ref
  14.8 1.4 %constant_dynamic-slice_fusion = (f32[48,128]{1,0:T(8,128)}, f32[48,128]{1,0:T(8,128)}) fusion(f32[384,128]{1,0:T(8,128)} %param.13, s32[]{:T(128)S(6)} %select_n.17, f32[384,128]{1,0:T(8,128)} %param.10), kind=kLoop, calls=%fused_computation.39 | loop fusion | bytes 98308 | tf_op jit(solution)/shard_map/dynamic_slice | solution.py:126
  16.2 0.1 iota_add_fusion
  16.3 0.1 convert_add_fusion
  16.4 15.5 %all-to-all-done.1 = bf16[10,384,128]{2,0,1:T(8,128)(2,1)S(1)} async-done(((bf16[10,384,128]{2,0,1:T(8,128)(2,1)}), bf16[10,384,128]{2,0,1:T(8,128)(2,1)S(1)}, u32[]{:S(2)}, u32[]{:S(2)}) %all-to-all-start.1) | async-done | bytes 983072 | tf_op jit(solution)/shard_map/all_to_all | solution.py:110
  31.9 3.4 %all-to-all-start = ((bf16[10,16,512]{2,0,1:T(8,128)(2,1)}), bf16[10,16,512]{2,0,1:T(8,128)(2,1)S(1)}, u32[]{:S(2)}, u32[]{:S(2)}) async-start(bf16[10,16,512]{2,0,1:T(8,128)(2,1)} %copy.70), calls=%async_computation | async-start | bytes 524288 | tf_op jit(solution)/shard_map/all_to_all | solution.py:111
  35.3 0.8 dynamic-slice_bitcast_fusion
  36.1 0.7 copy.78.len_ref
  36.8 0.7 add.150.centers_ref
  37.5 0.0 collective-permute-done.1
  37.5 0.7 reshape.134.pairs_ref
  38.2 2.5 %weights.1.w_ref = f32[48,6144]{1,0:T(8,128)} custom-call(s32[1]{0:T(128)} %bitcast.5.base_ref, s32[48,256]{1,0:T(8,128)} %reshape.134.pairs_ref, f32[48,1]{1,0:T(8,128)} %add.150.centers_ref, f32[48,128]{1,0:T(8,128)} %get-tuple-element.8.prec_ref, f32[48,128]{1,0:T(8,128)} %get-tuple-element.7.pos_ref), custom_call_target="tpu_custom_call" | custom-call | tf_op jit(solution)/shard_map/weights/pallas_call | solution.py:130
  40.7 1.2 %copy.73 = bf16[10,8,48,128]{3,2,0,1:T(8,128)(2,1)} copy(bf16[10,8,48,128]{3,0,2,1:T(8,128)(2,1)S(1)} %bitcast.59) | data formatting | bytes 1966080 | tf_op jit(solution)/shard_map/all_to_all | solution.py:110
  41.9 21.0 %gram.1 = bf16[3840,96]{1,0:T(8,128)(2,1)} custom-call(bf16[80,48,128]{2,1,0:T(8,128)(2,1)} %bitcast.61, s32[48,1]{1,0:T(8,128)} %copy.78.len_ref, f32[48,128]{1,0:T(8,128)} %constant_dynamic-slice_fusion.2.value_ref, f32[48,6144]{1,0:T(8,128)} %weights.1.w_ref), custom_call_target="tpu_custom_call" | custom-call | tf_op jit(solution)/shard_map/gram/pallas_call | solution.py:139
  62.9 0.0 all-to-all-done
  62.9 5.0 %all-to-all-start.2 = ((bf16[8,6,80,96]{3,2,1,0:T(8,128)(2,1)}), bf16[8,6,80,96]{3,2,1,0:T(8,128)(2,1)S(1)}, u32[]{:S(2)}, u32[]{:S(2)}) async-start(bf16[8,6,80,96]{3,2,1,0:T(8,128)(2,1)} %bitcast.60), calls=%async_computation.2 | async-start | bytes 1966080 | tf_op jit(solution)/shard_map/all_to_all | solution.py:153
  67.9 0.2 copy.79
  68.1 0.1 convert_reduce_fusion.1
  68.3 15.2 %all-to-all-done.2 = bf16[8,6,80,96]{3,2,1,0:T(8,128)(2,1)S(1)} async-done(((bf16[8,6,80,96]{3,2,1,0:T(8,128)(2,1)}), bf16[8,6,80,96]{3,2,1,0:T(8,128)(2,1)S(1)}, u32[]{:S(2)}, u32[]{:S(2)}) %all-to-all-start.2) | async-done | bytes 737312 | tf_op jit(solution)/shard_map/all_to_all | solution.py:153
  83.4 0.2 convert_reduce_fusion
  83.7 3.8 %collective-permute-start.3 = (f32[2,80,96]{2,1,0:T(8,128)S(1)}, f32[2,80,96]{2,1,0:T(8,128)S(1)}, u32[]{:S(2)}, u32[]{:S(2)}) collective-permute-start(f32[2,80,96]{2,1,0:T(8,128)S(1)} %get-tuple-element.6), channel_id=1, source_target_pairs={{0,1},{1,2},{2,3},{3,4},{4,5},{5,6},{6,7},{7,8},{8,9},{9,10},{10,1... | collective-permute-start | bytes 184328 | tf_op jit(solution)/shard_map/ppermute | solution.py:20
  87.4 0.0 collective-permute-start.2
  87.4 0.1 fusion.6
  87.6 1.3 %collective-permute-done.3 = f32[2,80,96]{2,1,0:T(8,128)S(1)} collective-permute-done((f32[2,80,96]{2,1,0:T(8,128)S(1)}, f32[2,80,96]{2,1,0:T(8,128)S(1)}, u32[]{:S(2)}, u32[]{:S(2)}) %collective-permute-start.3) | collective-permute-done | bytes 61472 | tf_op jit(solution)/shard_map/ppermute | solution.py:20
  88.9 6.0 %collective-permute-done.2 = f32[2,80,96]{2,1,0:T(8,128)S(1)} collective-permute-done((f32[2,80,96]{2,1,0:T(8,128)S(1)}, f32[2,80,96]{2,1,0:T(8,128)S(1)}, u32[]{:S(2)}, u32[]{:S(2)}) %collective-permute-start.2) | collective-permute-done | bytes 61472 | tf_op jit(solution)/shard_map/ppermute | solution.py:20
  94.9 0.1 abs_reduce_fusion
  95.0 0.1 reduce_max.9
  95.2 0.3 fusion.5
  95.4 0.2 fusion.16
  95.6 0.3 fusion.22
  95.9 0.2 fusion.3
  96.1 0.2 fusion.26
  96.3 0.2 fusion.27
  96.5 0.2 fusion.8
  96.7 0.2 fusion.2
  97.0 0.2 convolution_divide_fusion
  97.2 0.2 convolution_bitcast_fusion
  97.4 0.2 fusion.28
  97.7 0.3 fusion.1
  98.0 0.2 copy.82
  98.2 8.5 %all_to_all.50 = bf16[80,2,512]{2,1,0:T(2,128)(2,1)S(1)} all-to-all(bf16[80,2,512]{2,1,0:T(2,128)(2,1)S(1)} %copy.82), channel_id=1, replica_groups=mesh['mem'=8,'grid'=32] {'mem'}, dimensions={0} | all-to-all | bytes 327680 | tf_op jit(solution)/shard_map/all_to_all | solution.py:166
  106.7 0.1 copy.83
  106.8 0.7 all_to_all.45
  (21 shorter events, 0.2 us)
Async XLA Ops:
  0.0 14.2 %copy-start = (f32[384,128]{1,0:T(8,128)S(1)}, f32[384,128]{1,0:T(8,128)}, u32[]{:S(2)}) copy-start(f32[384,128]{1,0:T(8,128)} %param.9) | copy-start | bytes 589828
  0.0 37.5 %collective-permute-start.1 = (s32[16,256]{1,0:T(8,128)}, s32[16,256]{1,0:T(8,128)S(1)}, u32[]{:S(2)}, u32[]{:S(2)}) collective-permute-start(s32[16,256]{1,0:T(8,128)} %param.12), channel_id=1, source_target_pairs={{0,31},{1,0},{2,1},{3,2},{4,3},{5,4},{6,5},{7,6},{8,7},{9,8},{10,9... | collective-permute-start | bytes 49160 | tf_op jit(solution)/shard_map/ppermute | solution.py:20
  0.7 36.8 %collective-permute-start = (s32[16,256]{1,0:T(8,128)}, s32[16,256]{1,0:T(8,128)S(1)}, u32[]{:S(2)}, u32[]{:S(2)}) collective-permute-start(s32[16,256]{1,0:T(8,128)} %param.12), channel_id=1, source_target_pairs={{0,1},{1,2},{2,3},{3,4},{4,5},{5,6},{6,7},{7,8},{8,9},{9,10},{10,1... | collective-permute-start | bytes 49160 | tf_op jit(solution)/shard_map/ppermute | solution.py:20
  8.4 5.0 %copy-start.1 = (bf16[10,16,512]{2,1,0:T(8,128)(2,1)S(1)}, bf16[10,16,512]{2,1,0:T(8,128)(2,1)}, u32[]{:S(2)}) copy-start(bf16[10,16,512]{2,1,0:T(8,128)(2,1)} %param.7) | copy-start | bytes 491524
  8.4 27.7 %copy-start.2 = (s32[16,256]{1,0:T(8,128)S(1)}, s32[16,256]{1,0:T(8,128)}, u32[]{:S(2)}) copy-start(s32[16,256]{1,0:T(8,128)} %param.12) | copy-start | bytes 49156
  8.4 23.5 %all-to-all-start.1 = ((bf16[10,384,128]{2,0,1:T(8,128)(2,1)}), bf16[10,384,128]{2,0,1:T(8,128)(2,1)S(1)}, u32[]{:S(2)}, u32[]{:S(2)}) async-start(bf16[10,384,128]{2,0,1:T(8,128)(2,1)} %copy.72), calls=%async_computation.1 | async-start | bytes 3145728 | tf_op jit(solution)/shard_map/all_to_all | solution.py:110
  31.9 31.0 %all-to-all-start = ((bf16[10,16,512]{2,0,1:T(8,128)(2,1)}), bf16[10,16,512]{2,0,1:T(8,128)(2,1)S(1)}, u32[]{:S(2)}, u32[]{:S(2)}) async-start(bf16[10,16,512]{2,0,1:T(8,128)(2,1)} %copy.70), calls=%async_computation | async-start | bytes 524288 | tf_op jit(solution)/shard_map/all_to_all | solution.py:111
  62.9 20.5 %all-to-all-start.2 = ((bf16[8,6,80,96]{3,2,1,0:T(8,128)(2,1)}), bf16[8,6,80,96]{3,2,1,0:T(8,128)(2,1)S(1)}, u32[]{:S(2)}, u32[]{:S(2)}) async-start(bf16[8,6,80,96]{3,2,1,0:T(8,128)(2,1)} %bitcast.60), calls=%async_computation.2 | async-start | bytes 1966080 | tf_op jit(solution)/shard_map/all_to_all | solution.py:153
  83.7 5.2 %collective-permute-start.3 = (f32[2,80,96]{2,1,0:T(8,128)S(1)}, f32[2,80,96]{2,1,0:T(8,128)S(1)}, u32[]{:S(2)}, u32[]{:S(2)}) collective-permute-start(f32[2,80,96]{2,1,0:T(8,128)S(1)} %get-tuple-element.6), channel_id=1, source_target_pairs={{0,1},{1,2},{2,3},{3,4},{4,5},{5,6},{6,7},{7,8},{8,9},{9,10},{10,1... | collective-permute-start | bytes 184328 | tf_op jit(solution)/shard_map/ppermute | solution.py:20
  87.4 7.5 %collective-permute-start.2 = (f32[2,80,96]{2,1,0:T(8,128)S(1)}, f32[2,80,96]{2,1,0:T(8,128)S(1)}, u32[]{:S(2)}, u32[]{:S(2)}) collective-permute-start(f32[2,80,96]{2,1,0:T(8,128)S(1)} %get-tuple-element.5), channel_id=1, source_target_pairs={{0,31},{1,0},{2,1},{3,2},{4,3},{5,4},{6,5},{7,6},{8,7},{9,8},{10,9... | collective-permute-start | bytes 184328 | tf_op jit(solution)/shard_map/ppermute | solution.py:20

commit v2 on v1

v2 whole, which is shorter than its diff:
```python
import functools
import math

import jax
import jax.numpy as jnp
from jax import lax
from jax.experimental import pallas as pl
from jax.experimental.pallas import tpu as pltpu
from jax.sharding import PartitionSpec as P

NSIT = 3
LOCR = 8
LANES = 128

inflation = 1.1


def shift(value, axis, step):
    count = lax.axis_size(axis)
    return lax.ppermute(value, axis, [(i, (i + step) % count) for i in range(count)])


def pack_kernel(parts, size, src_ref, out_ref, sems):
    copies = [
        pltpu.make_async_copy(src_ref.at[:, m * size : (m + 1) * size, :], out_ref.at[m], sems.at[m])
        for m in range(parts)
    ]
    for copy in copies:
        copy.start()
    for copy in copies:
        copy.wait()


def weight_kernel(nb_total, obs, base_ref, pairs_ref, centers_ref, prec_ref, pos_ref, out_ref):
    pairs = pairs_ref[...] - base_ref[0]
    centers = centers_ref[...]
    for o in range(obs):
        hit = jnp.max(jnp.where(pairs == o, 1.0, 0.0), axis=1, keepdims=True)
        gap = jnp.abs(pos_ref[o : o + 1, :] - centers)
        distance = jnp.minimum(gap, nb_total - gap)
        relative = distance * (1.0 / LOCR)
        weight = prec_ref[o : o + 1, :] * jnp.exp(-0.5 * relative * relative)
        out_ref[:, o * LANES : (o + 1) * LANES] = jnp.where(hit > 0.0, weight, 0.0)


def accumulate(members, obs, first, blocks, chunk, batch, d_ref, w_ref, acc_ref):
    acc_ref[...] = jnp.zeros(acc_ref.shape, jnp.float32)
    width = chunk * LANES

    def step(c, carry):
        start = pl.multiple_of(c * width, width)
        full = d_ref[:, pl.ds(start, width)]
        d = full[:members].reshape(members // 16, 16, width)
        for b0 in range(0, blocks, batch):
            parts = []
            for b in range(b0, b0 + batch):
                row = w_ref[first + b : first + b + 1, pl.ds(start, width)]
                w = jnp.broadcast_to(row, (16, width)).astype(jnp.bfloat16)
                parts.append((d * w[None]).reshape(members, width))
            scaled = jnp.concatenate(parts, axis=0)
            acc_ref[b0 * members : (b0 + batch) * members, :] += lax.dot_general(
                scaled, full, (((1,), (1,)), ((), ())), preferred_element_type=jnp.float32
            )
        return carry

    lax.fori_loop(0, obs // chunk, step, 0)


def packed_system(members, blocks, acc_ref, out_ref):
    half = members // 2
    lane = lax.broadcasted_iota(jnp.int32, (half, LANES), 1)
    low = (lane == members + 2) | (lane == members + 3) | (lane >= LANES - half)
    for b in range(blocks):
        top = acc_ref[b * members : b * members + half, :]
        bottom = acc_ref[b * members + half : (b + 1) * members, :]
        out_ref[b * half : (b + 1) * half, :] = jnp.where(low, bottom, top).astype(out_ref.dtype)


def neighbour_kernel(members, obs, blocks, chunk, batch, prior_ref, len_ref, value_ref, w_ref, d_ref, low_ref, high_ref, dev_ref, acc_ref):
    half = members // 2
    total = prior_ref[0].astype(jnp.float32)
    for i in range(1, members):
        total = total + prior_ref[i].astype(jnp.float32)
    mean = total / members
    valid = lax.broadcasted_iota(jnp.int32, mean.shape, 1) < len_ref[...]
    for i in range(members):
        one = jnp.where(valid, prior_ref[i].astype(jnp.float32) - mean, 0.0)
        dev_ref[i * obs : (i + 1) * obs, :] = one
        if i >= half:
            at = LANES - members + i
            dev_ref[at * obs : (at + 1) * obs, :] = one
    departure = jnp.where(valid, value_ref[...] - mean, 0.0)
    high = departure.astype(jnp.bfloat16).astype(jnp.float32)
    for k in range(LANES - half - members):
        piece = (high, departure - high)[k % 2] if k < 4 else jnp.zeros(mean.shape, jnp.float32)
        dev_ref[(members + k) * obs : (members + k + 1) * obs, :] = piece
    for o in range(obs):
        d_ref[:, o * LANES : (o + 1) * LANES] = dev_ref[pl.ds(o, LANES, stride=obs), :].astype(jnp.bfloat16)
    for first, out_ref in ((0, low_ref), (2 * blocks, high_ref)):
        accumulate(members, obs, first, blocks, chunk, batch, d_ref, w_ref, acc_ref)
        packed_system(members, blocks, acc_ref, out_ref)


def own_kernel(members, obs, blocks, chunk, batch, d_ref, w_ref, out_ref, acc_ref):
    accumulate(members, obs, blocks, blocks, chunk, batch, d_ref, w_ref, acc_ref)
    packed_system(members, blocks, acc_ref, out_ref)


def finish_kernel(members, owned, parts, system_ref, state_ref, out_ref):
    half = members // 2
    highest = lax.Precision.HIGHEST
    total = system_ref[0].astype(jnp.float32)
    for m in range(1, parts):
        total = total + system_ref[m].astype(jnp.float32)
    rows = lax.broadcasted_iota(jnp.int32, (members, members), 0)
    cols = lax.broadcasted_iota(jnp.int32, (members, members), 1)
    identity = jnp.where(rows == cols, 1.0, 0.0)
    lane = lax.broadcasted_iota(jnp.int32, (half, LANES), 1)

    def dot(a, b):
        return jnp.dot(a, b, precision=highest, preferred_element_type=jnp.float32)

    y_iter, z_iter, bound, force = [], [], [], []
    for r in range(owned):
        part = total[r * half : (r + 1) * half]
        square = jnp.concatenate([part, jnp.zeros((LANES - half, LANES), jnp.float32)], axis=0)
        below = jnp.transpose(square)[half : 2 * half]
        right = pltpu.roll(part, members, 1)
        bottom = jnp.where(lane < half, below, right)
        system = jnp.concatenate([part, bottom], axis=0)[:, :members]
        system = system + (members - 1) / inflation * identity
        sums = jnp.sum(jnp.abs(system), axis=1, keepdims=True)
        bound.append(jnp.max(sums, axis=0, keepdims=True))
        y_iter.append(system / bound[r])
        f_top = part[:, members : members + 1] + part[:, members + 1 : members + 2]
        f_low = part[:, members + 2 : members + 3] + part[:, members + 3 : members + 4]
        force.append(jnp.concatenate([f_top, f_low], axis=0))
    for sweep in range(NSIT):
        if sweep == 0:
            factor = [1.5 * identity - 0.5 * y for y in y_iter]
            z_next = factor
        else:
            factor = [1.5 * identity - 0.5 * dot(z, y) for z, y in zip(z_iter, y_iter)]
            z_next = [dot(f, z) for f, z in zip(factor, z_iter)]
        if sweep + 1 < NSIT:
            y_iter = [dot(y, f) for y, f in zip(y_iter, factor)]
        z_iter = z_next
    for r in range(owned):
        root = z_iter[r] / jnp.sqrt(bound[r])
        first = dot(root, jnp.broadcast_to(force[r], (members, LANES)))
        shiftu = dot(root, first)[:, :1]
        transform = math.sqrt(members - 1) * root + shiftu
        state = state_ref[r].astype(jnp.float32)
        mean = jnp.sum(state, axis=0, keepdims=True) / members
        dev = (state - mean).astype(jnp.bfloat16)
        moved = jnp.dot(jnp.transpose(transform).astype(jnp.bfloat16), dev, preferred_element_type=jnp.float32)
        out_ref[r] = (mean + moved).astype(jnp.bfloat16)


def per_device(ens_state, obs_prior, obs_value, obs_prec, obs_len, pair_block, obs_pos):
    mem_count = lax.axis_size("mem")
    grid_count = lax.axis_size("grid")
    local = ens_state.shape[0]
    members = mem_count * local
    blocks_dev = ens_state.shape[1]
    obs_blocks = obs_prior.shape[1]
    owned = blocks_dev // mem_count
    obs = obs_blocks // mem_count
    half = members // 2
    nb_total = blocks_dev * grid_count
    mem_pos = lax.axis_index("mem")
    grid_pos = lax.axis_index("grid")
    vmem = pl.BlockSpec(memory_space=pltpu.VMEM)
    anywhere = pl.BlockSpec(memory_space=pl.ANY)

    packed = pl.pallas_call(
        functools.partial(pack_kernel, mem_count, obs),
        out_shape=jax.ShapeDtypeStruct((mem_count, local, obs, LANES), obs_prior.dtype),
        in_specs=[anywhere],
        out_specs=anywhere,
        scratch_shapes=[pltpu.SemaphoreType.DMA((mem_count,))],
        name="pack",
    )(obs_prior)
    prior = lax.all_to_all(packed, "mem", split_axis=0, concat_axis=0, tiled=True)
    prior = prior.reshape(members, obs, LANES)
    state = lax.all_to_all(ens_state, "mem", split_axis=1, concat_axis=0, tiled=True)
    from_low = shift(pair_block, "grid", 1)
    from_high = shift(pair_block, "grid", -1)

    pairs = jnp.concatenate([from_low, pair_block, from_high], axis=0)
    places = (grid_pos + jnp.arange(-1, 2, dtype=jnp.int32)) % grid_count
    ids = places[:, None] * blocks_dev + jnp.arange(blocks_dev, dtype=jnp.int32)[None, :]
    blocks = 3 * blocks_dev
    centers = ids.reshape(blocks, 1).astype(jnp.float32) + 0.5

    def mine(value):
        return lax.dynamic_slice_in_dim(value, mem_pos * obs, obs, 0)

    base = (grid_pos * obs_blocks + mem_pos * obs).reshape(1)
    weights = pl.pallas_call(
        functools.partial(weight_kernel, float(nb_total), obs),
        out_shape=jax.ShapeDtypeStruct((blocks, obs * LANES), jnp.float32),
        in_specs=[pl.BlockSpec(memory_space=pltpu.SMEM), vmem, vmem, vmem, vmem],
        out_specs=vmem,
        name="weights",
    )(base, pairs, centers, mine(obs_prec), mine(obs_pos))

    chunk, batch = 6, 4
    system = jax.ShapeDtypeStruct((blocks_dev * half, LANES), jnp.bfloat16)
    d_all, to_low, to_high = pl.pallas_call(
        functools.partial(neighbour_kernel, members, obs, blocks_dev, chunk, batch),
        out_shape=(jax.ShapeDtypeStruct((LANES, obs * LANES), jnp.bfloat16), system, system),
        in_specs=[vmem, vmem, vmem, vmem],
        out_specs=(vmem, vmem, vmem),
        scratch_shapes=[
            pltpu.VMEM((LANES * obs, LANES), jnp.float32),
            pltpu.VMEM((blocks_dev * members, LANES), jnp.float32),
        ],
        name="neighbours",
    )(prior, mine(obs_len)[:, None], mine(obs_value), weights)
    from_high = shift(to_low, "grid", -1)
    from_low = shift(to_high, "grid", 1)
    own = pl.pallas_call(
        functools.partial(own_kernel, members, obs, blocks_dev, chunk, batch),
        out_shape=jax.ShapeDtypeStruct(system.shape, jnp.float32),
        in_specs=[vmem, vmem],
        out_specs=vmem,
        scratch_shapes=[pltpu.VMEM((blocks_dev * members, LANES), jnp.float32)],
        name="own",
    )(d_all, weights)
    partial = own + from_low.astype(jnp.float32) + from_high.astype(jnp.float32)
    partial = partial.astype(jnp.bfloat16).reshape(mem_count, owned * half, LANES)
    swapped = lax.all_to_all(partial, "mem", split_axis=0, concat_axis=0, tiled=True)
    analysis = pl.pallas_call(
        functools.partial(finish_kernel, members, owned, mem_count),
        out_shape=jax.ShapeDtypeStruct((owned, members, ens_state.shape[2]), jnp.bfloat16),
        in_specs=[vmem, vmem],
        out_specs=vmem,
        name="finish",
    )(swapped, jnp.transpose(state, (1, 0, 2)))
    return lax.all_to_all(
        jnp.transpose(analysis, (1, 0, 2)), "mem", split_axis=0, concat_axis=1, tiled=True
    )


def solution(mesh):
    placed = (
        P("mem", "grid", None),
        P("mem", "grid", None),
        P("grid", None),
        P("grid", None),
        P("grid"),
        P("grid", None),
        P("grid", None),
    )
    return jax.shard_map(
        per_device, mesh=mesh, in_specs=placed, out_specs=P("mem", "grid", None), check_vma=False
    )
```

time: 108 us -> 116 us (1.074)
  the two profiles are of different devices: /device:TPU:101 before, /device:TPU:2 now
where the time goes in v2:
time: 116 us; the launch traced here: 115 us
  Pallas kernels  60.4 us (52%)
  starting transfers between devices  29.1 us (25%)
  local copies, waits for them, and re-layouts  9.4 us (8%)
  blocking collectives  9.29 us (8%)
  waiting for transfers between devices  4.74 us (4%)
  other arithmetic  2.41 us (2%)
    pallas_call x1, Pallas kernels, per_device(): pl.pallas_call(functools.partial(pack_kernel, mem_count, obs), out_shape=...  31 us
    pallas_call x1, Pallas kernels, per_device(): pl.pallas_call(functools.partial(neighbour_kernel, members, obs, blocks_d...  14.8 us
    ppermute x4, starting transfers between devices, shift(): lax.ppermute(value, axis, [(i, (i + step) % count) for i in range(count)])  11.7 us
    all_to_all x1, blocking collectives, per_device(): lax.all_to_all(jnp.transpose(analysis, (1, 0, 2)), 'mem', split_axis=0, c...  9.29 us
    pallas_call x1, Pallas kernels, per_device(): pl.pallas_call(functools.partial(own_kernel, members, obs, blocks_dev, ch...  8.05 us
    all_to_all x1, starting transfers between devices, per_device(): lax.all_to_all(packed, 'mem', split_axis=0, concat_axis=0, tiled=True)  5.94 us
    all_to_all x1, starting transfers between devices, per_device(): lax.all_to_all(partial, 'mem', split_axis=0, concat_axis=0, tiled=True)  5.7 us
    all_to_all x1, starting transfers between devices, per_device(): lax.all_to_all(ens_state, 'mem', split_axis=1, concat_axis=0, tiled=True)  5.69 us
  transfers between devices with their start and end apart: 7, of which 1 were waited for; matrix products, arithmetic and copies ran while one was open for 7% of the time, Pallas kernels for 9%

profile of v2, /device:TPU:2, one launch (start us, length us, event | category | flops | bytes accessed | tf_op | source)
XLA Modules:
  0.0 115.4 jit_solution(12023914201258208169)
XLA Ops:
  0.0 0.0 copy-start
  0.0 0.0 copy-start.4
  0.0 31.0 %pack.1 = bf16[8,10,48,128]{3,2,1,0:T(8,128)(2,1)} custom-call(bf16[10,384,128]{2,1,0:T(8,128)(2,1)} %src_ref.1), custom_call_target="tpu_custom_call" | custom-call | tf_op jit(solution)/shard_map/pack/pallas_call | solution.py:176
  31.0 5.9 %all-to-all-start = ((bf16[8,10,48,128]{3,2,1,0:T(8,128)(2,1)}), bf16[8,10,48,128]{3,2,1,0:T(8,128)(2,1)S(1)}, u32[]{:S(2)}, u32[]{:S(2)}) async-start(bf16[8,10,48,128]{3,2,1,0:T(8,128)(2,1)} %pack.1), calls=%async_computation | async-start | bytes 1966080 | tf_op jit(solution)/shard_map/all_to_all | solution.py:184
  36.9 0.0 copy-done.4
  36.9 0.0 collective-permute-start
  36.9 6.4 %collective-permute-start.1 = (s32[16,256]{1,0:T(8,128)S(1)}, s32[16,256]{1,0:T(8,128)S(1)}, u32[]{:S(2)}, u32[]{:S(2)}) collective-permute-start(s32[16,256]{1,0:T(8,128)S(1)} %copy-done.4), channel_id=1, source_target_pairs={{0,31},{1,0},{2,1},{3,2},{4,3},{5,4},{6,5},{7,6},{8,7},{9,8},{10,9... | collective-permute-start | bytes 49160 | tf_op jit(solution)/shard_map/ppermute | solution.py:20
  43.3 0.0 copy-done
  43.3 0.6 constant_dynamic-slice_fusion.2.value_ref
  43.9 1.4 %constant_dynamic-slice_fusion = (f32[48,128]{1,0:T(8,128)}, f32[48,128]{1,0:T(8,128)}) fusion(f32[384,128]{1,0:T(8,128)} %param.13, s32[]{:T(128)S(6)} %select_n.17, f32[384,128]{1,0:T(8,128)} %param.10), kind=kLoop, calls=%fused_computation.7 | loop fusion | bytes 98308 | tf_op jit(solution)/shard_map/dynamic_slice | solution.py:197
  45.3 0.1 convert_add_fusion
  45.4 0.8 dynamic-slice_bitcast_fusion
  46.1 0.7 add.86.centers_ref
  46.8 0.7 copy.24.len_ref
  47.5 0.0 collective-permute-done
  47.5 0.0 collective-permute-done.1
  47.5 0.6 pad_add_fusion.pairs_ref
  48.2 0.0 copy-start.3
  48.2 2.6 %weights.1.w_ref = f32[48,6144]{1,0:T(8,128)} custom-call(s32[1]{0:T(128)} %bitcast.2.base_ref, s32[48,256]{1,0:T(8,128)} %pad_add_fusion.pairs_ref, f32[48,1]{1,0:T(8,128)} %add.86.centers_ref, f32[48,128]{1,0:T(8,128)} %get-tuple-element.12.prec_ref, f32[48,128]{1,0:T(8,128)} %get-tuple-element.11.pos_ref), custom_call_target="tpu_custom_call" | custom-call | tf_op jit(solution)/shard_map/weights/pallas_call | solution.py:200
  50.7 0.0 all-to-all-done
  50.7 0.0 copy-start.1
  50.7 1.0 copy-done.1
  51.7 14.8 %neighbours.1 = (bf16[128,6144]{1,0:T(8,128)(2,1)}, bf16[640,128]{1,0:T(8,128)(2,1)}, bf16[640,128]{1,0:T(8,128)(2,1)}) custom-call(bf16[80,48,128]{2,1,0:T(8,128)(2,1)} %bitcast.16, s32[48,1]{1,0:T(8,128)} %copy.24.len_ref, f32[48,128]{1,0:T(8,128)} %constant_dynamic-slice_fusion.2.value_ref, f32[48,6144]{1,0:T(8,128)} %weights.1.w_ref), custom_call_target="tpu_custom_call" | custom-call | tf_op jit(solution)/shard_map/neighbours/pallas_call | solution.py:210
  66.5 2.8 %collective-permute-start.2 = (bf16[640,128]{1,0:T(8,128)(2,1)}, bf16[640,128]{1,0:T(8,128)(2,1)S(1)}, u32[]{:S(2)}, u32[]{:S(2)}) collective-permute-start(bf16[640,128]{1,0:T(8,128)(2,1)} %get-tuple-element.9), channel_id=1, source_target_pairs={{0,1},{1,2},{2,3},{3,4},{4,5},{5,6},{6,7},{7,8},{8,9},{9,10},{10,1... | collective-permute-start | bytes 491528 | tf_op jit(solution)/shard_map/ppermute | solution.py:20
  69.3 2.6 %collective-permute-start.3 = (bf16[640,128]{1,0:T(8,128)(2,1)}, bf16[640,128]{1,0:T(8,128)(2,1)S(1)}, u32[]{:S(2)}, u32[]{:S(2)}) collective-permute-start(bf16[640,128]{1,0:T(8,128)(2,1)} %get-tuple-element.10), channel_id=1, source_target_pairs={{0,31},{1,0},{2,1},{3,2},{4,3},{5,4},{6,5},{7,6},{8,7},{9,8},{10,9... | collective-permute-start | bytes 491528 | tf_op jit(solution)/shard_map/ppermute | solution.py:20
  71.9 0.0 copy-done.3
  71.9 0.8 copy.25
  72.7 5.7 %all-to-all-start.2 = ((bf16[10,16,512]{2,0,1:T(8,128)(2,1)}), bf16[10,16,512]{2,0,1:T(8,128)(2,1)S(1)}, u32[]{:S(2)}, u32[]{:S(2)}) async-start(bf16[10,16,512]{2,0,1:T(8,128)(2,1)} %copy.25), calls=%async_computation.2 | async-start | bytes 524288 | tf_op jit(solution)/shard_map/all_to_all | solution.py:186
  78.4 8.1 %own.1 = f32[640,128]{1,0:T(8,128)} custom-call(bf16[128,6144]{1,0:T(8,128)(2,1)} %get-tuple-element.8.d_ref, f32[48,6144]{1,0:T(8,128)} %weights.1.w_ref), custom_call_target="tpu_custom_call" | custom-call | tf_op jit(solution)/shard_map/own/pallas_call | solution.py:223
  86.4 0.0 collective-permute-done.2
  86.4 0.0 collective-permute-done.3
  86.4 1.7 %add_convert_fusion = bf16[640,128]{1,0:T(8,128)(2,1)} fusion(bf16[640,128]{1,0:T(8,128)(2,1)S(1)} %collective-permute-done.3, f32[640,128]{1,0:T(8,128)} %own.1, bf16[640,128]{1,0:T(8,128)(2,1)S(1)} %collective-permute-done.2), kind=kLoop, calls=%fused_computation | loop fusion | flops 409600 | bytes 819200 | tf_op jit(solution)/shard_map/convert_element_type | solution.py:232
  88.1 0.0 all-to-all-done.2
  88.1 5.7 %all-to-all-start.1 = ((bf16[8,80,128]{2,1,0:T(8,128)(2,1)}), bf16[8,80,128]{2,1,0:T(8,128)(2,1)S(1)}, u32[]{:S(2)}, u32[]{:S(2)}) async-start(bf16[8,80,128]{2,1,0:T(8,128)(2,1)} %bitcast.3), calls=%async_computation.1 | async-start | bytes 327680 | tf_op jit(solution)/shard_map/all_to_all | solution.py:233
  93.9 0.2 copy.26
  94.0 0.7 copy.31
  94.7 4.7 %all-to-all-done.1.system_ref = bf16[8,80,128]{2,1,0:T(8,128)(2,1)S(1)} async-done(((bf16[8,80,128]{2,1,0:T(8,128)(2,1)}), bf16[8,80,128]{2,1,0:T(8,128)(2,1)S(1)}, u32[]{:S(2)}, u32[]{:S(2)}) %all-to-all-start.1) | async-done | bytes 163872 | tf_op jit(solution)/shard_map/all_to_all | solution.py:233
  99.4 0.0 copy-start.2
  99.4 0.7 copy-done.2
  100.1 4.0 %finish.1 = bf16[2,80,512]{2,1,0:T(8,128)(2,1)} custom-call(bf16[8,80,128]{2,1,0:T(8,128)(2,1)} %copy-done.2, bf16[2,80,512]{2,1,0:T(8,128)(2,1)} %bitcast.20), custom_call_target="tpu_custom_call" | custom-call | tf_op jit(solution)/shard_map/finish/pallas_call | solution.py:234
  104.1 1.1 copy.28
  105.2 9.3 %all_to_all.46 = bf16[80,2,512]{2,1,0:T(2,128)(2,1)S(1)} all-to-all(bf16[80,2,512]{2,1,0:T(2,128)(2,1)S(1)} %copy.28), channel_id=1, replica_groups=mesh['mem'=8,'grid'=32] {'mem'}, dimensions={0} | all-to-all | bytes 327680 | tf_op jit(solution)/shard_map/all_to_all | solution.py:241
  114.5 0.1 copy.29
  114.6 0.7 all_to_all.41
  (1 shorter events, 0.0 us)
Async XLA Ops:
  0.0 43.3 %copy-start = (f32[384,128]{1,0:T(8,128)S(1)}, f32[384,128]{1,0:T(8,128)}, u32[]{:S(2)}) copy-start(f32[384,128]{1,0:T(8,128)} %param.9) | copy-start | bytes 589828
  0.0 36.9 %copy-start.4 = (s32[16,256]{1,0:T(8,128)S(1)}, s32[16,256]{1,0:T(8,128)}, u32[]{:S(2)}) copy-start(s32[16,256]{1,0:T(8,128)} %param.12) | copy-start | bytes 49156
  31.0 19.8 %all-to-all-start = ((bf16[8,10,48,128]{3,2,1,0:T(8,128)(2,1)}), bf16[8,10,48,128]{3,2,1,0:T(8,128)(2,1)S(1)}, u32[]{:S(2)}, u32[]{:S(2)}) async-start(bf16[8,10,48,128]{3,2,1,0:T(8,128)(2,1)} %pack.1), calls=%async_computation | async-start | bytes 1966080 | tf_op jit(solution)/shard_map/all_to_all | solution.py:184
  36.9 10.6 %collective-permute-start = (s32[16,256]{1,0:T(8,128)S(1)}, s32[16,256]{1,0:T(8,128)S(1)}, u32[]{:S(2)}, u32[]{:S(2)}) collective-permute-start(s32[16,256]{1,0:T(8,128)S(1)} %copy-done.4), channel_id=1, source_target_pairs={{0,1},{1,2},{2,3},{3,4},{4,5},{5,6},{6,7},{7,8},{8,9},{9,10},{10,1... | collective-permute-start | bytes 49160 | tf_op jit(solution)/shard_map/ppermute | solution.py:20
  36.9 10.6 %collective-permute-start.1 = (s32[16,256]{1,0:T(8,128)S(1)}, s32[16,256]{1,0:T(8,128)S(1)}, u32[]{:S(2)}, u32[]{:S(2)}) collective-permute-start(s32[16,256]{1,0:T(8,128)S(1)} %copy-done.4), channel_id=1, source_target_pairs={{0,31},{1,0},{2,1},{3,2},{4,3},{5,4},{6,5},{7,6},{8,7},{9,8},{10,9... | collective-permute-start | bytes 49160 | tf_op jit(solution)/shard_map/ppermute | solution.py:20
  48.2 23.7 %copy-start.3 = (bf16[10,16,512]{2,1,0:T(8,128)(2,1)S(1)}, bf16[10,16,512]{2,1,0:T(8,128)(2,1)}, u32[]{:S(2)}) copy-start(bf16[10,16,512]{2,1,0:T(8,128)(2,1)} %param.7) | copy-start | bytes 491524
  50.7 1.0 copy-start.1
  66.5 19.9 %collective-permute-start.2 = (bf16[640,128]{1,0:T(8,128)(2,1)}, bf16[640,128]{1,0:T(8,128)(2,1)S(1)}, u32[]{:S(2)}, u32[]{:S(2)}) collective-permute-start(bf16[640,128]{1,0:T(8,128)(2,1)} %get-tuple-element.9), channel_id=1, source_target_pairs={{0,1},{1,2},{2,3},{3,4},{4,5},{5,6},{6,7},{7,8},{8,9},{9,10},{10,1... | collective-permute-start | bytes 491528 | tf_op jit(solution)/shard_map/ppermute | solution.py:20
  69.3 17.1 %collective-permute-start.3 = (bf16[640,128]{1,0:T(8,128)(2,1)}, bf16[640,128]{1,0:T(8,128)(2,1)S(1)}, u32[]{:S(2)}, u32[]{:S(2)}) collective-permute-start(bf16[640,128]{1,0:T(8,128)(2,1)} %get-tuple-element.10), channel_id=1, source_target_pairs={{0,31},{1,0},{2,1},{3,2},{4,3},{5,4},{6,5},{7,6},{8,7},{9,8},{10,9... | collective-permute-start | bytes 491528 | tf_op jit(solution)/shard_map/ppermute | solution.py:20
  72.7 15.4 %all-to-all-start.2 = ((bf16[10,16,512]{2,0,1:T(8,128)(2,1)}), bf16[10,16,512]{2,0,1:T(8,128)(2,1)S(1)}, u32[]{:S(2)}, u32[]{:S(2)}) async-start(bf16[10,16,512]{2,0,1:T(8,128)(2,1)} %copy.25), calls=%async_computation.2 | async-start | bytes 524288 | tf_op jit(solution)/shard_map/all_to_all | solution.py:186
  88.1 11.3 %all-to-all-start.1 = ((bf16[8,80,128]{2,1,0:T(8,128)(2,1)}), bf16[8,80,128]{2,1,0:T(8,128)(2,1)S(1)}, u32[]{:S(2)}, u32[]{:S(2)}) async-start(bf16[8,80,128]{2,1,0:T(8,128)(2,1)} %bitcast.3), calls=%async_computation.1 | async-start | bytes 327680 | tf_op jit(solution)/shard_map/all_to_all | solution.py:233
  99.4 0.7 copy-start.2

commit v3 on v2

--- a/solution.py
+++ b/solution.py
@@ -20,20 +20,67 @@
     return lax.ppermute(value, axis, [(i, (i + step) % count) for i in range(count)])
 
 
-def pack_kernel(parts, size, src_ref, out_ref, sems):
+def pack_kernel(parts, size, owned, src_ref, state_ref, out_ref, stage_ref, sems):
+    local = state_ref.shape[0]
+    pieces = state_ref.shape[2] // LANES
+    inward = [
+        pltpu.make_async_copy(
+            src_ref.at[:, m * size : (m + 1) * size, :], stage_ref.at[m, :, 0:size, :], sems.at[0, m]
+        )
+        for m in range(parts)
+    ]
+    outward = [
+        pltpu.make_async_copy(stage_ref.at[m], out_ref.at[m], sems.at[1, m]) for m in range(parts)
+    ]
+    for copy in inward:
+        copy.start()
+    for i in range(local):
+        value = state_ref[i].astype(jnp.float32)
+        for m in range(parts):
+            rows = value[m * owned : (m + 1) * owned]
+            rows = jnp.concatenate(
+                [rows[:, q * LANES : (q + 1) * LANES] for q in range(pieces)], axis=0
+            )
+            stage_ref[m, i, size : size + pieces * owned, :] = rows.astype(stage_ref.dtype)
+    for m in range(parts):
+        inward[m].wait()
+        outward[m].start()
+    for copy in outward:
+        copy.wait()
+
+
+def weight_kernel(nb_total, obs, len_ref, low_ref, mid_ref, high_ref, prec_all, pos_all, value_all, out_ref, aux_ref, prec_ref, pos_ref, sems):
+    place = lax.axis_index("mem")
+    grid_pos = lax.axis_index("grid")
+    grid_count = lax.axis_size("grid")
+    obs_blocks = prec_all.shape[0]
+    blocks_dev = mid_ref.shape[0]
+    mine = pl.ds(pl.multiple_of(place * obs, 8), obs)
     copies = [
-        pltpu.make_async_copy(src_ref.at[:, m * size : (m + 1) * size, :], out_ref.at[m], sems.at[m])
-        for m in range(parts)
+        pltpu.make_async_copy(prec_all.at[mine], prec_ref, sems.at[0]),
+        pltpu.make_async_copy(pos_all.at[mine], pos_ref, sems.at[1]),
+        pltpu.make_async_copy(value_all.at[mine], aux_ref.at[obs : 2 * obs], sems.at[2]),
     ]
     for copy in copies:
         copy.start()
+    row = lax.broadcasted_iota(jnp.int32, (obs, LANES), 0)
+    count = jnp.zeros((obs, LANES), jnp.int32)
+    for o in range(obs):
+        count = jnp.where(row == o, len_ref[place * obs + o], count)
+    lane = lax.broadcasted_iota(jnp.int32, (obs, LANES), 1)
+    aux_ref[0:obs, :] = jnp.where(lane < count, 1.0, 0.0)
+    base = grid_pos * obs_blocks + place * obs
+    pairs = jnp.concatenate([low_ref[...], mid_ref[...], high_ref[...]], axis=0) - base
+    index = lax.broadcasted_iota(jnp.int32, (blocks_dev, LANES), 0)
+    centers = jnp.concatenate(
+        [
+            index + lax.rem(grid_pos + grid_count + step, grid_count) * blocks_dev
+            for step in (-1, 0, 1)
+        ],
+        axis=0,
+    ).astype(jnp.float32) + 0.5
     for copy in copies:
         copy.wait()
-
-
-def weight_kernel(nb_total, obs, base_ref, pairs_ref, centers_ref, prec_ref, pos_ref, out_ref):
-    pairs = pairs_ref[...] - base_ref[0]
-    centers = centers_ref[...]
     for o in range(obs):
         hit = jnp.max(jnp.where(pairs == o, 1.0, 0.0), axis=1, keepdims=True)
         gap = jnp.abs(pos_ref[o : o + 1, :] - centers)
@@ -76,20 +123,20 @@
         out_ref[b * half : (b + 1) * half, :] = jnp.where(low, bottom, top).astype(out_ref.dtype)
 
 
-def neighbour_kernel(members, obs, blocks, chunk, batch, prior_ref, len_ref, value_ref, w_ref, d_ref, low_ref, high_ref, dev_ref, acc_ref):
+def neighbour_kernel(members, obs, blocks, chunk, batch, prior_ref, aux_ref, w_ref, d_ref, low_ref, high_ref, dev_ref, acc_ref):
     half = members // 2
     total = prior_ref[0].astype(jnp.float32)
     for i in range(1, members):
         total = total + prior_ref[i].astype(jnp.float32)
     mean = total / members
-    valid = lax.broadcasted_iota(jnp.int32, mean.shape, 1) < len_ref[...]
+    valid = aux_ref[0:obs, :] > 0.0
     for i in range(members):
         one = jnp.where(valid, prior_ref[i].astype(jnp.float32) - mean, 0.0)
         dev_ref[i * obs : (i + 1) * obs, :] = one
         if i >= half:
             at = LANES - members + i
             dev_ref[at * obs : (at + 1) * obs, :] = one
-    departure = jnp.where(valid, value_ref[...] - mean, 0.0)
+    departure = jnp.where(valid, aux_ref[obs : 2 * obs, :] - mean, 0.0)
     high = departure.astype(jnp.bfloat16).astype(jnp.float32)
     for k in range(LANES - half - members):
         piece = (high, departure - high)[k % 2] if k < 4 else jnp.zeros(mean.shape, jnp.float32)
@@ -106,8 +153,22 @@
     packed_system(members, blocks, acc_ref, out_ref)
 
 
-def finish_kernel(members, owned, parts, system_ref, state_ref, out_ref):
+def state_kernel(members, part_ref, dev_ref, mean_ref, wide_ref):
+    rows = part_ref.shape[1]
+    total = part_ref[0].astype(jnp.float32)
+    for i in range(1, members):
+        total = total + part_ref[i].astype(jnp.float32)
+    mean = total / members
+    mean_ref[...] = mean
+    for i in range(members):
+        wide_ref[i * rows : (i + 1) * rows, :] = part_ref[i].astype(jnp.float32) - mean
+    for k in range(rows):
+        dev_ref[:, k * LANES : (k + 1) * LANES] = wide_ref[pl.ds(k, members, stride=rows), :].astype(jnp.bfloat16)
+
+
+def finish_kernel(members, owned, parts, system_ref, dev_ref, mean_ref, out_ref, wide_ref):
     half = members // 2
+    rows_out = mean_ref.shape[0]
     highest = lax.Precision.HIGHEST
     total = system_ref[0].astype(jnp.float32)
     for m in range(1, parts):
@@ -150,11 +211,25 @@
         first = dot(root, jnp.broadcast_to(force[r], (members, LANES)))
         shiftu = dot(root, first)[:, :1]
         transform = math.sqrt(members - 1) * root + shiftu
-        state = state_ref[r].astype(jnp.float32)
-        mean = jnp.sum(state, axis=0, keepdims=True) / members
-        dev = (state - mean).astype(jnp.bfloat16)
-        moved = jnp.dot(jnp.transpose(transform).astype(jnp.bfloat16), dev, preferred_element_type=jnp.float32)
-        out_ref[r] = (mean + moved).astype(jnp.bfloat16)
+        turned = jnp.transpose(transform).astype(jnp.bfloat16)
+        for k in range(r, rows_out, owned):
+            moved = jnp.dot(
+                turned, dev_ref[:, k * LANES : (k + 1) * LANES], preferred_element_type=jnp.float32
+            )
+            wide_ref[pl.ds(k, members, stride=rows_out), :] = mean_ref[k : k + 1, :] + moved
+    out_ref[...] = wide_ref[...].astype(jnp.bfloat16)
+
+
+def unpack_kernel(owned, part_ref, out_ref):
+    parts, local, rows, _ = part_ref.shape
+    for i in range(local):
+        groups = []
+        for m in range(parts):
+            value = part_ref[m, i].astype(jnp.float32)
+            groups.append(
+                jnp.concatenate([value[k : k + owned] for k in range(0, rows, owned)], axis=1)
+            )
+        out_ref[i] = jnp.concatenate(groups, axis=0).astype(out_ref.dtype)
 
 
 def per_device(ens_state, obs_prior, obs_value, obs_prec, obs_len, pair_block, obs_pos):
@@ -168,56 +243,58 @@
     obs = obs_blocks // mem_count
     half = members // 2
     nb_total = blocks_dev * grid_count
-    mem_pos = lax.axis_index("mem")
-    grid_pos = lax.axis_index("grid")
     vmem = pl.BlockSpec(memory_space=pltpu.VMEM)
     anywhere = pl.BlockSpec(memory_space=pl.ANY)
 
+    pieces = ens_state.shape[2] // LANES
+    extra = pieces * owned
     packed = pl.pallas_call(
-        functools.partial(pack_kernel, mem_count, obs),
-        out_shape=jax.ShapeDtypeStruct((mem_count, local, obs, LANES), obs_prior.dtype),
-        in_specs=[anywhere],
+        functools.partial(pack_kernel, mem_count, obs, owned),
+        out_shape=jax.ShapeDtypeStruct((mem_count, local, obs + extra, LANES), obs_prior.dtype),
+        in_specs=[anywhere, vmem],
         out_specs=anywhere,
-        scratch_shapes=[pltpu.SemaphoreType.DMA((mem_count,))],
+        scratch_shapes=[
+            pltpu.VMEM((mem_count, local, obs + extra, LANES), obs_prior.dtype),
+            pltpu.SemaphoreType.DMA((2, mem_count)),
+        ],
         name="pack",
-    )(obs_prior)
+    )(obs_prior, ens_state)
     prior = lax.all_to_all(packed, "mem", split_axis=0, concat_axis=0, tiled=True)
-    prior = prior.reshape(members, obs, LANES)
-    state = lax.all_to_all(ens_state, "mem", split_axis=1, concat_axis=0, tiled=True)
+    prior = prior.reshape(members, obs + extra, LANES)
     from_low = shift(pair_block, "grid", 1)
     from_high = shift(pair_block, "grid", -1)
 
-    pairs = jnp.concatenate([from_low, pair_block, from_high], axis=0)
-    places = (grid_pos + jnp.arange(-1, 2, dtype=jnp.int32)) % grid_count
-    ids = places[:, None] * blocks_dev + jnp.arange(blocks_dev, dtype=jnp.int32)[None, :]
     blocks = 3 * blocks_dev
-    centers = ids.reshape(blocks, 1).astype(jnp.float32) + 0.5
-
-    def mine(value):
-        return lax.dynamic_slice_in_dim(value, mem_pos * obs, obs, 0)
-
-    base = (grid_pos * obs_blocks + mem_pos * obs).reshape(1)
-    weights = pl.pallas_call(
+    weights, aux = pl.pallas_call(
         functools.partial(weight_kernel, float(nb_total), obs),
-        out_shape=jax.ShapeDtypeStruct((blocks, obs * LANES), jnp.float32),
-        in_specs=[pl.BlockSpec(memory_space=pltpu.SMEM), vmem, vmem, vmem, vmem],
-        out_specs=vmem,
+        out_shape=(
+            jax.ShapeDtypeStruct((blocks, obs * LANES), jnp.float32),
+            jax.ShapeDtypeStruct((2 * obs, LANES), jnp.float32),
+        ),
+        in_specs=[pl.BlockSpec(memory_space=pltpu.SMEM), vmem, vmem, vmem, anywhere, anywhere, anywhere],
+        out_specs=(vmem, vmem),
+        scratch_shapes=[
+            pltpu.VMEM((obs, LANES), jnp.float32),
+            pltpu.VMEM((obs, LANES), jnp.float32),
+            pltpu.SemaphoreType.DMA((3,)),
+        ],
         name="weights",
-    )(base, pairs, centers, mine(obs_prec), mine(obs_pos))
+    )(obs_len, from_low, pair_block, from_high, obs_prec, obs_pos, obs_value)
 
     chunk, batch = 6, 4
     system = jax.ShapeDtypeStruct((blocks_dev * half, LANES), jnp.bfloat16)
     d_all, to_low, to_high = pl.pallas_call(
         functools.partial(neighbour_kernel, members, obs, blocks_dev, chunk, batch),
         out_shape=(jax.ShapeDtypeStruct((LANES, obs * LANES), jnp.bfloat16), system, system),
-        in_specs=[vmem, vmem, vmem, vmem],
+        grid=(1,),
+        in_specs=[pl.BlockSpec((members, obs, LANES), lambda i: (0, 0, 0)), vmem, vmem],
         out_specs=(vmem, vmem, vmem),
         scratch_shapes=[
             pltpu.VMEM((LANES * obs, LANES), jnp.float32),
             pltpu.VMEM((blocks_dev * members, LANES), jnp.float32),
         ],
         name="neighbours",
-    )(prior, mine(obs_len)[:, None], mine(obs_value), weights)
+    )(prior, aux, weights)
     from_high = shift(to_low, "grid", -1)
     from_low = shift(to_high, "grid", 1)
     own = pl.pallas_call(
@@ -231,16 +308,35 @@
     partial = own + from_low.astype(jnp.float32) + from_high.astype(jnp.float32)
     partial = partial.astype(jnp.bfloat16).reshape(mem_count, owned * half, LANES)
     swapped = lax.all_to_all(partial, "mem", split_axis=0, concat_axis=0, tiled=True)
+    deviation, mean = pl.pallas_call(
+        functools.partial(state_kernel, members),
+        out_shape=(
+            jax.ShapeDtypeStruct((members, extra * LANES), jnp.bfloat16),
+            jax.ShapeDtypeStruct((extra, LANES), jnp.float32),
+        ),
+        grid=(1,),
+        in_specs=[pl.BlockSpec((members, extra, LANES), lambda i: (0, obs // extra, 0))],
+        out_specs=(vmem, vmem),
+        scratch_shapes=[pltpu.VMEM((members * extra, LANES), jnp.float32)],
+        name="state",
+    )(prior)
     analysis = pl.pallas_call(
         functools.partial(finish_kernel, members, owned, mem_count),
-        out_shape=jax.ShapeDtypeStruct((owned, members, ens_state.shape[2]), jnp.bfloat16),
-        in_specs=[vmem, vmem],
+        out_shape=jax.ShapeDtypeStruct((members * extra, LANES), jnp.bfloat16),
+        in_specs=[vmem, vmem, vmem],
         out_specs=vmem,
+        scratch_shapes=[pltpu.VMEM((members * extra, LANES), jnp.float32)],
         name="finish",
-    )(swapped, jnp.transpose(state, (1, 0, 2)))
-    return lax.all_to_all(
-        jnp.transpose(analysis, (1, 0, 2)), "mem", split_axis=0, concat_axis=1, tiled=True
-    )
+    )(swapped, deviation, mean)
+    analysis = analysis.reshape(mem_count, local, extra, LANES)
+    analysis = lax.all_to_all(analysis, "mem", split_axis=0, concat_axis=0, tiled=True)
+    return pl.pallas_call(
+        functools.partial(unpack_kernel, owned),
+        out_shape=jax.ShapeDtypeStruct(ens_state.shape, jnp.bfloat16),
+        in_specs=[vmem],
+        out_specs=vmem,
+        name="unpack",
+    )(analysis)
 
 
 def solution(mesh):

time: 116 us -> 85 us (0.73)
  the two profiles are of different devices: /device:TPU:2 before, /device:TPU:196 now
where the time goes in v3:
time: 85 us; the launch traced here: 84.3 us
  Pallas kernels  36.5 us (43%)
  starting transfers between devices  17.4 us (20%)
  waiting for transfers between devices  14.9 us (18%)
  blocking collectives  10.8 us (13%)
  local copies, waits for them, and re-layouts  2.88 us (3%)
  other arithmetic  1.7 us (2%)
    pallas_call x1, Pallas kernels, per_device(): pl.pallas_call(functools.partial(neighbour_kernel, members, obs, blocks_d...  14.7 us
    all_to_all x1, blocking collectives, per_device(): lax.all_to_all(analysis, 'mem', split_axis=0, concat_axis=0, tiled=True)  10.8 us
    ppermute x4, waiting for transfers between devices, shift(): lax.ppermute(value, axis, [(i, (i + step) % count) for i in range(count)])  9.83 us
    pallas_call x1, Pallas kernels, per_device(): pl.pallas_call(functools.partial(own_kernel, members, obs, blocks_dev, ch...  8.01 us
    ppermute x4, starting transfers between devices, shift(): lax.ppermute(value, axis, [(i, (i + step) % count) for i in range(count)])  6.57 us
    all_to_all x1, starting transfers between devices, per_device(): lax.all_to_all(partial, 'mem', split_axis=0, concat_axis=0, tiled=True)  5.68 us
    all_to_all x1, starting transfers between devices, per_device(): lax.all_to_all(packed, 'mem', split_axis=0, concat_axis=0, tiled=True)  5.12 us
    all_to_all x1, waiting for transfers between devices, per_device(): lax.all_to_all(partial, 'mem', split_axis=0, concat_axis=0, tiled=True)  5.08 us
  transfers between devices with their start and end apart: 6, of which 2 were waited for; matrix products, arithmetic and copies ran while one was open for 0% of the time, Pallas kernels for 15%

profile of v3, /device:TPU:196, one launch (start us, length us, event | category | flops | bytes accessed | tf_op | source)
XLA Modules:
  0.0 84.3 jit_solution(7486804251333026975)
XLA Ops:
  0.0 3.0 %pack.1 = bf16[8,10,56,128]{3,2,1,0:T(8,128)(2,1)} custom-call(bf16[10,384,128]{2,1,0:T(8,128)(2,1)} %src_ref.1, bf16[10,16,512]{2,1,0:T(8,128)(2,1)} %state_ref.1), custom_call_target="tpu_custom_call" | custom-call | tf_op jit(solution)/shard_map/pack/pallas_call | solution.py:251
  3.0 0.0 copy-start.2
  3.0 5.1 %all-to-all-start = ((bf16[8,10,56,128]{3,2,1,0:T(8,128)(2,1)}), bf16[8,10,56,128]{3,2,1,0:T(8,128)(2,1)S(1)}, u32[]{:S(2)}, u32[]{:S(2)}) async-start(bf16[8,10,56,128]{3,2,1,0:T(8,128)(2,1)} %pack.1), calls=%async_computation | async-start | bytes 2293760 | tf_op jit(solution)/shard_map/all_to_all | solution.py:262
  8.2 0.0 copy-done.2
  8.2 0.1 collective-permute-start
  8.3 3.2 %collective-permute-start.1 = (s32[16,256]{1,0:T(8,128)S(1)}, s32[16,256]{1,0:T(8,128)S(1)}, u32[]{:S(2)}, u32[]{:S(2)}) collective-permute-start(s32[16,256]{1,0:T(8,128)S(1)} %copy-done.2), channel_id=1, source_target_pairs={{0,31},{1,0},{2,1},{3,2},{4,3},{5,4},{6,5},{7,6},{8,7},{9,8},{10,9... | collective-permute-start | bytes 49160 | tf_op jit(solution)/shard_map/ppermute | solution.py:20
  11.5 9.8 %collective-permute-done.low_ref = s32[16,256]{1,0:T(8,128)S(1)} collective-permute-done((s32[16,256]{1,0:T(8,128)S(1)}, s32[16,256]{1,0:T(8,128)S(1)}, u32[]{:S(2)}, u32[]{:S(2)}) %collective-permute-start) | collective-permute-done | bytes 16416 | tf_op jit(solution)/shard_map/ppermute | solution.py:20
  21.3 0.0 copy-start.3
  21.3 0.0 collective-permute-done.1.high_ref
  21.3 0.6 copy-done.3
  21.9 0.0 copy-start.4
  21.9 0.6 copy-done.4
  22.5 3.3 %weights.1 = (f32[48,6144]{1,0:T(8,128)}, f32[96,128]{1,0:T(8,128)}) custom-call(s32[384]{0:T(512)} %len_ref.1, s32[16,256]{1,0:T(8,128)} %copy-done.3, s32[16,256]{1,0:T(8,128)} %mid_ref.1, s32[16,256]{1,0:T(8,128)} %copy-done.4, f32[384,128]{1,0:T(8,128)} %prec_all.1, f32[384,128]{1,0:T(8,128)} %pos_all.1, f32[384,128]{1,0:T(8,128)} %value_all.1), custom_call_target="tpu_custom_call" | custom-call | tf_op jit(solution)/shard_map/weights/pallas_call | solution.py:268
  25.8 0.0 all-to-all-done
  25.8 0.0 copy-start
  25.8 1.0 %copy-done = bf16[8,10,56,128]{3,2,1,0:T(8,128)(2,1)} copy-done((bf16[8,10,56,128]{3,2,1,0:T(8,128)(2,1)}, bf16[8,10,56,128]{3,2,1,0:T(8,128)(2,1)S(1)}, u32[]{:S(2)}) %copy-start) | copy-done | bytes 1146904
  26.8 14.7 %neighbours.1 = (bf16[128,6144]{1,0:T(8,128)(2,1)}, bf16[640,128]{1,0:T(8,128)(2,1)}, bf16[640,128]{1,0:T(8,128)(2,1)}) custom-call(bf16[80,56,128]{2,1,0:T(8,128)(2,1)} %bitcast.3, f32[96,128]{1,0:T(8,128)} %get-tuple-element.12.aux_ref, f32[48,6144]{1,0:T(8,128)} %get-tuple-element.13.w_ref), custom_call_target="tpu_custom_call" | custom-call | tf_op jit(solution)/shard_map/neighbours/pallas_call | solution.py:286
  41.6 0.0 collective-permute-start.2
  41.6 3.2 %collective-permute-start.3 = (bf16[640,128]{1,0:T(8,128)(2,1)}, bf16[640,128]{1,0:T(8,128)(2,1)S(1)}, u32[]{:S(2)}, u32[]{:S(2)}) collective-permute-start(bf16[640,128]{1,0:T(8,128)(2,1)} %get-tuple-element.16), channel_id=1, source_target_pairs={{0,31},{1,0},{2,1},{3,2},{4,3},{5,4},{6,5},{7,6},{8,7},{9,8},{10,9... | collective-permute-start | bytes 491528 | tf_op jit(solution)/shard_map/ppermute | solution.py:20
  44.8 8.0 %own.1 = f32[640,128]{1,0:T(8,128)} custom-call(bf16[128,6144]{1,0:T(8,128)(2,1)} %get-tuple-element.14.d_ref, f32[48,6144]{1,0:T(8,128)} %get-tuple-element.13.w_ref), custom_call_target="tpu_custom_call" | custom-call | tf_op jit(solution)/shard_map/own/pallas_call | solution.py:300
  52.8 0.0 collective-permute-done.2
  52.8 0.0 collective-permute-done.3
  52.8 1.7 %add_convert_fusion = bf16[640,128]{1,0:T(8,128)(2,1)} fusion(bf16[640,128]{1,0:T(8,128)(2,1)S(1)} %collective-permute-done.3, f32[640,128]{1,0:T(8,128)} %own.1, bf16[640,128]{1,0:T(8,128)(2,1)S(1)} %collective-permute-done.2), kind=kLoop, calls=%fused_computation | loop fusion | flops 409600 | bytes 819200 | tf_op jit(solution)/shard_map/convert_element_type | solution.py:309
  54.5 5.7 %all-to-all-start.1 = ((bf16[8,80,128]{2,1,0:T(8,128)(2,1)}), bf16[8,80,128]{2,1,0:T(8,128)(2,1)S(1)}, u32[]{:S(2)}, u32[]{:S(2)}) async-start(bf16[8,80,128]{2,1,0:T(8,128)(2,1)} %bitcast.1), calls=%async_computation.1 | async-start | bytes 327680 | tf_op jit(solution)/shard_map/all_to_all | solution.py:310
  60.2 1.7 %state.1 = (bf16[80,1024]{1,0:T(8,128)(2,1)}, f32[8,128]{1,0:T(8,128)}) custom-call(bf16[80,56,128]{2,1,0:T(8,128)(2,1)} %bitcast.4), custom_call_target="tpu_custom_call" | custom-call | tf_op jit(solution)/shard_map/state/pallas_call | solution.py:311
  62.0 5.1 %all-to-all-done.1.system_ref = bf16[8,80,128]{2,1,0:T(8,128)(2,1)S(1)} async-done(((bf16[8,80,128]{2,1,0:T(8,128)(2,1)}), bf16[8,80,128]{2,1,0:T(8,128)(2,1)S(1)}, u32[]{:S(2)}, u32[]{:S(2)}) %all-to-all-start.1) | async-done | bytes 163872 | tf_op jit(solution)/shard_map/all_to_all | solution.py:310
  67.1 0.0 copy-start.1
  67.1 0.7 copy-done.1
  67.7 4.1 %finish.1 = bf16[640,128]{1,0:T(8,128)(2,1)} custom-call(bf16[8,80,128]{2,1,0:T(8,128)(2,1)} %copy-done.1, bf16[80,1024]{1,0:T(8,128)(2,1)} %get-tuple-element.17.dev_ref, f32[8,128]{1,0:T(8,128)} %get-tuple-element.18.mean_ref), custom_call_target="tpu_custom_call" | custom-call | tf_op jit(solution)/shard_map/finish/pallas_call | solution.py:323
  71.8 10.8 %all_to_all.15.part_ref = bf16[8,10,8,128]{3,2,1,0:T(8,128)(2,1)} all-to-all(bf16[8,10,8,128]{3,2,1,0:T(8,128)(2,1)} %bitcast.5), channel_id=1, replica_groups=mesh['mem'=8,'grid'=32] {'mem'}, dimensions={0} | all-to-all | bytes 327680 | tf_op jit(solution)/shard_map/all_to_all | solution.py:332
  82.6 1.7 %unpack.1 = bf16[10,16,512]{2,1,0:T(8,128)(2,1)} custom-call(bf16[8,10,8,128]{3,2,1,0:T(8,128)(2,1)} %all_to_all.15.part_ref), custom_call_target="tpu_custom_call" | custom-call | tf_op jit(solution)/shard_map/unpack/pallas_call | solution.py:333
Async XLA Ops:
  3.0 5.1 %copy-start.2 = (s32[16,256]{1,0:T(8,128)S(1)}, s32[16,256]{1,0:T(8,128)}, u32[]{:S(2)}) copy-start(s32[16,256]{1,0:T(8,128)} %mid_ref.1) | copy-start | bytes 49156
  3.0 22.8 %all-to-all-start = ((bf16[8,10,56,128]{3,2,1,0:T(8,128)(2,1)}), bf16[8,10,56,128]{3,2,1,0:T(8,128)(2,1)S(1)}, u32[]{:S(2)}, u32[]{:S(2)}) async-start(bf16[8,10,56,128]{3,2,1,0:T(8,128)(2,1)} %pack.1), calls=%async_computation | async-start | bytes 2293760 | tf_op jit(solution)/shard_map/all_to_all | solution.py:262
  8.2 13.1 %collective-permute-start = (s32[16,256]{1,0:T(8,128)S(1)}, s32[16,256]{1,0:T(8,128)S(1)}, u32[]{:S(2)}, u32[]{:S(2)}) collective-permute-start(s32[16,256]{1,0:T(8,128)S(1)} %copy-done.2), channel_id=1, source_target_pairs={{0,1},{1,2},{2,3},{3,4},{4,5},{5,6},{6,7},{7,8},{8,9},{9,10},{10,1... | collective-permute-start | bytes 49160 | tf_op jit(solution)/shard_map/ppermute | solution.py:20
  8.3 13.1 %collective-permute-start.1 = (s32[16,256]{1,0:T(8,128)S(1)}, s32[16,256]{1,0:T(8,128)S(1)}, u32[]{:S(2)}, u32[]{:S(2)}) collective-permute-start(s32[16,256]{1,0:T(8,128)S(1)} %copy-done.2), channel_id=1, source_target_pairs={{0,31},{1,0},{2,1},{3,2},{4,3},{5,4},{6,5},{7,6},{8,7},{9,8},{10,9... | collective-permute-start | bytes 49160 | tf_op jit(solution)/shard_map/ppermute | solution.py:20
  21.3 0.6 copy-start.3
  21.9 0.6 copy-start.4
  25.8 1.0 %copy-start = (bf16[8,10,56,128]{3,2,1,0:T(8,128)(2,1)}, bf16[8,10,56,128]{3,2,1,0:T(8,128)(2,1)S(1)}, u32[]{:S(2)}) copy-start(bf16[8,10,56,128]{3,2,1,0:T(8,128)(2,1)S(1)} %all-to-all-done) | copy-start | bytes 3440644
  41.6 11.3 %collective-permute-start.2 = (bf16[640,128]{1,0:T(8,128)(2,1)}, bf16[640,128]{1,0:T(8,128)(2,1)S(1)}, u32[]{:S(2)}, u32[]{:S(2)}) collective-permute-start(bf16[640,128]{1,0:T(8,128)(2,1)} %get-tuple-element.15), channel_id=1, source_target_pairs={{0,1},{1,2},{2,3},{3,4},{4,5},{5,6},{6,7},{7,8},{8,9},{9,10},{10,1... | collective-permute-start | bytes 491528 | tf_op jit(solution)/shard_map/ppermute | solution.py:20
  41.6 11.3 %collective-permute-start.3 = (bf16[640,128]{1,0:T(8,128)(2,1)}, bf16[640,128]{1,0:T(8,128)(2,1)S(1)}, u32[]{:S(2)}, u32[]{:S(2)}) collective-permute-start(bf16[640,128]{1,0:T(8,128)(2,1)} %get-tuple-element.16), channel_id=1, source_target_pairs={{0,31},{1,0},{2,1},{3,2},{4,3},{5,4},{6,5},{7,6},{8,7},{9,8},{10,9... | collective-permute-start | bytes 491528 | tf_op jit(solution)/shard_map/ppermute | solution.py:20
  54.5 12.5 %all-to-all-start.1 = ((bf16[8,80,128]{2,1,0:T(8,128)(2,1)}), bf16[8,80,128]{2,1,0:T(8,128)(2,1)S(1)}, u32[]{:S(2)}, u32[]{:S(2)}) async-start(bf16[8,80,128]{2,1,0:T(8,128)(2,1)} %bitcast.1), calls=%async_computation.1 | async-start | bytes 327680 | tf_op jit(solution)/shard_map/all_to_all | solution.py:310
  67.1 0.7 copy-start.1

commit v4 on v3

--- a/solution.py
+++ b/solution.py
@@ -20,19 +20,16 @@
     return lax.ppermute(value, axis, [(i, (i + step) % count) for i in range(count)])
 
 
-def pack_kernel(parts, size, owned, src_ref, state_ref, out_ref, stage_ref, sems):
+def pack_kernel(parts, size, owned, src_ref, state_ref, out_ref, rows_ref, sems):
     local = state_ref.shape[0]
     pieces = state_ref.shape[2] // LANES
-    inward = [
+    copies = [
         pltpu.make_async_copy(
-            src_ref.at[:, m * size : (m + 1) * size, :], stage_ref.at[m, :, 0:size, :], sems.at[0, m]
+            src_ref.at[:, m * size : (m + 1) * size, :], out_ref.at[m, :, 0:size, :], sems.at[m]
         )
         for m in range(parts)
     ]
-    outward = [
-        pltpu.make_async_copy(stage_ref.at[m], out_ref.at[m], sems.at[1, m]) for m in range(parts)
-    ]
-    for copy in inward:
+    for copy in copies:
         copy.start()
     for i in range(local):
         value = state_ref[i].astype(jnp.float32)
@@ -41,12 +38,12 @@
             rows = jnp.concatenate(
                 [rows[:, q * LANES : (q + 1) * LANES] for q in range(pieces)], axis=0
             )
-            stage_ref[m, i, size : size + pieces * owned, :] = rows.astype(stage_ref.dtype)
-    for m in range(parts):
-        inward[m].wait()
-        outward[m].start()
-    for copy in outward:
+            rows_ref[m, i] = rows.astype(rows_ref.dtype)
+    last = pltpu.make_async_copy(rows_ref, out_ref.at[:, :, size:, :], sems.at[parts])
+    last.start()
+    for copy in copies:
         copy.wait()
+    last.wait()
 
 
 def weight_kernel(nb_total, obs, len_ref, low_ref, mid_ref, high_ref, prec_all, pos_all, value_all, out_ref, aux_ref, prec_ref, pos_ref, sems):
@@ -125,13 +122,13 @@
 
 def neighbour_kernel(members, obs, blocks, chunk, batch, prior_ref, aux_ref, w_ref, d_ref, low_ref, high_ref, dev_ref, acc_ref):
     half = members // 2
-    total = prior_ref[0].astype(jnp.float32)
+    total = prior_ref[0, 0:obs].astype(jnp.float32)
     for i in range(1, members):
-        total = total + prior_ref[i].astype(jnp.float32)
+        total = total + prior_ref[i, 0:obs].astype(jnp.float32)
     mean = total / members
     valid = aux_ref[0:obs, :] > 0.0
     for i in range(members):
-        one = jnp.where(valid, prior_ref[i].astype(jnp.float32) - mean, 0.0)
+        one = jnp.where(valid, prior_ref[i, 0:obs].astype(jnp.float32) - mean, 0.0)
         dev_ref[i * obs : (i + 1) * obs, :] = one
         if i >= half:
             at = LANES - members + i
@@ -154,16 +151,22 @@
 
 
 def state_kernel(members, part_ref, dev_ref, mean_ref, wide_ref):
-    rows = part_ref.shape[1]
-    total = part_ref[0].astype(jnp.float32)
+    rows = mean_ref.shape[0]
+    first = part_ref.shape[1] - rows
+    total = part_ref[0, first:].astype(jnp.float32)
     for i in range(1, members):
-        total = total + part_ref[i].astype(jnp.float32)
+        total = total + part_ref[i, first:].astype(jnp.float32)
     mean = total / members
     mean_ref[...] = mean
     for i in range(members):
-        wide_ref[i * rows : (i + 1) * rows, :] = part_ref[i].astype(jnp.float32) - mean
+        wide_ref[i * rows : (i + 1) * rows, :] = part_ref[i, first:].astype(jnp.float32) - mean
     for k in range(rows):
         dev_ref[:, k * LANES : (k + 1) * LANES] = wide_ref[pl.ds(k, members, stride=rows), :].astype(jnp.bfloat16)
+
+
+def merge_kernel(own_ref, low_ref, high_ref, out_ref):
+    total = own_ref[...] + low_ref[...].astype(jnp.float32) + high_ref[...].astype(jnp.float32)
+    out_ref[...] = total.astype(jnp.bfloat16)
 
 
 def finish_kernel(members, owned, parts, system_ref, dev_ref, mean_ref, out_ref, wide_ref):
@@ -247,18 +250,23 @@
     anywhere = pl.BlockSpec(memory_space=pl.ANY)
 
     pieces = ens_state.shape[2] // LANES
+
+    def near(value):
+        return pltpu.with_memory_space_constraint(value, pltpu.VMEM)
+
     extra = pieces * owned
     packed = pl.pallas_call(
         functools.partial(pack_kernel, mem_count, obs, owned),
         out_shape=jax.ShapeDtypeStruct((mem_count, local, obs + extra, LANES), obs_prior.dtype),
-        in_specs=[anywhere, vmem],
+        in_specs=[vmem, vmem],
         out_specs=anywhere,
         scratch_shapes=[
-            pltpu.VMEM((mem_count, local, obs + extra, LANES), obs_prior.dtype),
-            pltpu.SemaphoreType.DMA((2, mem_count)),
+            pltpu.VMEM((mem_count, local, extra, LANES), ens_state.dtype),
+            pltpu.SemaphoreType.DMA((mem_count + 1,)),
         ],
+        compiler_params=pltpu.CompilerParams(vmem_limit_bytes=16 * 2**20),
         name="pack",
-    )(obs_prior, ens_state)
+    )(near(obs_prior), near(ens_state))
     prior = lax.all_to_all(packed, "mem", split_axis=0, concat_axis=0, tiled=True)
     prior = prior.reshape(members, obs + extra, LANES)
     from_low = shift(pair_block, "grid", 1)
@@ -268,8 +276,8 @@
     weights, aux = pl.pallas_call(
         functools.partial(weight_kernel, float(nb_total), obs),
         out_shape=(
-            jax.ShapeDtypeStruct((blocks, obs * LANES), jnp.float32),
-            jax.ShapeDtypeStruct((2 * obs, LANES), jnp.float32),
+            pltpu.VMEM((blocks, obs * LANES), jnp.float32),
+            pltpu.VMEM((2 * obs, LANES), jnp.float32),
         ),
         in_specs=[pl.BlockSpec(memory_space=pltpu.SMEM), vmem, vmem, vmem, anywhere, anywhere, anywhere],
         out_specs=(vmem, vmem),
@@ -278,56 +286,66 @@
             pltpu.VMEM((obs, LANES), jnp.float32),
             pltpu.SemaphoreType.DMA((3,)),
         ],
+        compiler_params=pltpu.CompilerParams(vmem_limit_bytes=16 * 2**20),
         name="weights",
-    )(obs_len, from_low, pair_block, from_high, obs_prec, obs_pos, obs_value)
+    )(obs_len, near(from_low), pair_block, near(from_high), obs_prec, obs_pos, obs_value)
 
     chunk, batch = 6, 4
-    system = jax.ShapeDtypeStruct((blocks_dev * half, LANES), jnp.bfloat16)
+    system = pltpu.VMEM((blocks_dev * half, LANES), jnp.bfloat16)
     d_all, to_low, to_high = pl.pallas_call(
         functools.partial(neighbour_kernel, members, obs, blocks_dev, chunk, batch),
-        out_shape=(jax.ShapeDtypeStruct((LANES, obs * LANES), jnp.bfloat16), system, system),
-        grid=(1,),
-        in_specs=[pl.BlockSpec((members, obs, LANES), lambda i: (0, 0, 0)), vmem, vmem],
+        out_shape=(pltpu.VMEM((LANES, obs * LANES), jnp.bfloat16), system, system),
+        in_specs=[vmem, vmem, vmem],
         out_specs=(vmem, vmem, vmem),
         scratch_shapes=[
             pltpu.VMEM((LANES * obs, LANES), jnp.float32),
             pltpu.VMEM((blocks_dev * members, LANES), jnp.float32),
         ],
+        compiler_params=pltpu.CompilerParams(vmem_limit_bytes=16 * 2**20),
         name="neighbours",
-    )(prior, aux, weights)
+    )(near(prior), near(aux), near(weights))
     from_high = shift(to_low, "grid", -1)
     from_low = shift(to_high, "grid", 1)
     own = pl.pallas_call(
         functools.partial(own_kernel, members, obs, blocks_dev, chunk, batch),
-        out_shape=jax.ShapeDtypeStruct(system.shape, jnp.float32),
+        out_shape=pltpu.VMEM((blocks_dev * half, LANES), jnp.float32),
         in_specs=[vmem, vmem],
         out_specs=vmem,
         scratch_shapes=[pltpu.VMEM((blocks_dev * members, LANES), jnp.float32)],
+        compiler_params=pltpu.CompilerParams(vmem_limit_bytes=16 * 2**20),
         name="own",
-    )(d_all, weights)
-    partial = own + from_low.astype(jnp.float32) + from_high.astype(jnp.float32)
-    partial = partial.astype(jnp.bfloat16).reshape(mem_count, owned * half, LANES)
+    )(near(d_all), near(weights))
+    partial = pl.pallas_call(
+        merge_kernel,
+        out_shape=pltpu.VMEM((blocks_dev * half, LANES), jnp.bfloat16),
+        in_specs=[vmem, vmem, vmem],
+        out_specs=vmem,
+        compiler_params=pltpu.CompilerParams(vmem_limit_bytes=16 * 2**20),
+        name="merge",
+    )(near(own), near(from_low), near(from_high))
+    partial = partial.reshape(mem_count, owned * half, LANES)
     swapped = lax.all_to_all(partial, "mem", split_axis=0, concat_axis=0, tiled=True)
     deviation, mean = pl.pallas_call(
         functools.partial(state_kernel, members),
         out_shape=(
-            jax.ShapeDtypeStruct((members, extra * LANES), jnp.bfloat16),
-            jax.ShapeDtypeStruct((extra, LANES), jnp.float32),
+            pltpu.VMEM((members, extra * LANES), jnp.bfloat16),
+            pltpu.VMEM((extra, LANES), jnp.float32),
         ),
-        grid=(1,),
-        in_specs=[pl.BlockSpec((members, extra, LANES), lambda i: (0, obs // extra, 0))],
+        in_specs=[vmem],
         out_specs=(vmem, vmem),
         scratch_shapes=[pltpu.VMEM((members * extra, LANES), jnp.float32)],
+        compiler_params=pltpu.CompilerParams(vmem_limit_bytes=16 * 2**20),
         name="state",
-    )(prior)
+    )(near(prior))
     analysis = pl.pallas_call(
         functools.partial(finish_kernel, members, owned, mem_count),
         out_shape=jax.ShapeDtypeStruct((members * extra, LANES), jnp.bfloat16),
         in_specs=[vmem, vmem, vmem],
         out_specs=vmem,
         scratch_shapes=[pltpu.VMEM((members * extra, LANES), jnp.float32)],
+        compiler_params=pltpu.CompilerParams(vmem_limit_bytes=16 * 2**20),
         name="finish",
-    )(swapped, deviation, mean)
+    )(near(swapped), near(deviation), near(mean))
     analysis = analysis.reshape(mem_count, local, extra, LANES)
     analysis = lax.all_to_all(analysis, "mem", split_axis=0, concat_axis=0, tiled=True)
     return pl.pallas_call(
@@ -335,8 +353,9 @@
         out_shape=jax.ShapeDtypeStruct(ens_state.shape, jnp.bfloat16),
         in_specs=[vmem],
         out_specs=vmem,
+        compiler_params=pltpu.CompilerParams(vmem_limit_bytes=16 * 2**20),
         name="unpack",
-    )(analysis)
+    )(near(analysis))
 
 
 def solution(mesh):

time: 85 us -> 73.3 us (0.86)
  the two profiles are of different devices: /device:TPU:196 before, /device:TPU:2 now
where the time goes in v4:
time: 73.3 us; the launch traced here: 72.9 us
  Pallas kernels  24.5 us (33%)
  starting transfers between devices  23.6 us (32%)
  waiting for transfers between devices  13.2 us (18%)
  blocking collectives  9.27 us (13%)
  local copies, waits for them, and re-layouts  2.15 us (3%)
    pallas_call x1, Pallas kernels, per_device(): pl.pallas_call(functools.partial(neighbour_kernel, members, obs, blocks_d...  12.5 us
    ppermute x4, starting transfers between devices, shift(): lax.ppermute(value, axis, [(i, (i + step) % count) for i in range(count)])  12.3 us
    all_to_all x1, blocking collectives, per_device(): lax.all_to_all(analysis, 'mem', split_axis=0, concat_axis=0, tiled=True)  9.27 us
    all_to_all x1, waiting for transfers between devices, per_device(): lax.all_to_all(packed, 'mem', split_axis=0, concat_axis=0, tiled=True)  6.34 us
    all_to_all x1, starting transfers between devices, per_device(): lax.all_to_all(packed, 'mem', split_axis=0, concat_axis=0, tiled=True)  6.07 us
    pallas_call x1, Pallas kernels, per_device(): pl.pallas_call(functools.partial(own_kernel, members, obs, blocks_dev, ch...  5.55 us
    all_to_all x1, waiting for transfers between devices, per_device(): lax.all_to_all(partial, 'mem', split_axis=0, concat_axis=0, tiled=True)  5.45 us
    all_to_all x1, starting transfers between devices, per_device(): lax.all_to_all(partial, 'mem', split_axis=0, concat_axis=0, tiled=True)  5.28 us
  transfers between devices with their start and end apart: 6, of which 3 were waited for; matrix products, arithmetic and copies ran while one was open for 0% of the time, Pallas kernels for 10%

profile of v4, /device:TPU:2, one launch (start us, length us, event | category | flops | bytes accessed | tf_op | source)
XLA Modules:
  0.0 72.9 jit_solution(6345481974274392554)
XLA Ops:
  0.0 0.0 copy-start
  0.0 1.2 %copy-done = bf16[10,384,128]{2,1,0:T(8,128)(2,1)S(1)} copy-done((bf16[10,384,128]{2,1,0:T(8,128)(2,1)S(1)}, bf16[10,384,128]{2,1,0:T(8,128)(2,1)}, u32[]{:S(2)}) %copy-start) | copy-done | bytes 983064
  1.2 0.0 copy-start.4
  1.2 0.9 %copy-done.4 = bf16[10,16,512]{2,1,0:T(8,128)(2,1)S(1)} copy-done((bf16[10,16,512]{2,1,0:T(8,128)(2,1)S(1)}, bf16[10,16,512]{2,1,0:T(8,128)(2,1)}, u32[]{:S(2)}) %copy-start.4) | copy-done | bytes 163864
  2.1 1.1 %pack.1 = bf16[8,10,56,128]{3,2,1,0:T(8,128)(2,1)} custom-call(bf16[10,384,128]{2,1,0:T(8,128)(2,1)S(1)} %copy-done, bf16[10,16,512]{2,1,0:T(8,128)(2,1)S(1)} %copy-done.4), custom_call_target="tpu_custom_call" | custom-call | tf_op jit(solution)/shard_map/pack/pallas_call | solution.py:258
  3.2 0.0 copy-start.5
  3.2 0.0 copy-start.1
  3.3 0.0 copy-start.2
  3.3 0.0 copy-start.3
  3.3 0.0 copy-start.6
  3.3 6.1 %all-to-all-start = ((bf16[8,10,56,128]{3,2,1,0:T(8,128)(2,1)}), bf16[8,10,56,128]{3,2,1,0:T(8,128)(2,1)S(1)}, u32[]{:S(2)}, u32[]{:S(2)}) async-start(bf16[8,10,56,128]{3,2,1,0:T(8,128)(2,1)} %pack.1), calls=%async_computation | async-start | bytes 2293760 | tf_op jit(solution)/shard_map/all_to_all | solution.py:270
  9.4 0.0 copy-done.5
  9.4 0.0 collective-permute-start
  9.4 6.4 %collective-permute-start.1 = (s32[16,256]{1,0:T(8,128)S(1)}, s32[16,256]{1,0:T(8,128)S(1)}, u32[]{:S(2)}, u32[]{:S(2)}) collective-permute-start(s32[16,256]{1,0:T(8,128)S(1)} %copy-done.5), channel_id=1, source_target_pairs={{0,31},{1,0},{2,1},{3,2},{4,3},{5,4},{6,5},{7,6},{8,7},{9,8},{10,9... | collective-permute-start | bytes 49160 | tf_op jit(solution)/shard_map/ppermute | solution.py:20
  15.7 1.4 %collective-permute-done.low_ref = s32[16,256]{1,0:T(8,128)S(1)} collective-permute-done((s32[16,256]{1,0:T(8,128)S(1)}, s32[16,256]{1,0:T(8,128)S(1)}, u32[]{:S(2)}, u32[]{:S(2)}) %collective-permute-start) | collective-permute-done | bytes 16416 | tf_op jit(solution)/shard_map/ppermute | solution.py:20
  17.2 0.0 collective-permute-done.1.high_ref
  17.2 0.0 copy-done.1
  17.2 0.0 copy-done.2
  17.2 0.0 copy-done.3
  17.2 0.0 copy-done.6
  17.2 1.4 %weights.1 = (f32[48,6144]{1,0:T(8,128)S(1)}, f32[96,128]{1,0:T(8,128)S(1)}) custom-call(s32[384]{0:T(512)S(1)} %copy-done.6, s32[16,256]{1,0:T(8,128)S(1)} %collective-permute-done.low_ref, s32[16,256]{1,0:T(8,128)S(1)} %copy-done.5, s32[16,256]{1,0:T(8,128)S(1)} %collective-permute-done.1.high_ref, f32[384,128]{1,0:T(8,128)S(1)} %copy-done.1, ...), custom_call_target="tpu_custom_call" | custom-call | tf_op jit(solution)/shard_map/weights/pallas_call | solution.py:276
  18.6 6.3 %all-to-all-done = bf16[8,10,56,128]{3,2,1,0:T(8,128)(2,1)S(1)} async-done(((bf16[8,10,56,128]{3,2,1,0:T(8,128)(2,1)}), bf16[8,10,56,128]{3,2,1,0:T(8,128)(2,1)S(1)}, u32[]{:S(2)}, u32[]{:S(2)}) %all-to-all-start) | async-done | bytes 1146912 | tf_op jit(solution)/shard_map/all_to_all | solution.py:270
  24.9 12.5 %neighbours.1 = (bf16[128,6144]{1,0:T(8,128)(2,1)S(1)}, bf16[640,128]{1,0:T(8,128)(2,1)S(1)}, bf16[640,128]{1,0:T(8,128)(2,1)S(1)}) custom-call(bf16[80,56,128]{2,1,0:T(8,128)(2,1)S(1)} %bitcast.3, f32[96,128]{1,0:T(8,128)S(1)} %get-tuple-element.12.aux_ref, f32[48,6144]{1,0:T(8,128)S(1)} %get-tuple-element.13.w_ref), custom_call_target="tpu_custom_call" | custom-call | tf_op jit(solution)/shard_map/neighbours/pallas_call | solution.py:295
  37.4 1.1 %collective-permute-start.2 = (bf16[640,128]{1,0:T(8,128)(2,1)S(1)}, bf16[640,128]{1,0:T(8,128)(2,1)S(1)}, u32[]{:S(2)}, u32[]{:S(2)}) collective-permute-start(bf16[640,128]{1,0:T(8,128)(2,1)S(1)} %get-tuple-element.15), channel_id=1, source_target_pairs={{0,1},{1,2},{2,3},{3,4},{4,5},{5,6},{6,7},{7,8},{8,9},{9,10},{10,1... | collective-permute-start | bytes 491528 | tf_op jit(solution)/shard_map/ppermute | solution.py:20
  38.6 4.8 %collective-permute-start.3 = (bf16[640,128]{1,0:T(8,128)(2,1)S(1)}, bf16[640,128]{1,0:T(8,128)(2,1)S(1)}, u32[]{:S(2)}, u32[]{:S(2)}) collective-permute-start(bf16[640,128]{1,0:T(8,128)(2,1)S(1)} %get-tuple-element.16), channel_id=1, source_target_pairs={{0,31},{1,0},{2,1},{3,2},{4,3},{5,4},{6,5},{7,6},{8,7},{9,8},{10,9... | collective-permute-start | bytes 491528 | tf_op jit(solution)/shard_map/ppermute | solution.py:20
  43.3 5.6 %own.1.own_ref = f32[640,128]{1,0:T(8,128)S(1)} custom-call(bf16[128,6144]{1,0:T(8,128)(2,1)S(1)} %get-tuple-element.14.d_ref, f32[48,6144]{1,0:T(8,128)S(1)} %get-tuple-element.13.w_ref), custom_call_target="tpu_custom_call" | custom-call | tf_op jit(solution)/shard_map/own/pallas_call | solution.py:309
  48.9 0.0 collective-permute-done.2.low_ref
  48.9 0.0 collective-permute-done.3.high_ref
  48.9 0.7 merge.1
  49.6 5.3 %all-to-all-start.1 = ((bf16[8,80,128]{2,1,0:T(8,128)(2,1)}), bf16[8,80,128]{2,1,0:T(8,128)(2,1)S(1)}, u32[]{:S(2)}, u32[]{:S(2)}) async-start(bf16[8,80,128]{2,1,0:T(8,128)(2,1)} %bitcast.1), calls=%async_computation.1 | async-start | bytes 327680 | tf_op jit(solution)/shard_map/all_to_all | solution.py:327
  54.9 0.2 state.1
  55.1 5.4 %all-to-all-done.1.system_ref = bf16[8,80,128]{2,1,0:T(8,128)(2,1)S(1)} async-done(((bf16[8,80,128]{2,1,0:T(8,128)(2,1)}), bf16[8,80,128]{2,1,0:T(8,128)(2,1)S(1)}, u32[]{:S(2)}, u32[]{:S(2)}) %all-to-all-start.1) | async-done | bytes 163872 | tf_op jit(solution)/shard_map/all_to_all | solution.py:327
  60.5 2.4 %finish.1 = bf16[640,128]{1,0:T(8,128)(2,1)S(1)} custom-call(bf16[8,80,128]{2,1,0:T(8,128)(2,1)S(1)} %all-to-all-done.1.system_ref, bf16[80,1024]{1,0:T(8,128)(2,1)S(1)} %get-tuple-element.17.dev_ref, f32[8,128]{1,0:T(8,128)S(1)} %get-tuple-element.18.mean_ref), custom_call_target="tpu_custom_call" | custom-call | tf_op jit(solution)/shard_map/finish/pallas_call | solution.py:340
  62.9 9.3 %all_to_all.15.part_ref = bf16[8,10,8,128]{3,2,1,0:T(8,128)(2,1)S(1)} all-to-all(bf16[8,10,8,128]{3,2,1,0:T(8,128)(2,1)S(1)} %bitcast.5), channel_id=1, replica_groups=mesh['mem'=8,'grid'=32] {'mem'}, dimensions={0} | all-to-all | bytes 327680 | tf_op jit(solution)/shard_map/all_to_all | solution.py:350
  72.2 0.8 %unpack.1 = bf16[10,16,512]{2,1,0:T(8,128)(2,1)} custom-call(bf16[8,10,8,128]{3,2,1,0:T(8,128)(2,1)S(1)} %all_to_all.15.part_ref), custom_call_target="tpu_custom_call" | custom-call | tf_op jit(solution)/shard_map/unpack/pallas_call | solution.py:351
Async XLA Ops:
  0.0 1.2 %copy-start = (bf16[10,384,128]{2,1,0:T(8,128)(2,1)S(1)}, bf16[10,384,128]{2,1,0:T(8,128)(2,1)}, u32[]{:S(2)}) copy-start(bf16[10,384,128]{2,1,0:T(8,128)(2,1)} %src_ref.1) | copy-start | bytes 2949124
  1.2 0.9 %copy-start.4 = (bf16[10,16,512]{2,1,0:T(8,128)(2,1)S(1)}, bf16[10,16,512]{2,1,0:T(8,128)(2,1)}, u32[]{:S(2)}) copy-start(bf16[10,16,512]{2,1,0:T(8,128)(2,1)} %state_ref.1) | copy-start | bytes 491524
  3.2 6.1 %copy-start.5 = (s32[16,256]{1,0:T(8,128)S(1)}, s32[16,256]{1,0:T(8,128)}, u32[]{:S(2)}) copy-start(s32[16,256]{1,0:T(8,128)} %mid_ref.1) | copy-start | bytes 49156
  3.2 14.0 %copy-start.1 = (f32[384,128]{1,0:T(8,128)S(1)}, f32[384,128]{1,0:T(8,128)}, u32[]{:S(2)}) copy-start(f32[384,128]{1,0:T(8,128)} %prec_all.1) | copy-start | bytes 589828
  3.3 13.9 %copy-start.2 = (f32[384,128]{1,0:T(8,128)S(1)}, f32[384,128]{1,0:T(8,128)}, u32[]{:S(2)}) copy-start(f32[384,128]{1,0:T(8,128)} %pos_all.1) | copy-start | bytes 589828
  3.3 13.9 %copy-start.3 = (f32[384,128]{1,0:T(8,128)S(1)}, f32[384,128]{1,0:T(8,128)}, u32[]{:S(2)}) copy-start(f32[384,128]{1,0:T(8,128)} %value_all.1) | copy-start | bytes 589828
  3.3 13.9 %copy-start.6 = (s32[384]{0:T(512)S(1)}, s32[384]{0:T(512)}, u32[]{:S(2)}) copy-start(s32[384]{0:T(512)} %len_ref.1) | copy-start | bytes 4612
  3.3 21.7 %all-to-all-start = ((bf16[8,10,56,128]{3,2,1,0:T(8,128)(2,1)}), bf16[8,10,56,128]{3,2,1,0:T(8,128)(2,1)S(1)}, u32[]{:S(2)}, u32[]{:S(2)}) async-start(bf16[8,10,56,128]{3,2,1,0:T(8,128)(2,1)} %pack.1), calls=%async_computation | async-start | bytes 2293760 | tf_op jit(solution)/shard_map/all_to_all | solution.py:270
  9.4 7.8 %collective-permute-start = (s32[16,256]{1,0:T(8,128)S(1)}, s32[16,256]{1,0:T(8,128)S(1)}, u32[]{:S(2)}, u32[]{:S(2)}) collective-permute-start(s32[16,256]{1,0:T(8,128)S(1)} %copy-done.5), channel_id=1, source_target_pairs={{0,1},{1,2},{2,3},{3,4},{4,5},{5,6},{6,7},{7,8},{8,9},{9,10},{10,1... | collective-permute-start | bytes 49160 | tf_op jit(solution)/shard_map/ppermute | solution.py:20
  9.4 7.8 %collective-permute-start.1 = (s32[16,256]{1,0:T(8,128)S(1)}, s32[16,256]{1,0:T(8,128)S(1)}, u32[]{:S(2)}, u32[]{:S(2)}) collective-permute-start(s32[16,256]{1,0:T(8,128)S(1)} %copy-done.5), channel_id=1, source_target_pairs={{0,31},{1,0},{2,1},{3,2},{4,3},{5,4},{6,5},{7,6},{8,7},{9,8},{10,9... | collective-permute-start | bytes 49160 | tf_op jit(solution)/shard_map/ppermute | solution.py:20
  37.4 11.5 %collective-permute-start.2 = (bf16[640,128]{1,0:T(8,128)(2,1)S(1)}, bf16[640,128]{1,0:T(8,128)(2,1)S(1)}, u32[]{:S(2)}, u32[]{:S(2)}) collective-permute-start(bf16[640,128]{1,0:T(8,128)(2,1)S(1)} %get-tuple-element.15), channel_id=1, source_target_pairs={{0,1},{1,2},{2,3},{3,4},{4,5},{5,6},{6,7},{7,8},{8,9},{9,10},{10,1... | collective-permute-start | bytes 491528 | tf_op jit(solution)/shard_map/ppermute | solution.py:20
  38.6 10.3 %collective-permute-start.3 = (bf16[640,128]{1,0:T(8,128)(2,1)S(1)}, bf16[640,128]{1,0:T(8,128)(2,1)S(1)}, u32[]{:S(2)}, u32[]{:S(2)}) collective-permute-start(bf16[640,128]{1,0:T(8,128)(2,1)S(1)} %get-tuple-element.16), channel_id=1, source_target_pairs={{0,31},{1,0},{2,1},{3,2},{4,3},{5,4},{6,5},{7,6},{8,7},{9,8},{10,9... | collective-permute-start | bytes 491528 | tf_op jit(solution)/shard_map/ppermute | solution.py:20
  49.6 10.9 %all-to-all-start.1 = ((bf16[8,80,128]{2,1,0:T(8,128)(2,1)}), bf16[8,80,128]{2,1,0:T(8,128)(2,1)S(1)}, u32[]{:S(2)}, u32[]{:S(2)}) async-start(bf16[8,80,128]{2,1,0:T(8,128)(2,1)} %bitcast.1), calls=%async_computation.1 | async-start | bytes 327680 | tf_op jit(solution)/shard_map/all_to_all | solution.py:327

commit v5 on v4

--- a/solution.py
+++ b/solution.py
@@ -20,17 +20,23 @@
     return lax.ppermute(value, axis, [(i, (i + step) % count) for i in range(count)])
 
 
-def pack_kernel(parts, size, owned, src_ref, state_ref, out_ref, rows_ref, sems):
-    local = state_ref.shape[0]
-    pieces = state_ref.shape[2] // LANES
-    copies = [
-        pltpu.make_async_copy(
-            src_ref.at[:, m * size : (m + 1) * size, :], out_ref.at[m, :, 0:size, :], sems.at[m]
-        )
+def pack_kernel(parts, size, owned, src_ref, state_all, out_ref, stage_ref, state_ref, rows_ref, sems, last):
+    local = state_all.shape[0]
+    pieces = state_all.shape[2] // LANES
+    inward = [
+        pltpu.make_async_copy(src_ref.at[:, m * size : (m + 1) * size, :], stage_ref.at[m], sems.at[0, m])
         for m in range(parts)
     ]
-    for copy in copies:
+    outward = [
+        pltpu.make_async_copy(stage_ref.at[m], out_ref.at[m, :, 0:size, :], sems.at[1, m])
+        for m in range(parts)
+    ]
+    state_in = pltpu.make_async_copy(state_all, state_ref, last.at[0])
+    state_out = pltpu.make_async_copy(rows_ref, out_ref.at[:, :, size:, :], last.at[1])
+    state_in.start()
+    for copy in inward:
         copy.start()
+    state_in.wait()
     for i in range(local):
         value = state_ref[i].astype(jnp.float32)
         for m in range(parts):
@@ -39,11 +45,13 @@
                 [rows[:, q * LANES : (q + 1) * LANES] for q in range(pieces)], axis=0
             )
             rows_ref[m, i] = rows.astype(rows_ref.dtype)
-    last = pltpu.make_async_copy(rows_ref, out_ref.at[:, :, size:, :], sems.at[parts])
-    last.start()
-    for copy in copies:
+    for m in range(parts):
+        inward[m].wait()
+        outward[m].start()
+    state_out.start()
+    for copy in outward:
         copy.wait()
-    last.wait()
+    state_out.wait()
 
 
 def weight_kernel(nb_total, obs, len_ref, low_ref, mid_ref, high_ref, prec_all, pos_all, value_all, out_ref, aux_ref, prec_ref, pos_ref, sems):
@@ -258,15 +266,18 @@
     packed = pl.pallas_call(
         functools.partial(pack_kernel, mem_count, obs, owned),
         out_shape=jax.ShapeDtypeStruct((mem_count, local, obs + extra, LANES), obs_prior.dtype),
-        in_specs=[vmem, vmem],
-        out_specs=anywhere,
+        in_specs=[pl.BlockSpec(memory_space=pltpu.HBM), pl.BlockSpec(memory_space=pltpu.HBM)],
+        out_specs=pl.BlockSpec(memory_space=pltpu.HBM),
         scratch_shapes=[
+            pltpu.VMEM((mem_count, local, obs, LANES), obs_prior.dtype),
+            pltpu.VMEM(ens_state.shape, ens_state.dtype),
             pltpu.VMEM((mem_count, local, extra, LANES), ens_state.dtype),
-            pltpu.SemaphoreType.DMA((mem_count + 1,)),
+            pltpu.SemaphoreType.DMA((2, mem_count)),
+            pltpu.SemaphoreType.DMA((2,)),
         ],
         compiler_params=pltpu.CompilerParams(vmem_limit_bytes=16 * 2**20),
         name="pack",
-    )(near(obs_prior), near(ens_state))
+    )(obs_prior, ens_state)
     prior = lax.all_to_all(packed, "mem", split_axis=0, concat_axis=0, tiled=True)
     prior = prior.reshape(members, obs + extra, LANES)
     from_low = shift(pair_block, "grid", 1)

time: 73.3 us -> 73.8 us (level)
  no operation moved by 1% of the time
where the time goes in v5:
time: 73.8 us; the launch traced here: 73.5 us
  Pallas kernels  25.1 us (34%)
  starting transfers between devices  23.6 us (32%)
  waiting for transfers between devices  13.2 us (18%)
  blocking collectives  9.27 us (13%)
  local copies, waits for them, and re-layouts  2.15 us (3%)
    pallas_call x1, Pallas kernels, per_device(): pl.pallas_call(functools.partial(neighbour_kernel, members, obs, blocks_d...  12.5 us
    ppermute x4, starting transfers between devices, shift(): lax.ppermute(value, axis, [(i, (i + step) % count) for i in range(count)])  12.3 us
    all_to_all x1, blocking collectives, per_device(): lax.all_to_all(analysis, 'mem', split_axis=0, concat_axis=0, tiled=True)  9.27 us
    all_to_all x1, waiting for transfers between devices, per_device(): lax.all_to_all(packed, 'mem', split_axis=0, concat_axis=0, tiled=True)  6.34 us
    all_to_all x1, starting transfers between devices, per_device(): lax.all_to_all(packed, 'mem', split_axis=0, concat_axis=0, tiled=True)  6.07 us
    pallas_call x1, Pallas kernels, per_device(): pl.pallas_call(functools.partial(own_kernel, members, obs, blocks_dev, ch...  5.55 us
    all_to_all x1, waiting for transfers between devices, per_device(): lax.all_to_all(partial, 'mem', split_axis=0, concat_axis=0, tiled=True)  5.45 us
    all_to_all x1, starting transfers between devices, per_device(): lax.all_to_all(partial, 'mem', split_axis=0, concat_axis=0, tiled=True)  5.28 us
  transfers between devices with their start and end apart: 6, of which 3 were waited for; matrix products, arithmetic and copies ran while one was open for 0% of the time, Pallas kernels for 10%

profile of v5, /device:TPU:2, one launch (start us, length us, event | category | flops | bytes accessed | tf_op | source)
XLA Modules:
  0.0 73.5 jit_solution(2107110721245641685)
XLA Ops:
  0.0 0.0 copy-start
  0.0 1.2 %copy-done = bf16[10,384,128]{2,1,0:T(8,128)(2,1)S(1)} copy-done((bf16[10,384,128]{2,1,0:T(8,128)(2,1)S(1)}, bf16[10,384,128]{2,1,0:T(8,128)(2,1)}, u32[]{:S(2)}) %copy-start) | copy-done | bytes 983064
  1.2 0.0 copy-start.4
  1.2 0.9 %copy-done.4 = bf16[10,16,512]{2,1,0:T(8,128)(2,1)S(1)} copy-done((bf16[10,16,512]{2,1,0:T(8,128)(2,1)S(1)}, bf16[10,16,512]{2,1,0:T(8,128)(2,1)}, u32[]{:S(2)}) %copy-start.4) | copy-done | bytes 163864
  2.1 1.6 %pack.1 = bf16[8,10,56,128]{3,2,1,0:T(8,128)(2,1)} custom-call(bf16[10,384,128]{2,1,0:T(8,128)(2,1)S(1)} %copy-done, bf16[10,16,512]{2,1,0:T(8,128)(2,1)S(1)} %copy-done.4), custom_call_target="tpu_custom_call" | custom-call | tf_op jit(solution)/shard_map/pack/pallas_call | solution.py:266
  3.7 0.0 copy-start.5
  3.8 0.0 copy-start.1
  3.8 0.0 copy-start.2
  3.8 0.0 copy-start.3
  3.8 0.0 copy-start.6
  3.8 6.1 %all-to-all-start = ((bf16[8,10,56,128]{3,2,1,0:T(8,128)(2,1)}), bf16[8,10,56,128]{3,2,1,0:T(8,128)(2,1)S(1)}, u32[]{:S(2)}, u32[]{:S(2)}) async-start(bf16[8,10,56,128]{3,2,1,0:T(8,128)(2,1)} %pack.1), calls=%async_computation | async-start | bytes 2293760 | tf_op jit(solution)/shard_map/all_to_all | solution.py:281
  9.9 0.0 copy-done.5
  9.9 0.0 collective-permute-start
  9.9 6.4 %collective-permute-start.1 = (s32[16,256]{1,0:T(8,128)S(1)}, s32[16,256]{1,0:T(8,128)S(1)}, u32[]{:S(2)}, u32[]{:S(2)}) collective-permute-start(s32[16,256]{1,0:T(8,128)S(1)} %copy-done.5), channel_id=1, source_target_pairs={{0,31},{1,0},{2,1},{3,2},{4,3},{5,4},{6,5},{7,6},{8,7},{9,8},{10,9... | collective-permute-start | bytes 49160 | tf_op jit(solution)/shard_map/ppermute | solution.py:20
  16.3 1.4 %collective-permute-done.low_ref = s32[16,256]{1,0:T(8,128)S(1)} collective-permute-done((s32[16,256]{1,0:T(8,128)S(1)}, s32[16,256]{1,0:T(8,128)S(1)}, u32[]{:S(2)}, u32[]{:S(2)}) %collective-permute-start) | collective-permute-done | bytes 16416 | tf_op jit(solution)/shard_map/ppermute | solution.py:20
  17.7 0.0 collective-permute-done.1.high_ref
  17.7 0.0 copy-done.1
  17.7 0.0 copy-done.2
  17.7 0.0 copy-done.3
  17.7 0.0 copy-done.6
  17.7 1.4 %weights.1 = (f32[48,6144]{1,0:T(8,128)S(1)}, f32[96,128]{1,0:T(8,128)S(1)}) custom-call(s32[384]{0:T(512)S(1)} %copy-done.6, s32[16,256]{1,0:T(8,128)S(1)} %collective-permute-done.low_ref, s32[16,256]{1,0:T(8,128)S(1)} %copy-done.5, s32[16,256]{1,0:T(8,128)S(1)} %collective-permute-done.1.high_ref, f32[384,128]{1,0:T(8,128)S(1)} %copy-done.1, ...), custom_call_target="tpu_custom_call" | custom-call | tf_op jit(solution)/shard_map/weights/pallas_call | solution.py:287
  19.1 6.3 %all-to-all-done = bf16[8,10,56,128]{3,2,1,0:T(8,128)(2,1)S(1)} async-done(((bf16[8,10,56,128]{3,2,1,0:T(8,128)(2,1)}), bf16[8,10,56,128]{3,2,1,0:T(8,128)(2,1)S(1)}, u32[]{:S(2)}, u32[]{:S(2)}) %all-to-all-start) | async-done | bytes 1146912 | tf_op jit(solution)/shard_map/all_to_all | solution.py:281
  25.5 12.5 %neighbours.1 = (bf16[128,6144]{1,0:T(8,128)(2,1)S(1)}, bf16[640,128]{1,0:T(8,128)(2,1)S(1)}, bf16[640,128]{1,0:T(8,128)(2,1)S(1)}) custom-call(bf16[80,56,128]{2,1,0:T(8,128)(2,1)S(1)} %bitcast.3, f32[96,128]{1,0:T(8,128)S(1)} %get-tuple-element.12.aux_ref, f32[48,6144]{1,0:T(8,128)S(1)} %get-tuple-element.13.w_ref), custom_call_target="tpu_custom_call" | custom-call | tf_op jit(solution)/shard_map/neighbours/pallas_call | solution.py:306
  37.9 1.1 %collective-permute-start.2 = (bf16[640,128]{1,0:T(8,128)(2,1)S(1)}, bf16[640,128]{1,0:T(8,128)(2,1)S(1)}, u32[]{:S(2)}, u32[]{:S(2)}) collective-permute-start(bf16[640,128]{1,0:T(8,128)(2,1)S(1)} %get-tuple-element.15), channel_id=1, source_target_pairs={{0,1},{1,2},{2,3},{3,4},{4,5},{5,6},{6,7},{7,8},{8,9},{9,10},{10,1... | collective-permute-start | bytes 491528 | tf_op jit(solution)/shard_map/ppermute | solution.py:20
  39.1 4.8 %collective-permute-start.3 = (bf16[640,128]{1,0:T(8,128)(2,1)S(1)}, bf16[640,128]{1,0:T(8,128)(2,1)S(1)}, u32[]{:S(2)}, u32[]{:S(2)}) collective-permute-start(bf16[640,128]{1,0:T(8,128)(2,1)S(1)} %get-tuple-element.16), channel_id=1, source_target_pairs={{0,31},{1,0},{2,1},{3,2},{4,3},{5,4},{6,5},{7,6},{8,7},{9,8},{10,9... | collective-permute-start | bytes 491528 | tf_op jit(solution)/shard_map/ppermute | solution.py:20
  43.8 5.5 %own.1.own_ref = f32[640,128]{1,0:T(8,128)S(1)} custom-call(bf16[128,6144]{1,0:T(8,128)(2,1)S(1)} %get-tuple-element.14.d_ref, f32[48,6144]{1,0:T(8,128)S(1)} %get-tuple-element.13.w_ref), custom_call_target="tpu_custom_call" | custom-call | tf_op jit(solution)/shard_map/own/pallas_call | solution.py:320
  49.4 0.0 collective-permute-done.2.low_ref
  49.4 0.0 collective-permute-done.3.high_ref
  49.4 0.7 merge.1
  50.1 5.3 %all-to-all-start.1 = ((bf16[8,80,128]{2,1,0:T(8,128)(2,1)}), bf16[8,80,128]{2,1,0:T(8,128)(2,1)S(1)}, u32[]{:S(2)}, u32[]{:S(2)}) async-start(bf16[8,80,128]{2,1,0:T(8,128)(2,1)} %bitcast.1), calls=%async_computation.1 | async-start | bytes 327680 | tf_op jit(solution)/shard_map/all_to_all | solution.py:338
  55.4 0.2 state.1
  55.6 5.4 %all-to-all-done.1.system_ref = bf16[8,80,128]{2,1,0:T(8,128)(2,1)S(1)} async-done(((bf16[8,80,128]{2,1,0:T(8,128)(2,1)}), bf16[8,80,128]{2,1,0:T(8,128)(2,1)S(1)}, u32[]{:S(2)}, u32[]{:S(2)}) %all-to-all-start.1) | async-done | bytes 163872 | tf_op jit(solution)/shard_map/all_to_all | solution.py:338
  61.0 2.4 %finish.1 = bf16[640,128]{1,0:T(8,128)(2,1)S(1)} custom-call(bf16[8,80,128]{2,1,0:T(8,128)(2,1)S(1)} %all-to-all-done.1.system_ref, bf16[80,1024]{1,0:T(8,128)(2,1)S(1)} %get-tuple-element.17.dev_ref, f32[8,128]{1,0:T(8,128)S(1)} %get-tuple-element.18.mean_ref), custom_call_target="tpu_custom_call" | custom-call | tf_op jit(solution)/shard_map/finish/pallas_call | solution.py:351
  63.4 9.3 %all_to_all.15.part_ref = bf16[8,10,8,128]{3,2,1,0:T(8,128)(2,1)S(1)} all-to-all(bf16[8,10,8,128]{3,2,1,0:T(8,128)(2,1)S(1)} %bitcast.5), channel_id=1, replica_groups=mesh['mem'=8,'grid'=32] {'mem'}, dimensions={0} | all-to-all | bytes 327680 | tf_op jit(solution)/shard_map/all_to_all | solution.py:361
  72.7 0.8 %unpack.1 = bf16[10,16,512]{2,1,0:T(8,128)(2,1)} custom-call(bf16[8,10,8,128]{3,2,1,0:T(8,128)(2,1)S(1)} %all_to_all.15.part_ref), custom_call_target="tpu_custom_call" | custom-call | tf_op jit(solution)/shard_map/unpack/pallas_call | solution.py:362
Async XLA Ops:
  0.0 1.2 %copy-start = (bf16[10,384,128]{2,1,0:T(8,128)(2,1)S(1)}, bf16[10,384,128]{2,1,0:T(8,128)(2,1)}, u32[]{:S(2)}) copy-start(bf16[10,384,128]{2,1,0:T(8,128)(2,1)} %src_ref.1) | copy-start | bytes 2949124
  1.2 0.9 %copy-start.4 = (bf16[10,16,512]{2,1,0:T(8,128)(2,1)S(1)}, bf16[10,16,512]{2,1,0:T(8,128)(2,1)}, u32[]{:S(2)}) copy-start(bf16[10,16,512]{2,1,0:T(8,128)(2,1)} %state_all.1) | copy-start | bytes 491524
  3.7 6.1 %copy-start.5 = (s32[16,256]{1,0:T(8,128)S(1)}, s32[16,256]{1,0:T(8,128)}, u32[]{:S(2)}) copy-start(s32[16,256]{1,0:T(8,128)} %mid_ref.1) | copy-start | bytes 49156
  3.8 14.0 %copy-start.1 = (f32[384,128]{1,0:T(8,128)S(1)}, f32[384,128]{1,0:T(8,128)}, u32[]{:S(2)}) copy-start(f32[384,128]{1,0:T(8,128)} %prec_all.1) | copy-start | bytes 589828
  3.8 13.9 %copy-start.2 = (f32[384,128]{1,0:T(8,128)S(1)}, f32[384,128]{1,0:T(8,128)}, u32[]{:S(2)}) copy-start(f32[384,128]{1,0:T(8,128)} %pos_all.1) | copy-start | bytes 589828
  3.8 13.9 %copy-start.3 = (f32[384,128]{1,0:T(8,128)S(1)}, f32[384,128]{1,0:T(8,128)}, u32[]{:S(2)}) copy-start(f32[384,128]{1,0:T(8,128)} %value_all.1) | copy-start | bytes 589828
  3.8 13.9 %copy-start.6 = (s32[384]{0:T(512)S(1)}, s32[384]{0:T(512)}, u32[]{:S(2)}) copy-start(s32[384]{0:T(512)} %len_ref.1) | copy-start | bytes 4612
  3.8 21.7 %all-to-all-start = ((bf16[8,10,56,128]{3,2,1,0:T(8,128)(2,1)}), bf16[8,10,56,128]{3,2,1,0:T(8,128)(2,1)S(1)}, u32[]{:S(2)}, u32[]{:S(2)}) async-start(bf16[8,10,56,128]{3,2,1,0:T(8,128)(2,1)} %pack.1), calls=%async_computation | async-start | bytes 2293760 | tf_op jit(solution)/shard_map/all_to_all | solution.py:281
  9.9 7.8 %collective-permute-start = (s32[16,256]{1,0:T(8,128)S(1)}, s32[16,256]{1,0:T(8,128)S(1)}, u32[]{:S(2)}, u32[]{:S(2)}) collective-permute-start(s32[16,256]{1,0:T(8,128)S(1)} %copy-done.5), channel_id=1, source_target_pairs={{0,1},{1,2},{2,3},{3,4},{4,5},{5,6},{6,7},{7,8},{8,9},{9,10},{10,1... | collective-permute-start | bytes 49160 | tf_op jit(solution)/shard_map/ppermute | solution.py:20
  9.9 7.8 %collective-permute-start.1 = (s32[16,256]{1,0:T(8,128)S(1)}, s32[16,256]{1,0:T(8,128)S(1)}, u32[]{:S(2)}, u32[]{:S(2)}) collective-permute-start(s32[16,256]{1,0:T(8,128)S(1)} %copy-done.5), channel_id=1, source_target_pairs={{0,31},{1,0},{2,1},{3,2},{4,3},{5,4},{6,5},{7,6},{8,7},{9,8},{10,9... | collective-permute-start | bytes 49160 | tf_op jit(solution)/shard_map/ppermute | solution.py:20
  37.9 11.4 %collective-permute-start.2 = (bf16[640,128]{1,0:T(8,128)(2,1)S(1)}, bf16[640,128]{1,0:T(8,128)(2,1)S(1)}, u32[]{:S(2)}, u32[]{:S(2)}) collective-permute-start(bf16[640,128]{1,0:T(8,128)(2,1)S(1)} %get-tuple-element.15), channel_id=1, source_target_pairs={{0,1},{1,2},{2,3},{3,4},{4,5},{5,6},{6,7},{7,8},{8,9},{9,10},{10,1... | collective-permute-start | bytes 491528 | tf_op jit(solution)/shard_map/ppermute | solution.py:20
  39.1 10.3 %collective-permute-start.3 = (bf16[640,128]{1,0:T(8,128)(2,1)S(1)}, bf16[640,128]{1,0:T(8,128)(2,1)S(1)}, u32[]{:S(2)}, u32[]{:S(2)}) collective-permute-start(bf16[640,128]{1,0:T(8,128)(2,1)S(1)} %get-tuple-element.16), channel_id=1, source_target_pairs={{0,31},{1,0},{2,1},{3,2},{4,3},{5,4},{6,5},{7,6},{8,7},{9,8},{10,9... | collective-permute-start | bytes 491528 | tf_op jit(solution)/shard_map/ppermute | solution.py:20
  50.1 10.9 %all-to-all-start.1 = ((bf16[8,80,128]{2,1,0:T(8,128)(2,1)}), bf16[8,80,128]{2,1,0:T(8,128)(2,1)S(1)}, u32[]{:S(2)}, u32[]{:S(2)}) async-start(bf16[8,80,128]{2,1,0:T(8,128)(2,1)} %bitcast.1), calls=%async_computation.1 | async-start | bytes 327680 | tf_op jit(solution)/shard_map/all_to_all | solution.py:338

commit v6 on v5

--- a/solution.py
+++ b/solution.py
@@ -11,6 +11,8 @@
 NSIT = 3
 LOCR = 8
 LANES = 128
+COUNT = 127
+UNIT = 4
 
 inflation = 1.1
 
@@ -54,7 +56,7 @@
     state_out.wait()
 
 
-def weight_kernel(nb_total, obs, len_ref, low_ref, mid_ref, high_ref, prec_all, pos_all, value_all, out_ref, aux_ref, prec_ref, pos_ref, sems):
+def weight_kernel(nb_total, obs, len_ref, low_ref, mid_ref, high_ref, prec_all, pos_all, value_all, out_ref, aux_ref, list_ref, prec_ref, pos_ref, sems):
     place = lax.axis_index("mem")
     grid_pos = lax.axis_index("grid")
     grid_count = lax.axis_size("grid")
@@ -86,75 +88,91 @@
     ).astype(jnp.float32) + 0.5
     for copy in copies:
         copy.wait()
+    blocks = 3 * blocks_dev
+    slot = lax.broadcasted_iota(jnp.int32, (blocks, LANES), 1)
+    found = jnp.zeros((blocks, LANES), jnp.int32)
+    chosen = jnp.full((blocks, LANES), obs, jnp.int32)
     for o in range(obs):
         hit = jnp.max(jnp.where(pairs == o, 1.0, 0.0), axis=1, keepdims=True)
+        hit = jnp.broadcast_to(hit, (blocks, LANES)).astype(jnp.int32)
+        chosen = jnp.where(slot == jnp.where(hit > 0, found, -1), o, chosen)
+        found = found + hit
         gap = jnp.abs(pos_ref[o : o + 1, :] - centers)
         distance = jnp.minimum(gap, nb_total - gap)
         relative = distance * (1.0 / LOCR)
         weight = prec_ref[o : o + 1, :] * jnp.exp(-0.5 * relative * relative)
-        out_ref[:, o * LANES : (o + 1) * LANES] = jnp.where(hit > 0.0, weight, 0.0)
-
-
-def accumulate(members, obs, first, blocks, chunk, batch, d_ref, w_ref, acc_ref):
+        out_ref[pl.ds(o, blocks, stride=obs), :] = weight
+    out_ref[blocks * obs :, :] = jnp.zeros((8, LANES), jnp.float32)
+    list_ref[...] = jnp.where(slot == COUNT, found, chosen)
+
+
+def accumulate(members, obs, first, blocks, list_ref, d_ref, w_ref, acc_ref):
+    rows = d_ref.shape[1]
     acc_ref[...] = jnp.zeros(acc_ref.shape, jnp.float32)
-    width = chunk * LANES
-
-    def step(c, carry):
-        start = pl.multiple_of(c * width, width)
-        full = d_ref[:, pl.ds(start, width)]
-        d = full[:members].reshape(members // 16, 16, width)
-        for b0 in range(0, blocks, batch):
-            parts = []
-            for b in range(b0, b0 + batch):
-                row = w_ref[first + b : first + b + 1, pl.ds(start, width)]
-                w = jnp.broadcast_to(row, (16, width)).astype(jnp.bfloat16)
-                parts.append((d * w[None]).reshape(members, width))
-            scaled = jnp.concatenate(parts, axis=0)
-            acc_ref[b0 * members : (b0 + batch) * members, :] += lax.dot_general(
-                scaled, full, (((1,), (1,)), ((), ())), preferred_element_type=jnp.float32
+    longest = list_ref[first, COUNT]
+    for b in range(1, blocks):
+        longest = jnp.maximum(longest, list_ref[first + b, COUNT])
+
+    def step(turn, carry):
+        for b in range(blocks):
+            full, scaled = [], []
+            for k in range(UNIT):
+                o = list_ref[first + b, turn * UNIT + k]
+                d = d_ref[o]
+                row = w_ref[pl.ds((first + b) * obs + o, 1), :]
+                w = jnp.broadcast_to(row, (16, LANES)).astype(jnp.bfloat16)
+                full.append(d)
+                scaled.append((d[:members].reshape(members // 16, 16, LANES) * w[None]).reshape(members, LANES))
+            acc_ref[b * members : (b + 1) * members, 0:rows] += lax.dot_general(
+                jnp.concatenate(scaled, axis=1),
+                jnp.concatenate(full, axis=1),
+                (((1,), (1,)), ((), ())),
+                preferred_element_type=jnp.float32,
             )
         return carry
 
-    lax.fori_loop(0, obs // chunk, step, 0)
+    lax.fori_loop(0, (longest + UNIT - 1) // UNIT, step, 0)
 
 
 def packed_system(members, blocks, acc_ref, out_ref):
     half = members // 2
     lane = lax.broadcasted_iota(jnp.int32, (half, LANES), 1)
-    low = (lane == members + 2) | (lane == members + 3) | (lane >= LANES - half)
     for b in range(blocks):
         top = acc_ref[b * members : b * members + half, :]
         bottom = acc_ref[b * members + half : (b + 1) * members, :]
-        out_ref[b * half : (b + 1) * half, :] = jnp.where(low, bottom, top).astype(out_ref.dtype)
-
-
-def neighbour_kernel(members, obs, blocks, chunk, batch, prior_ref, aux_ref, w_ref, d_ref, low_ref, high_ref, dev_ref, acc_ref):
-    half = members // 2
+        corner = pltpu.roll(bottom, LANES - members, 1)
+        force = pltpu.roll(bottom, 2, 1)
+        value = jnp.where(lane >= members + 2, force, top)
+        value = jnp.where(lane >= LANES - half, corner, value)
+        out_ref[b * half : (b + 1) * half, :] = value.astype(out_ref.dtype)
+
+
+def neighbour_kernel(members, obs, blocks, list_ref, prior_ref, aux_ref, w_ref, d_ref, low_ref, high_ref, dev_ref, acc_ref):
+    rows = d_ref.shape[1]
     total = prior_ref[0, 0:obs].astype(jnp.float32)
     for i in range(1, members):
         total = total + prior_ref[i, 0:obs].astype(jnp.float32)
     mean = total / members
     valid = aux_ref[0:obs, :] > 0.0
     for i in range(members):
-        one = jnp.where(valid, prior_ref[i, 0:obs].astype(jnp.float32) - mean, 0.0)
-        dev_ref[i * obs : (i + 1) * obs, :] = one
-        if i >= half:
-            at = LANES - members + i
-            dev_ref[at * obs : (at + 1) * obs, :] = one
+        dev_ref[i * obs : (i + 1) * obs, :] = jnp.where(
+            valid, prior_ref[i, 0:obs].astype(jnp.float32) - mean, 0.0
+        )
     departure = jnp.where(valid, aux_ref[obs : 2 * obs, :] - mean, 0.0)
     high = departure.astype(jnp.bfloat16).astype(jnp.float32)
-    for k in range(LANES - half - members):
-        piece = (high, departure - high)[k % 2] if k < 4 else jnp.zeros(mean.shape, jnp.float32)
-        dev_ref[(members + k) * obs : (members + k + 1) * obs, :] = piece
+    dev_ref[members * obs : (members + 1) * obs, :] = high
+    dev_ref[(members + 1) * obs : (members + 2) * obs, :] = departure - high
+    dev_ref[(members + 2) * obs :, :] = jnp.zeros(((rows - members - 2) * obs, LANES), jnp.float32)
     for o in range(obs):
-        d_ref[:, o * LANES : (o + 1) * LANES] = dev_ref[pl.ds(o, LANES, stride=obs), :].astype(jnp.bfloat16)
+        d_ref[o] = dev_ref[pl.ds(o, rows, stride=obs), :].astype(jnp.bfloat16)
+    d_ref[obs] = jnp.zeros((rows, LANES), jnp.bfloat16)
     for first, out_ref in ((0, low_ref), (2 * blocks, high_ref)):
-        accumulate(members, obs, first, blocks, chunk, batch, d_ref, w_ref, acc_ref)
+        accumulate(members, obs, first, blocks, list_ref, d_ref, w_ref, acc_ref)
         packed_system(members, blocks, acc_ref, out_ref)
 
 
-def own_kernel(members, obs, blocks, chunk, batch, d_ref, w_ref, out_ref, acc_ref):
-    accumulate(members, obs, blocks, blocks, chunk, batch, d_ref, w_ref, acc_ref)
+def own_kernel(members, obs, blocks, list_ref, d_ref, w_ref, out_ref, acc_ref):
+    accumulate(members, obs, blocks, blocks, list_ref, d_ref, w_ref, acc_ref)
     packed_system(members, blocks, acc_ref, out_ref)
 
 
@@ -263,6 +281,10 @@
         return pltpu.with_memory_space_constraint(value, pltpu.VMEM)
 
     extra = pieces * owned
+
+    def far(value):
+        return pltpu.with_memory_space_constraint(value, pltpu.HBM)
+
     packed = pl.pallas_call(
         functools.partial(pack_kernel, mem_count, obs, owned),
         out_shape=jax.ShapeDtypeStruct((mem_count, local, obs + extra, LANES), obs_prior.dtype),
@@ -277,21 +299,22 @@
         ],
         compiler_params=pltpu.CompilerParams(vmem_limit_bytes=16 * 2**20),
         name="pack",
-    )(obs_prior, ens_state)
+    )(far(obs_prior), far(ens_state))
     prior = lax.all_to_all(packed, "mem", split_axis=0, concat_axis=0, tiled=True)
     prior = prior.reshape(members, obs + extra, LANES)
     from_low = shift(pair_block, "grid", 1)
     from_high = shift(pair_block, "grid", -1)
 
     blocks = 3 * blocks_dev
-    weights, aux = pl.pallas_call(
+    weights, aux, lists = pl.pallas_call(
         functools.partial(weight_kernel, float(nb_total), obs),
         out_shape=(
-            pltpu.VMEM((blocks, obs * LANES), jnp.float32),
+            pltpu.VMEM((blocks * obs + 8, LANES), jnp.float32),
             pltpu.VMEM((2 * obs, LANES), jnp.float32),
+            jax.ShapeDtypeStruct((blocks, LANES), jnp.int32),
         ),
         in_specs=[pl.BlockSpec(memory_space=pltpu.SMEM), vmem, vmem, vmem, anywhere, anywhere, anywhere],
-        out_specs=(vmem, vmem),
+        out_specs=(vmem, vmem, vmem),
         scratch_shapes=[
             pltpu.VMEM((obs, LANES), jnp.float32),
             pltpu.VMEM((obs, LANES), jnp.float32),
@@ -301,31 +324,32 @@
         name="weights",
     )(obs_len, near(from_low), pair_block, near(from_high), obs_prec, obs_pos, obs_value)
 
-    chunk, batch = 6, 4
+    rows = -(-(members + 2) // 16) * 16
+    scalars = pl.BlockSpec(memory_space=pltpu.SMEM)
     system = pltpu.VMEM((blocks_dev * half, LANES), jnp.bfloat16)
     d_all, to_low, to_high = pl.pallas_call(
-        functools.partial(neighbour_kernel, members, obs, blocks_dev, chunk, batch),
-        out_shape=(pltpu.VMEM((LANES, obs * LANES), jnp.bfloat16), system, system),
-        in_specs=[vmem, vmem, vmem],
+        functools.partial(neighbour_kernel, members, obs, blocks_dev),
+        out_shape=(pltpu.VMEM((obs + 1, rows, LANES), jnp.bfloat16), system, system),
+        in_specs=[scalars, vmem, vmem, vmem],
         out_specs=(vmem, vmem, vmem),
         scratch_shapes=[
-            pltpu.VMEM((LANES * obs, LANES), jnp.float32),
+            pltpu.VMEM((rows * obs, LANES), jnp.float32),
             pltpu.VMEM((blocks_dev * members, LANES), jnp.float32),
         ],
         compiler_params=pltpu.CompilerParams(vmem_limit_bytes=16 * 2**20),
         name="neighbours",
-    )(near(prior), near(aux), near(weights))
+    )(lists, near(prior), near(aux), near(weights))
     from_high = shift(to_low, "grid", -1)
     from_low = shift(to_high, "grid", 1)
     own = pl.pallas_call(
-        functools.partial(own_kernel, members, obs, blocks_dev, chunk, batch),
+        functools.partial(own_kernel, members, obs, blocks_dev),
         out_shape=pltpu.VMEM((blocks_dev * half, LANES), jnp.float32),
-        in_specs=[vmem, vmem],
+        in_specs=[scalars, vmem, vmem],
         out_specs=vmem,
         scratch_shapes=[pltpu.VMEM((blocks_dev * members, LANES), jnp.float32)],
         compiler_params=pltpu.CompilerParams(vmem_limit_bytes=16 * 2**20),
         name="own",
-    )(near(d_all), near(weights))
+    )(lists, near(d_all), near(weights))
     partial = pl.pallas_call(
         merge_kernel,
         out_shape=pltpu.VMEM((blocks_dev * half, LANES), jnp.bfloat16),

time: 73.8 us -> 66.3 us (0.90)
  the two profiles are of different devices: /device:TPU:2 before, /device:TPU:101 now
where the time goes in v6:
time: 66.3 us; the launch traced here: 66 us
  waiting for transfers between devices  20.3 us (31%)
  Pallas kernels  19.6 us (30%)
  starting transfers between devices  17.9 us (27%)
  blocking collectives  8.07 us (12%)
    ppermute x4, waiting for transfers between devices, shift(): lax.ppermute(value, axis, [(i, (i + step) % count) for i in range(count)])  11.7 us
    ppermute x4, starting transfers between devices, shift(): lax.ppermute(value, axis, [(i, (i + step) % count) for i in range(count)])  9.04 us
    all_to_all x1, blocking collectives, per_device(): lax.all_to_all(analysis, 'mem', split_axis=0, concat_axis=0, tiled=True)  8.07 us
    pallas_call x1, Pallas kernels, per_device(): pl.pallas_call(functools.partial(neighbour_kernel, members, obs, blocks_d...  7.36 us
    all_to_all x1, waiting for transfers between devices, per_device(): lax.all_to_all(partial, 'mem', split_axis=0, concat_axis=0, tiled=True)  5.51 us
    all_to_all x1, starting transfers between devices, per_device(): lax.all_to_all(packed, 'mem', split_axis=0, concat_axis=0, tiled=True)  4.97 us
    all_to_all x1, starting transfers between devices, per_device(): lax.all_to_all(partial, 'mem', split_axis=0, concat_axis=0, tiled=True)  3.92 us
    pallas_call x1, Pallas kernels, per_device(): pl.pallas_call(functools.partial(own_kernel, members, obs, blocks_dev), o...  3.72 us
  transfers between devices with their start and end apart: 6, of which 5 were waited for; matrix products, arithmetic and copies ran while one was open for 0% of the time, Pallas kernels for 9%

profile of v6, /device:TPU:101, one launch (start us, length us, event | category | flops | bytes accessed | tf_op | source)
XLA Modules:
  0.0 66.0 jit_solution(191714894291645052)
XLA Ops:
  0.0 2.6 %pack.1 = bf16[8,10,56,128]{3,2,1,0:T(8,128)(2,1)} custom-call(bf16[10,384,128]{2,1,0:T(8,128)(2,1)} %src_ref.1, bf16[10,16,512]{2,1,0:T(8,128)(2,1)} %state_all.1), custom_call_target="tpu_custom_call" | custom-call | tf_op jit(solution)/shard_map/pack/pallas_call | solution.py:288
  2.6 0.0 copy-start.3
  2.6 0.0 copy-start
  2.6 0.0 copy-start.1
  2.6 0.0 copy-start.2
  2.6 0.0 copy-start.4
  2.6 5.0 %all-to-all-start = ((bf16[8,10,56,128]{3,2,1,0:T(8,128)(2,1)}), bf16[8,10,56,128]{3,2,1,0:T(8,128)(2,1)S(1)}, u32[]{:S(2)}, u32[]{:S(2)}) async-start(bf16[8,10,56,128]{3,2,1,0:T(8,128)(2,1)} %pack.1), calls=%async_computation | async-start | bytes 2293760 | tf_op jit(solution)/shard_map/all_to_all | solution.py:303
  7.6 0.0 copy-done.3
  7.6 4.0 %collective-permute-start = (s32[16,256]{1,0:T(8,128)S(1)}, s32[16,256]{1,0:T(8,128)S(1)}, u32[]{:S(2)}, u32[]{:S(2)}) collective-permute-start(s32[16,256]{1,0:T(8,128)S(1)} %copy-done.3), channel_id=1, source_target_pairs={{0,1},{1,2},{2,3},{3,4},{4,5},{5,6},{6,7},{7,8},{8,9},{9,10},{10,1... | collective-permute-start | bytes 49160 | tf_op jit(solution)/shard_map/ppermute | solution.py:22
  11.6 0.0 collective-permute-start.1
  11.6 0.9 %collective-permute-done.low_ref = s32[16,256]{1,0:T(8,128)S(1)} collective-permute-done((s32[16,256]{1,0:T(8,128)S(1)}, s32[16,256]{1,0:T(8,128)S(1)}, u32[]{:S(2)}, u32[]{:S(2)}) %collective-permute-start) | collective-permute-done | bytes 16416 | tf_op jit(solution)/shard_map/ppermute | solution.py:22
  12.5 6.2 %collective-permute-done.1.high_ref = s32[16,256]{1,0:T(8,128)S(1)} collective-permute-done((s32[16,256]{1,0:T(8,128)S(1)}, s32[16,256]{1,0:T(8,128)S(1)}, u32[]{:S(2)}, u32[]{:S(2)}) %collective-permute-start.1) | collective-permute-done | bytes 16416 | tf_op jit(solution)/shard_map/ppermute | solution.py:22
  18.7 0.0 copy-done
  18.7 0.0 copy-done.1
  18.7 0.0 copy-done.2
  18.7 0.0 copy-done.4
  18.7 1.9 %weights.1 = (f32[2312,128]{1,0:T(8,128)S(1)}, f32[96,128]{1,0:T(8,128)S(1)}, s32[48,128]{1,0:T(8,128)S(1)}) custom-call(s32[384]{0:T(512)S(1)} %copy-done.4, s32[16,256]{1,0:T(8,128)S(1)} %collective-permute-done.low_ref, s32[16,256]{1,0:T(8,128)S(1)} %copy-done.3, s32[16,256]{1,0:T(8,128)S(1)} %collective-permute-done.1.high_ref, f32[384,128]{1,0:T(8,128)S(1)} %copy-done, ...), custom_call_target="tpu_custom_call" | custom-call | tf_op jit(solution)/shard_map/weights/pallas_call | solution.py:309
  20.6 3.1 %all-to-all-done = bf16[8,10,56,128]{3,2,1,0:T(8,128)(2,1)S(1)} async-done(((bf16[8,10,56,128]{3,2,1,0:T(8,128)(2,1)}), bf16[8,10,56,128]{3,2,1,0:T(8,128)(2,1)S(1)}, u32[]{:S(2)}, u32[]{:S(2)}) %all-to-all-start) | async-done | bytes 1146912 | tf_op jit(solution)/shard_map/all_to_all | solution.py:303
  23.7 7.4 %neighbours.1 = (bf16[49,96,128]{2,1,0:T(8,128)(2,1)S(1)}, bf16[640,128]{1,0:T(8,128)(2,1)S(1)}, bf16[640,128]{1,0:T(8,128)(2,1)S(1)}) custom-call(s32[48,128]{1,0:T(8,128)S(1)} %get-tuple-element.13.list_ref, bf16[80,56,128]{2,1,0:T(8,128)(2,1)S(1)} %bitcast.3, f32[96,128]{1,0:T(8,128)S(1)} %get-tuple-element.14.aux_ref, ...), custom_call_target="tpu_custom_call" | custom-call | tf_op jit(solution)/shard_map/neighbours/pallas_call | solution.py:330
  31.1 5.0 %collective-permute-start.2 = (bf16[640,128]{1,0:T(8,128)(2,1)S(1)}, bf16[640,128]{1,0:T(8,128)(2,1)S(1)}, u32[]{:S(2)}, u32[]{:S(2)}) collective-permute-start(bf16[640,128]{1,0:T(8,128)(2,1)S(1)} %get-tuple-element.17), channel_id=1, source_target_pairs={{0,1},{1,2},{2,3},{3,4},{4,5},{5,6},{6,7},{7,8},{8,9},{9,10},{10,1... | collective-permute-start | bytes 491528 | tf_op jit(solution)/shard_map/ppermute | solution.py:22
  36.1 0.0 collective-permute-start.3
  36.1 3.7 %own.1.own_ref = f32[640,128]{1,0:T(8,128)S(1)} custom-call(s32[48,128]{1,0:T(8,128)S(1)} %get-tuple-element.13.list_ref, bf16[49,96,128]{2,1,0:T(8,128)(2,1)S(1)} %get-tuple-element.16.d_ref, f32[2312,128]{1,0:T(8,128)S(1)} %get-tuple-element.15.w_ref), custom_call_target="tpu_custom_call" | custom-call | tf_op jit(solution)/shard_map/own/pallas_call | solution.py:344
  39.8 0.0 collective-permute-done.2.low_ref
  39.8 4.6 %collective-permute-done.3.high_ref = bf16[640,128]{1,0:T(8,128)(2,1)S(1)} collective-permute-done((bf16[640,128]{1,0:T(8,128)(2,1)S(1)}, bf16[640,128]{1,0:T(8,128)(2,1)S(1)}, u32[]{:S(2)}, u32[]{:S(2)}) %collective-permute-start.3) | collective-permute-done | bytes 163872 | tf_op jit(solution)/shard_map/ppermute | solution.py:22
  44.5 0.7 %merge.1 = bf16[640,128]{1,0:T(8,128)(2,1)} custom-call(f32[640,128]{1,0:T(8,128)S(1)} %own.1.own_ref, bf16[640,128]{1,0:T(8,128)(2,1)S(1)} %collective-permute-done.2.low_ref, bf16[640,128]{1,0:T(8,128)(2,1)S(1)} %collective-permute-done.3.high_ref), custom_call_target="tpu_custom_call" | custom-call | tf_op jit(solution)/shard_map/merge/pallas_call | solution.py:353
  45.2 3.9 %all-to-all-start.1 = ((bf16[8,80,128]{2,1,0:T(8,128)(2,1)}), bf16[8,80,128]{2,1,0:T(8,128)(2,1)S(1)}, u32[]{:S(2)}, u32[]{:S(2)}) async-start(bf16[8,80,128]{2,1,0:T(8,128)(2,1)} %bitcast.1), calls=%async_computation.1 | async-start | bytes 327680 | tf_op jit(solution)/shard_map/all_to_all | solution.py:362
  49.1 0.2 state.1
  49.3 5.5 %all-to-all-done.1.system_ref = bf16[8,80,128]{2,1,0:T(8,128)(2,1)S(1)} async-done(((bf16[8,80,128]{2,1,0:T(8,128)(2,1)}), bf16[8,80,128]{2,1,0:T(8,128)(2,1)S(1)}, u32[]{:S(2)}, u32[]{:S(2)}) %all-to-all-start.1) | async-done | bytes 163872 | tf_op jit(solution)/shard_map/all_to_all | solution.py:362
  54.8 2.4 %finish.1 = bf16[640,128]{1,0:T(8,128)(2,1)S(1)} custom-call(bf16[8,80,128]{2,1,0:T(8,128)(2,1)S(1)} %all-to-all-done.1.system_ref, bf16[80,1024]{1,0:T(8,128)(2,1)S(1)} %get-tuple-element.19.dev_ref, f32[8,128]{1,0:T(8,128)S(1)} %get-tuple-element.20.mean_ref), custom_call_target="tpu_custom_call" | custom-call | tf_op jit(solution)/shard_map/finish/pallas_call | solution.py:375
  57.2 8.1 %all_to_all.15.part_ref = bf16[8,10,8,128]{3,2,1,0:T(8,128)(2,1)S(1)} all-to-all(bf16[8,10,8,128]{3,2,1,0:T(8,128)(2,1)S(1)} %bitcast.5), channel_id=1, replica_groups=mesh['mem'=8,'grid'=32] {'mem'}, dimensions={0} | all-to-all | bytes 327680 | tf_op jit(solution)/shard_map/all_to_all | solution.py:385
  65.3 0.8 %unpack.1 = bf16[10,16,512]{2,1,0:T(8,128)(2,1)} custom-call(bf16[8,10,8,128]{3,2,1,0:T(8,128)(2,1)S(1)} %all_to_all.15.part_ref), custom_call_target="tpu_custom_call" | custom-call | tf_op jit(solution)/shard_map/unpack/pallas_call | solution.py:386
Async XLA Ops:
  2.6 5.0 %copy-start.3 = (s32[16,256]{1,0:T(8,128)S(1)}, s32[16,256]{1,0:T(8,128)}, u32[]{:S(2)}) copy-start(s32[16,256]{1,0:T(8,128)} %mid_ref.1) | copy-start | bytes 49156
  2.6 16.1 %copy-start = (f32[384,128]{1,0:T(8,128)S(1)}, f32[384,128]{1,0:T(8,128)}, u32[]{:S(2)}) copy-start(f32[384,128]{1,0:T(8,128)} %prec_all.1) | copy-start | bytes 589828
  2.6 16.1 %copy-start.1 = (f32[384,128]{1,0:T(8,128)S(1)}, f32[384,128]{1,0:T(8,128)}, u32[]{:S(2)}) copy-start(f32[384,128]{1,0:T(8,128)} %pos_all.1) | copy-start | bytes 589828
  2.6 16.1 %copy-start.2 = (f32[384,128]{1,0:T(8,128)S(1)}, f32[384,128]{1,0:T(8,128)}, u32[]{:S(2)}) copy-start(f32[384,128]{1,0:T(8,128)} %value_all.1) | copy-start | bytes 589828
  2.6 16.1 %copy-start.4 = (s32[384]{0:T(512)S(1)}, s32[384]{0:T(512)}, u32[]{:S(2)}) copy-start(s32[384]{0:T(512)} %len_ref.1) | copy-start | bytes 4612
  2.6 21.1 %all-to-all-start = ((bf16[8,10,56,128]{3,2,1,0:T(8,128)(2,1)}), bf16[8,10,56,128]{3,2,1,0:T(8,128)(2,1)S(1)}, u32[]{:S(2)}, u32[]{:S(2)}) async-start(bf16[8,10,56,128]{3,2,1,0:T(8,128)(2,1)} %pack.1), calls=%async_computation | async-start | bytes 2293760 | tf_op jit(solution)/shard_map/all_to_all | solution.py:303
  7.6 4.9 %collective-permute-start = (s32[16,256]{1,0:T(8,128)S(1)}, s32[16,256]{1,0:T(8,128)S(1)}, u32[]{:S(2)}, u32[]{:S(2)}) collective-permute-start(s32[16,256]{1,0:T(8,128)S(1)} %copy-done.3), channel_id=1, source_target_pairs={{0,1},{1,2},{2,3},{3,4},{4,5},{5,6},{6,7},{7,8},{8,9},{9,10},{10,1... | collective-permute-start | bytes 49160 | tf_op jit(solution)/shard_map/ppermute | solution.py:22
  11.6 7.1 %collective-permute-start.1 = (s32[16,256]{1,0:T(8,128)S(1)}, s32[16,256]{1,0:T(8,128)S(1)}, u32[]{:S(2)}, u32[]{:S(2)}) collective-permute-start(s32[16,256]{1,0:T(8,128)S(1)} %copy-done.3), channel_id=1, source_target_pairs={{0,31},{1,0},{2,1},{3,2},{4,3},{5,4},{6,5},{7,6},{8,7},{9,8},{10,9... | collective-permute-start | bytes 49160 | tf_op jit(solution)/shard_map/ppermute | solution.py:22
  31.1 8.8 %collective-permute-start.2 = (bf16[640,128]{1,0:T(8,128)(2,1)S(1)}, bf16[640,128]{1,0:T(8,128)(2,1)S(1)}, u32[]{:S(2)}, u32[]{:S(2)}) collective-permute-start(bf16[640,128]{1,0:T(8,128)(2,1)S(1)} %get-tuple-element.17), channel_id=1, source_target_pairs={{0,1},{1,2},{2,3},{3,4},{4,5},{5,6},{6,7},{7,8},{8,9},{9,10},{10,1... | collective-permute-start | bytes 491528 | tf_op jit(solution)/shard_map/ppermute | solution.py:22
  36.1 8.4 %collective-permute-start.3 = (bf16[640,128]{1,0:T(8,128)(2,1)S(1)}, bf16[640,128]{1,0:T(8,128)(2,1)S(1)}, u32[]{:S(2)}, u32[]{:S(2)}) collective-permute-start(bf16[640,128]{1,0:T(8,128)(2,1)S(1)} %get-tuple-element.18), channel_id=1, source_target_pairs={{0,31},{1,0},{2,1},{3,2},{4,3},{5,4},{6,5},{7,6},{8,7},{9,8},{10,9... | collective-permute-start | bytes 491528 | tf_op jit(solution)/shard_map/ppermute | solution.py:22
  45.2 9.6 %all-to-all-start.1 = ((bf16[8,80,128]{2,1,0:T(8,128)(2,1)}), bf16[8,80,128]{2,1,0:T(8,128)(2,1)S(1)}, u32[]{:S(2)}, u32[]{:S(2)}) async-start(bf16[8,80,128]{2,1,0:T(8,128)(2,1)} %bitcast.1), calls=%async_computation.1 | async-start | bytes 327680 | tf_op jit(solution)/shard_map/all_to_all | solution.py:362

commit v7 on v6

--- a/solution.py
+++ b/solution.py
@@ -17,9 +17,16 @@
 inflation = 1.1
 
 
-def shift(value, axis, step):
-    count = lax.axis_size(axis)
-    return lax.ppermute(value, axis, [(i, (i + step) % count) for i in range(count)])
+def shift(value, step):
+    mem_count = lax.axis_size("mem")
+    grid_count = lax.axis_size("grid")
+    pairs = []
+    for m in range(mem_count):
+        for g in range(grid_count):
+            crossing = g % 2 == (1 if step > 0 else 0)
+            other = m ^ 1 if crossing and mem_count % 2 == 0 else m
+            pairs.append((m * grid_count + g, other * grid_count + (g + step) % grid_count))
+    return lax.ppermute(value, ("mem", "grid"), pairs)
 
 
 def pack_kernel(parts, size, owned, src_ref, state_all, out_ref, stage_ref, state_ref, rows_ref, sems, last):
@@ -56,7 +63,7 @@
     state_out.wait()
 
 
-def weight_kernel(nb_total, obs, len_ref, low_ref, mid_ref, high_ref, prec_all, pos_all, value_all, out_ref, aux_ref, list_ref, prec_ref, pos_ref, sems):
+def weight_kernel(nb_total, obs, len_ref, low_ref, mid_ref, high_ref, prec_all, pos_all, value_all, out_ref, aux_ref, list_ref, prec_ref, pos_ref, table_ref, sems):
     place = lax.axis_index("mem")
     grid_pos = lax.axis_index("grid")
     grid_count = lax.axis_size("grid")
@@ -103,7 +110,10 @@
         weight = prec_ref[o : o + 1, :] * jnp.exp(-0.5 * relative * relative)
         out_ref[pl.ds(o, blocks, stride=obs), :] = weight
     out_ref[blocks * obs :, :] = jnp.zeros((8, LANES), jnp.float32)
-    list_ref[...] = jnp.where(slot == COUNT, found, chosen)
+    table_ref[...] = jnp.where(slot == COUNT, found, chosen)
+    copy = pltpu.make_async_copy(table_ref, list_ref, sems.at[3])
+    copy.start()
+    copy.wait()
 
 
 def accumulate(members, obs, first, blocks, list_ref, d_ref, w_ref, acc_ref):
@@ -302,8 +312,8 @@
     )(far(obs_prior), far(ens_state))
     prior = lax.all_to_all(packed, "mem", split_axis=0, concat_axis=0, tiled=True)
     prior = prior.reshape(members, obs + extra, LANES)
-    from_low = shift(pair_block, "grid", 1)
-    from_high = shift(pair_block, "grid", -1)
+    from_low = shift(pair_block, 1)
+    from_high = shift(pair_block, -1)
 
     blocks = 3 * blocks_dev
     weights, aux, lists = pl.pallas_call(
@@ -311,14 +321,15 @@
         out_shape=(
             pltpu.VMEM((blocks * obs + 8, LANES), jnp.float32),
             pltpu.VMEM((2 * obs, LANES), jnp.float32),
-            jax.ShapeDtypeStruct((blocks, LANES), jnp.int32),
+            pltpu.SMEM((blocks, LANES), jnp.int32),
         ),
         in_specs=[pl.BlockSpec(memory_space=pltpu.SMEM), vmem, vmem, vmem, anywhere, anywhere, anywhere],
-        out_specs=(vmem, vmem, vmem),
+        out_specs=(vmem, vmem, pl.BlockSpec(memory_space=pltpu.SMEM)),
         scratch_shapes=[
             pltpu.VMEM((obs, LANES), jnp.float32),
             pltpu.VMEM((obs, LANES), jnp.float32),
-            pltpu.SemaphoreType.DMA((3,)),
+            pltpu.VMEM((blocks, LANES), jnp.int32),
+            pltpu.SemaphoreType.DMA((4,)),
         ],
         compiler_params=pltpu.CompilerParams(vmem_limit_bytes=16 * 2**20),
         name="weights",
@@ -338,9 +349,9 @@
         ],
         compiler_params=pltpu.CompilerParams(vmem_limit_bytes=16 * 2**20),
         name="neighbours",
-    )(lists, near(prior), near(aux), near(weights))
-    from_high = shift(to_low, "grid", -1)
-    from_low = shift(to_high, "grid", 1)
+    )(pltpu.with_memory_space_constraint(lists, pltpu.SMEM), near(prior), near(aux), near(weights))
+    from_high = shift(to_low, -1)
+    from_low = shift(to_high, 1)
     own = pl.pallas_call(
         functools.partial(own_kernel, members, obs, blocks_dev),
         out_shape=pltpu.VMEM((blocks_dev * half, LANES), jnp.float32),
@@ -349,7 +360,7 @@
         scratch_shapes=[pltpu.VMEM((blocks_dev * members, LANES), jnp.float32)],
         compiler_params=pltpu.CompilerParams(vmem_limit_bytes=16 * 2**20),
         name="own",
-    )(lists, near(d_all), near(weights))
+    )(pltpu.with_memory_space_constraint(lists, pltpu.SMEM), near(d_all), near(weights))
     partial = pl.pallas_call(
         merge_kernel,
         out_shape=pltpu.VMEM((blocks_dev * half, LANES), jnp.bfloat16),

time: 66.3 us -> 64.8 us (0.977)
  the two profiles are of different devices: /device:TPU:101 before, /device:TPU:2 now
where the time goes in v7:
time: 64.8 us; the launch traced here: 64.5 us
  starting transfers between devices  22.9 us (35%)
  Pallas kernels  19.3 us (30%)
  waiting for transfers between devices  12.9 us (20%)
  blocking collectives  9.29 us (14%)
    ppermute x4, starting transfers between devices, shift(): return lax.ppermute(value, ('mem', 'grid'), pairs)  10.9 us
    all_to_all x1, blocking collectives, per_device(): lax.all_to_all(analysis, 'mem', split_axis=0, concat_axis=0, tiled=True)  9.29 us
    pallas_call x1, Pallas kernels, per_device(): pl.pallas_call(functools.partial(neighbour_kernel, members, obs, blocks_d...  6.48 us
    all_to_all x1, starting transfers between devices, per_device(): lax.all_to_all(packed, 'mem', split_axis=0, concat_axis=0, tiled=True)  6.07 us
    all_to_all x1, waiting for transfers between devices, per_device(): lax.all_to_all(packed, 'mem', split_axis=0, concat_axis=0, tiled=True)  6 us
    all_to_all x1, starting transfers between devices, per_device(): lax.all_to_all(partial, 'mem', split_axis=0, concat_axis=0, tiled=True)  5.88 us
    all_to_all x1, waiting for transfers between devices, per_device(): lax.all_to_all(partial, 'mem', split_axis=0, concat_axis=0, tiled=True)  5.42 us
    pallas_call x1, Pallas kernels, per_device(): pl.pallas_call(functools.partial(own_kernel, members, obs, blocks_dev), o...  3.4 us
  transfers between devices with their start and end apart: 6, of which 4 were waited for; matrix products, arithmetic and copies ran while one was open for 0% of the time, Pallas kernels for 10%

profile of v7, /device:TPU:2, one launch (start us, length us, event | category | flops | bytes accessed | tf_op | source)
XLA Modules:
  0.0 64.5 jit_solution(15695995087326024159)
XLA Ops:
  0.0 2.6 %pack.1 = bf16[8,10,56,128]{3,2,1,0:T(8,128)(2,1)} custom-call(bf16[10,384,128]{2,1,0:T(8,128)(2,1)} %src_ref.1, bf16[10,16,512]{2,1,0:T(8,128)(2,1)} %state_all.1), custom_call_target="tpu_custom_call" | custom-call | tf_op jit(solution)/shard_map/pack/pallas_call | solution.py:298
  2.6 0.0 copy-start.3
  2.6 0.0 copy-start
  2.6 0.0 copy-start.1
  2.6 0.0 copy-start.2
  2.6 0.0 copy-start.4
  2.6 6.1 %all-to-all-start = ((bf16[8,10,56,128]{3,2,1,0:T(8,128)(2,1)}), bf16[8,10,56,128]{3,2,1,0:T(8,128)(2,1)S(1)}, u32[]{:S(2)}, u32[]{:S(2)}) async-start(bf16[8,10,56,128]{3,2,1,0:T(8,128)(2,1)} %pack.1), calls=%async_computation | async-start | bytes 2293760 | tf_op jit(solution)/shard_map/all_to_all | solution.py:313
  8.7 0.0 copy-done.3
  8.7 0.0 collective-permute-start
  8.7 5.3 %collective-permute-start.1 = (s32[16,256]{1,0:T(8,128)S(1)}, s32[16,256]{1,0:T(8,128)S(1)}, u32[]{:S(2)}, u32[]{:S(2)}) collective-permute-start(s32[16,256]{1,0:T(8,128)S(1)} %copy-done.3), channel_id=1, source_target_pairs={{0,63},{1,0},{2,33},{3,2},{4,35},{5,4},{6,37},{7,6},{8,39},{9,8},{... | collective-permute-start | bytes 49160 | tf_op jit(solution)/shard_map/ppermute | solution.py:29
  14.0 1.3 %collective-permute-done.low_ref = s32[16,256]{1,0:T(8,128)S(1)} collective-permute-done((s32[16,256]{1,0:T(8,128)S(1)}, s32[16,256]{1,0:T(8,128)S(1)}, u32[]{:S(2)}, u32[]{:S(2)}) %collective-permute-start) | collective-permute-done | bytes 16416 | tf_op jit(solution)/shard_map/ppermute | solution.py:29
  15.3 0.1 collective-permute-done.1.high_ref
  15.4 0.0 copy-done
  15.4 0.0 copy-done.1
  15.4 0.0 copy-done.2
  15.4 0.0 copy-done.4
  15.4 2.8 %weights.1 = (f32[2312,128]{1,0:T(8,128)S(1)}, f32[96,128]{1,0:T(8,128)S(1)}, s32[48,128]{1,0:T(8,128)S(4)}) custom-call(s32[384]{0:T(512)S(1)} %copy-done.4, s32[16,256]{1,0:T(8,128)S(1)} %collective-permute-done.low_ref, s32[16,256]{1,0:T(8,128)S(1)} %copy-done.3, s32[16,256]{1,0:T(8,128)S(1)} %collective-permute-done.1.high_ref, f32[384,128]{1,0:T(8,128)S(1)} %copy-done, ...), custom_call_target="tpu_custom_call" | custom-call | tf_op jit(solution)/shard_map/weights/pallas_call | solution.py:319
  18.3 6.0 %all-to-all-done = bf16[8,10,56,128]{3,2,1,0:T(8,128)(2,1)S(1)} async-done(((bf16[8,10,56,128]{3,2,1,0:T(8,128)(2,1)}), bf16[8,10,56,128]{3,2,1,0:T(8,128)(2,1)S(1)}, u32[]{:S(2)}, u32[]{:S(2)}) %all-to-all-start) | async-done | bytes 1146912 | tf_op jit(solution)/shard_map/all_to_all | solution.py:313
  24.3 6.5 %neighbours.1 = (bf16[49,96,128]{2,1,0:T(8,128)(2,1)S(1)}, bf16[640,128]{1,0:T(8,128)(2,1)S(1)}, bf16[640,128]{1,0:T(8,128)(2,1)S(1)}) custom-call(s32[48,128]{1,0:T(8,128)S(4)} %get-tuple-element.13.list_ref, bf16[80,56,128]{2,1,0:T(8,128)(2,1)S(1)} %bitcast.3, f32[96,128]{1,0:T(8,128)S(1)} %get-tuple-element.14.aux_ref, ...), custom_call_target="tpu_custom_call" | custom-call | tf_op jit(solution)/shard_map/neighbours/pallas_call | solution.py:341
  30.8 0.1 collective-permute-start.2
  30.9 5.6 %collective-permute-start.3 = (bf16[640,128]{1,0:T(8,128)(2,1)S(1)}, bf16[640,128]{1,0:T(8,128)(2,1)S(1)}, u32[]{:S(2)}, u32[]{:S(2)}) collective-permute-start(bf16[640,128]{1,0:T(8,128)(2,1)S(1)} %get-tuple-element.18), channel_id=1, source_target_pairs={{0,63},{1,0},{2,33},{3,2},{4,35},{5,4},{6,37},{7,6},{8,39},{9,8},{... | collective-permute-start | bytes 491528 | tf_op jit(solution)/shard_map/ppermute | solution.py:29
  36.4 3.4 %own.1.own_ref = f32[640,128]{1,0:T(8,128)S(1)} custom-call(s32[48,128]{1,0:T(8,128)S(4)} %get-tuple-element.13.list_ref, bf16[49,96,128]{2,1,0:T(8,128)(2,1)S(1)} %get-tuple-element.16.d_ref, f32[2312,128]{1,0:T(8,128)S(1)} %get-tuple-element.15.w_ref), custom_call_target="tpu_custom_call" | custom-call | tf_op jit(solution)/shard_map/own/pallas_call | solution.py:355
  39.8 0.0 collective-permute-done.2.low_ref
  39.9 0.0 collective-permute-done.3.high_ref
  39.9 0.7 %merge.1 = bf16[640,128]{1,0:T(8,128)(2,1)} custom-call(f32[640,128]{1,0:T(8,128)S(1)} %own.1.own_ref, bf16[640,128]{1,0:T(8,128)(2,1)S(1)} %collective-permute-done.2.low_ref, bf16[640,128]{1,0:T(8,128)(2,1)S(1)} %collective-permute-done.3.high_ref), custom_call_target="tpu_custom_call" | custom-call | tf_op jit(solution)/shard_map/merge/pallas_call | solution.py:364
  40.6 5.9 %all-to-all-start.1 = ((bf16[8,80,128]{2,1,0:T(8,128)(2,1)}), bf16[8,80,128]{2,1,0:T(8,128)(2,1)S(1)}, u32[]{:S(2)}, u32[]{:S(2)}) async-start(bf16[8,80,128]{2,1,0:T(8,128)(2,1)} %bitcast.1), calls=%async_computation.1 | async-start | bytes 327680 | tf_op jit(solution)/shard_map/all_to_all | solution.py:373
  46.5 0.2 state.1
  46.6 5.4 %all-to-all-done.1.system_ref = bf16[8,80,128]{2,1,0:T(8,128)(2,1)S(1)} async-done(((bf16[8,80,128]{2,1,0:T(8,128)(2,1)}), bf16[8,80,128]{2,1,0:T(8,128)(2,1)S(1)}, u32[]{:S(2)}, u32[]{:S(2)}) %all-to-all-start.1) | async-done | bytes 163872 | tf_op jit(solution)/shard_map/all_to_all | solution.py:373
  52.1 2.4 %finish.1 = bf16[640,128]{1,0:T(8,128)(2,1)S(1)} custom-call(bf16[8,80,128]{2,1,0:T(8,128)(2,1)S(1)} %all-to-all-done.1.system_ref, bf16[80,1024]{1,0:T(8,128)(2,1)S(1)} %get-tuple-element.19.dev_ref, f32[8,128]{1,0:T(8,128)S(1)} %get-tuple-element.20.mean_ref), custom_call_target="tpu_custom_call" | custom-call | tf_op jit(solution)/shard_map/finish/pallas_call | solution.py:386
  54.5 9.3 %all_to_all.15.part_ref = bf16[8,10,8,128]{3,2,1,0:T(8,128)(2,1)S(1)} all-to-all(bf16[8,10,8,128]{3,2,1,0:T(8,128)(2,1)S(1)} %bitcast.5), channel_id=1, replica_groups=mesh['mem'=8,'grid'=32] {'mem'}, dimensions={0} | all-to-all | bytes 327680 | tf_op jit(solution)/shard_map/all_to_all | solution.py:396
  63.8 0.8 %unpack.1 = bf16[10,16,512]{2,1,0:T(8,128)(2,1)} custom-call(bf16[8,10,8,128]{3,2,1,0:T(8,128)(2,1)S(1)} %all_to_all.15.part_ref), custom_call_target="tpu_custom_call" | custom-call | tf_op jit(solution)/shard_map/unpack/pallas_call | solution.py:397
Async XLA Ops:
  2.6 6.1 %copy-start.3 = (s32[16,256]{1,0:T(8,128)S(1)}, s32[16,256]{1,0:T(8,128)}, u32[]{:S(2)}) copy-start(s32[16,256]{1,0:T(8,128)} %mid_ref.1) | copy-start | bytes 49156
  2.6 12.9 %copy-start = (f32[384,128]{1,0:T(8,128)S(1)}, f32[384,128]{1,0:T(8,128)}, u32[]{:S(2)}) copy-start(f32[384,128]{1,0:T(8,128)} %prec_all.1) | copy-start | bytes 589828
  2.6 12.8 %copy-start.1 = (f32[384,128]{1,0:T(8,128)S(1)}, f32[384,128]{1,0:T(8,128)}, u32[]{:S(2)}) copy-start(f32[384,128]{1,0:T(8,128)} %pos_all.1) | copy-start | bytes 589828
  2.6 12.8 %copy-start.2 = (f32[384,128]{1,0:T(8,128)S(1)}, f32[384,128]{1,0:T(8,128)}, u32[]{:S(2)}) copy-start(f32[384,128]{1,0:T(8,128)} %value_all.1) | copy-start | bytes 589828
  2.6 12.8 %copy-start.4 = (s32[384]{0:T(512)S(1)}, s32[384]{0:T(512)}, u32[]{:S(2)}) copy-start(s32[384]{0:T(512)} %len_ref.1) | copy-start | bytes 4612
  2.6 21.7 %all-to-all-start = ((bf16[8,10,56,128]{3,2,1,0:T(8,128)(2,1)}), bf16[8,10,56,128]{3,2,1,0:T(8,128)(2,1)S(1)}, u32[]{:S(2)}, u32[]{:S(2)}) async-start(bf16[8,10,56,128]{3,2,1,0:T(8,128)(2,1)} %pack.1), calls=%async_computation | async-start | bytes 2293760 | tf_op jit(solution)/shard_map/all_to_all | solution.py:313
  8.7 6.6 %collective-permute-start = (s32[16,256]{1,0:T(8,128)S(1)}, s32[16,256]{1,0:T(8,128)S(1)}, u32[]{:S(2)}, u32[]{:S(2)}) collective-permute-start(s32[16,256]{1,0:T(8,128)S(1)} %copy-done.3), channel_id=1, source_target_pairs={{0,1},{1,34},{2,3},{3,36},{4,5},{5,38},{6,7},{7,40},{8,9},{9,42},{... | collective-permute-start | bytes 49160 | tf_op jit(solution)/shard_map/ppermute | solution.py:29
  8.7 6.7 %collective-permute-start.1 = (s32[16,256]{1,0:T(8,128)S(1)}, s32[16,256]{1,0:T(8,128)S(1)}, u32[]{:S(2)}, u32[]{:S(2)}) collective-permute-start(s32[16,256]{1,0:T(8,128)S(1)} %copy-done.3), channel_id=1, source_target_pairs={{0,63},{1,0},{2,33},{3,2},{4,35},{5,4},{6,37},{7,6},{8,39},{9,8},{... | collective-permute-start | bytes 49160 | tf_op jit(solution)/shard_map/ppermute | solution.py:29
  30.8 9.1 %collective-permute-start.2 = (bf16[640,128]{1,0:T(8,128)(2,1)S(1)}, bf16[640,128]{1,0:T(8,128)(2,1)S(1)}, u32[]{:S(2)}, u32[]{:S(2)}) collective-permute-start(bf16[640,128]{1,0:T(8,128)(2,1)S(1)} %get-tuple-element.17), channel_id=1, source_target_pairs={{0,1},{1,34},{2,3},{3,36},{4,5},{5,38},{6,7},{7,40},{8,9},{9,42},{... | collective-permute-start | bytes 491528 | tf_op jit(solution)/shard_map/ppermute | solution.py:29
  30.9 9.0 %collective-permute-start.3 = (bf16[640,128]{1,0:T(8,128)(2,1)S(1)}, bf16[640,128]{1,0:T(8,128)(2,1)S(1)}, u32[]{:S(2)}, u32[]{:S(2)}) collective-permute-start(bf16[640,128]{1,0:T(8,128)(2,1)S(1)} %get-tuple-element.18), channel_id=1, source_target_pairs={{0,63},{1,0},{2,33},{3,2},{4,35},{5,4},{6,37},{7,6},{8,39},{9,8},{... | collective-permute-start | bytes 491528 | tf_op jit(solution)/shard_map/ppermute | solution.py:29
  40.6 11.5 %all-to-all-start.1 = ((bf16[8,80,128]{2,1,0:T(8,128)(2,1)}), bf16[8,80,128]{2,1,0:T(8,128)(2,1)S(1)}, u32[]{:S(2)}, u32[]{:S(2)}) async-start(bf16[8,80,128]{2,1,0:T(8,128)(2,1)} %bitcast.1), calls=%async_computation.1 | async-start | bytes 327680 | tf_op jit(solution)/shard_map/all_to_all | solution.py:373

commit v8 on v7

--- a/solution.py
+++ b/solution.py
@@ -157,7 +157,7 @@
         out_ref[b * half : (b + 1) * half, :] = value.astype(out_ref.dtype)
 
 
-def neighbour_kernel(members, obs, blocks, list_ref, prior_ref, aux_ref, w_ref, d_ref, low_ref, high_ref, dev_ref, acc_ref):
+def low_kernel(members, obs, blocks, list_ref, prior_ref, aux_ref, w_ref, d_ref, low_ref, dev_ref, acc_ref):
     rows = d_ref.shape[1]
     total = prior_ref[0, 0:obs].astype(jnp.float32)
     for i in range(1, members):
@@ -176,13 +176,12 @@
     for o in range(obs):
         d_ref[o] = dev_ref[pl.ds(o, rows, stride=obs), :].astype(jnp.bfloat16)
     d_ref[obs] = jnp.zeros((rows, LANES), jnp.bfloat16)
-    for first, out_ref in ((0, low_ref), (2 * blocks, high_ref)):
-        accumulate(members, obs, first, blocks, list_ref, d_ref, w_ref, acc_ref)
-        packed_system(members, blocks, acc_ref, out_ref)
-
-
-def own_kernel(members, obs, blocks, list_ref, d_ref, w_ref, out_ref, acc_ref):
-    accumulate(members, obs, blocks, blocks, list_ref, d_ref, w_ref, acc_ref)
+    accumulate(members, obs, 0, blocks, list_ref, d_ref, w_ref, acc_ref)
+    packed_system(members, blocks, acc_ref, low_ref)
+
+
+def next_kernel(members, obs, first, blocks, list_ref, d_ref, w_ref, out_ref, acc_ref):
+    accumulate(members, obs, first, blocks, list_ref, d_ref, w_ref, acc_ref)
     packed_system(members, blocks, acc_ref, out_ref)
 
 
@@ -208,7 +207,6 @@
 def finish_kernel(members, owned, parts, system_ref, dev_ref, mean_ref, out_ref, wide_ref):
     half = members // 2
     rows_out = mean_ref.shape[0]
-    highest = lax.Precision.HIGHEST
     total = system_ref[0].astype(jnp.float32)
     for m in range(1, parts):
         total = total + system_ref[m].astype(jnp.float32)
@@ -217,8 +215,17 @@
     identity = jnp.where(rows == cols, 1.0, 0.0)
     lane = lax.broadcasted_iota(jnp.int32, (half, LANES), 1)
 
+    def split(value):
+        top = value.astype(jnp.bfloat16)
+        return top, (value - top.astype(jnp.float32)).astype(jnp.bfloat16)
+
     def dot(a, b):
-        return jnp.dot(a, b, precision=highest, preferred_element_type=jnp.float32)
+        (a_top, a_low), (b_top, b_low) = split(a), split(b)
+
+        def one(x, y):
+            return jnp.dot(x, y, preferred_element_type=jnp.float32)
+
+        return one(a_top, b_top) + (one(a_top, b_low) + one(a_low, b_top))
 
     y_iter, z_iter, bound, force = [], [], [], []
     for r in range(owned):
@@ -292,6 +299,9 @@
 
     extra = pieces * owned
 
+    def scalar(value):
+        return pltpu.with_memory_space_constraint(value, pltpu.SMEM)
+
     def far(value):
         return pltpu.with_memory_space_constraint(value, pltpu.HBM)
 
@@ -338,29 +348,33 @@
     rows = -(-(members + 2) // 16) * 16
     scalars = pl.BlockSpec(memory_space=pltpu.SMEM)
     system = pltpu.VMEM((blocks_dev * half, LANES), jnp.bfloat16)
-    d_all, to_low, to_high = pl.pallas_call(
-        functools.partial(neighbour_kernel, members, obs, blocks_dev),
-        out_shape=(pltpu.VMEM((obs + 1, rows, LANES), jnp.bfloat16), system, system),
+    d_all, to_low = pl.pallas_call(
+        functools.partial(low_kernel, members, obs, blocks_dev),
+        out_shape=(pltpu.VMEM((obs + 1, rows, LANES), jnp.bfloat16), system),
         in_specs=[scalars, vmem, vmem, vmem],
-        out_specs=(vmem, vmem, vmem),
+        out_specs=(vmem, vmem),
         scratch_shapes=[
             pltpu.VMEM((rows * obs, LANES), jnp.float32),
             pltpu.VMEM((blocks_dev * members, LANES), jnp.float32),
         ],
         compiler_params=pltpu.CompilerParams(vmem_limit_bytes=16 * 2**20),
-        name="neighbours",
-    )(pltpu.with_memory_space_constraint(lists, pltpu.SMEM), near(prior), near(aux), near(weights))
+        name="low",
+    )(scalar(lists), near(prior), near(aux), near(weights))
     from_high = shift(to_low, -1)
+
+    def later(first, dtype):
+        return pl.pallas_call(
+            functools.partial(next_kernel, members, obs, first, blocks_dev),
+            out_shape=pltpu.VMEM((blocks_dev * half, LANES), dtype),
+            in_specs=[scalars, vmem, vmem],
+            out_specs=vmem,
+            scratch_shapes=[pltpu.VMEM((blocks_dev * members, LANES), jnp.float32)],
+            compiler_params=pltpu.CompilerParams(vmem_limit_bytes=16 * 2**20),
+        )(scalar(lists), near(d_all), near(weights))
+
+    to_high = later(2 * blocks_dev, jnp.bfloat16)
     from_low = shift(to_high, 1)
-    own = pl.pallas_call(
-        functools.partial(own_kernel, members, obs, blocks_dev),
-        out_shape=pltpu.VMEM((blocks_dev * half, LANES), jnp.float32),
-        in_specs=[scalars, vmem, vmem],
-        out_specs=vmem,
-        scratch_shapes=[pltpu.VMEM((blocks_dev * members, LANES), jnp.float32)],
-        compiler_params=pltpu.CompilerParams(vmem_limit_bytes=16 * 2**20),
-        name="own",
-    )(pltpu.with_memory_space_constraint(lists, pltpu.SMEM), near(d_all), near(weights))
+    own = later(blocks_dev, jnp.float32)
     partial = pl.pallas_call(
         merge_kernel,
         out_shape=pltpu.VMEM((blocks_dev * half, LANES), jnp.bfloat16),
@@ -385,7 +399,7 @@
     )(near(prior))
     analysis = pl.pallas_call(
         functools.partial(finish_kernel, members, owned, mem_count),
-        out_shape=jax.ShapeDtypeStruct((members * extra, LANES), jnp.bfloat16),
+        out_shape=pltpu.VMEM((members * extra, LANES), jnp.bfloat16),
         in_specs=[vmem, vmem, vmem],
         out_specs=vmem,
         scratch_shapes=[pltpu.VMEM((members * extra, LANES), jnp.float32)],

time: 64.8 us -> 64.8 us (level)
    pallas_call x2 -> x3, Pallas kernels: 9.88 us -> 9.96 us  [the longest x2 6.13 us: later(): pl.pallas_call(functools.partial(next_kernel, members, obs, first, blocks...]
where the time goes in v8:
time: 64.8 us; the launch traced here: 64.5 us
  starting transfers between devices  22.8 us (35%)
  Pallas kernels  19.3 us (30%)
  waiting for transfers between devices  12.9 us (20%)
  blocking collectives  9.29 us (14%)
    ppermute x4, starting transfers between devices, shift(): return lax.ppermute(value, ('mem', 'grid'), pairs)  10.9 us
    all_to_all x1, blocking collectives, per_device(): lax.all_to_all(analysis, 'mem', split_axis=0, concat_axis=0, tiled=True)  9.29 us
    pallas_call x2, Pallas kernels, later(): pl.pallas_call(functools.partial(next_kernel, members, obs, first, blocks...  6.13 us
    all_to_all x1, starting transfers between devices, per_device(): lax.all_to_all(packed, 'mem', split_axis=0, concat_axis=0, tiled=True)  6.07 us
    all_to_all x1, waiting for transfers between devices, per_device(): lax.all_to_all(packed, 'mem', split_axis=0, concat_axis=0, tiled=True)  6 us
    all_to_all x1, starting transfers between devices, per_device(): lax.all_to_all(partial, 'mem', split_axis=0, concat_axis=0, tiled=True)  5.85 us
    all_to_all x1, waiting for transfers between devices, per_device(): lax.all_to_all(partial, 'mem', split_axis=0, concat_axis=0, tiled=True)  5.42 us
    pallas_call x1, Pallas kernels, per_device(): pl.pallas_call(functools.partial(low_kernel, members, obs, blocks_dev), o...  3.84 us
  transfers between devices with their start and end apart: 6, of which 4 were waited for; matrix products, arithmetic and copies ran while one was open for 0% of the time, Pallas kernels for 10%

profile of v8, /device:TPU:2, one launch (start us, length us, event | category | flops | bytes accessed | tf_op | source)
XLA Modules:
  0.0 64.5 jit_solution(17045477362441791861)
XLA Ops:
  0.0 2.6 %pack.1 = bf16[8,10,56,128]{3,2,1,0:T(8,128)(2,1)} custom-call(bf16[10,384,128]{2,1,0:T(8,128)(2,1)} %src_ref.1, bf16[10,16,512]{2,1,0:T(8,128)(2,1)} %state_all.1), custom_call_target="tpu_custom_call" | custom-call | tf_op jit(solution)/shard_map/pack/pallas_call | solution.py:308
  2.6 0.0 copy-start.3
  2.6 0.0 copy-start
  2.6 0.0 copy-start.1
  2.6 0.0 copy-start.2
  2.6 0.0 copy-start.4
  2.6 6.1 %all-to-all-start = ((bf16[8,10,56,128]{3,2,1,0:T(8,128)(2,1)}), bf16[8,10,56,128]{3,2,1,0:T(8,128)(2,1)S(1)}, u32[]{:S(2)}, u32[]{:S(2)}) async-start(bf16[8,10,56,128]{3,2,1,0:T(8,128)(2,1)} %pack.1), calls=%async_computation | async-start | bytes 2293760 | tf_op jit(solution)/shard_map/all_to_all | solution.py:323
  8.7 0.0 copy-done.3
  8.7 0.0 collective-permute-start
  8.7 5.3 %collective-permute-start.1 = (s32[16,256]{1,0:T(8,128)S(1)}, s32[16,256]{1,0:T(8,128)S(1)}, u32[]{:S(2)}, u32[]{:S(2)}) collective-permute-start(s32[16,256]{1,0:T(8,128)S(1)} %copy-done.3), channel_id=1, source_target_pairs={{0,63},{1,0},{2,33},{3,2},{4,35},{5,4},{6,37},{7,6},{8,39},{9,8},{... | collective-permute-start | bytes 49160 | tf_op jit(solution)/shard_map/ppermute | solution.py:29
  14.0 1.3 %collective-permute-done.low_ref = s32[16,256]{1,0:T(8,128)S(1)} collective-permute-done((s32[16,256]{1,0:T(8,128)S(1)}, s32[16,256]{1,0:T(8,128)S(1)}, u32[]{:S(2)}, u32[]{:S(2)}) %collective-permute-start) | collective-permute-done | bytes 16416 | tf_op jit(solution)/shard_map/ppermute | solution.py:29
  15.3 0.1 collective-permute-done.1.high_ref
  15.4 0.0 copy-done
  15.4 0.0 copy-done.1
  15.4 0.0 copy-done.2
  15.4 0.0 copy-done.4
  15.4 2.8 %weights.1 = (f32[2312,128]{1,0:T(8,128)S(1)}, f32[96,128]{1,0:T(8,128)S(1)}, s32[48,128]{1,0:T(8,128)S(4)}) custom-call(s32[384]{0:T(512)S(1)} %copy-done.4, s32[16,256]{1,0:T(8,128)S(1)} %collective-permute-done.low_ref, s32[16,256]{1,0:T(8,128)S(1)} %copy-done.3, s32[16,256]{1,0:T(8,128)S(1)} %collective-permute-done.1.high_ref, f32[384,128]{1,0:T(8,128)S(1)} %copy-done, ...), custom_call_target="tpu_custom_call" | custom-call | tf_op jit(solution)/shard_map/weights/pallas_call | solution.py:329
  18.3 6.0 %all-to-all-done = bf16[8,10,56,128]{3,2,1,0:T(8,128)(2,1)S(1)} async-done(((bf16[8,10,56,128]{3,2,1,0:T(8,128)(2,1)}), bf16[8,10,56,128]{3,2,1,0:T(8,128)(2,1)S(1)}, u32[]{:S(2)}, u32[]{:S(2)}) %all-to-all-start) | async-done | bytes 1146912 | tf_op jit(solution)/shard_map/all_to_all | solution.py:323
  24.3 3.8 %low.1 = (bf16[49,96,128]{2,1,0:T(8,128)(2,1)S(1)}, bf16[640,128]{1,0:T(8,128)(2,1)S(1)}) custom-call(s32[48,128]{1,0:T(8,128)S(4)} %get-tuple-element.12.list_ref, bf16[80,56,128]{2,1,0:T(8,128)(2,1)S(1)} %bitcast.3, f32[96,128]{1,0:T(8,128)S(1)} %get-tuple-element.13.aux_ref, f32[2312,128]{1,0:T(8,128)S(1)} %get-tuple-element.14.w_ref), custom_call_target="tpu_custom_call" | custom-call | tf_op jit(solution)/shard_map/low/pallas_call | solution.py:351
  28.1 2.7 %shard_map.74 = bf16[640,128]{1,0:T(8,128)(2,1)S(1)} custom-call(s32[48,128]{1,0:T(8,128)S(4)} %get-tuple-element.12.list_ref, bf16[49,96,128]{2,1,0:T(8,128)(2,1)S(1)} %get-tuple-element.15.d_ref, f32[2312,128]{1,0:T(8,128)S(1)} %get-tuple-element.14.w_ref), custom_call_target="tpu_custom_call" | custom-call | tf_op jit(solution)/shard_map/pallas_call | solution.py:366
  30.8 0.1 collective-permute-start.2
  30.9 5.5 %collective-permute-start.3 = (bf16[640,128]{1,0:T(8,128)(2,1)S(1)}, bf16[640,128]{1,0:T(8,128)(2,1)S(1)}, u32[]{:S(2)}, u32[]{:S(2)}) collective-permute-start(bf16[640,128]{1,0:T(8,128)(2,1)S(1)} %get-tuple-element.16), channel_id=1, source_target_pairs={{0,63},{1,0},{2,33},{3,2},{4,35},{5,4},{6,37},{7,6},{8,39},{9,8},{... | collective-permute-start | bytes 491528 | tf_op jit(solution)/shard_map/ppermute | solution.py:29
  36.5 3.4 %shard_map.73.own_ref = f32[640,128]{1,0:T(8,128)S(1)} custom-call(s32[48,128]{1,0:T(8,128)S(4)} %get-tuple-element.12.list_ref, bf16[49,96,128]{2,1,0:T(8,128)(2,1)S(1)} %get-tuple-element.15.d_ref, f32[2312,128]{1,0:T(8,128)S(1)} %get-tuple-element.14.w_ref), custom_call_target="tpu_custom_call" | custom-call | tf_op jit(solution)/shard_map/pallas_call | solution.py:366
  39.9 0.0 collective-permute-done.2.low_ref
  39.9 0.0 collective-permute-done.3.high_ref
  39.9 0.7 %merge.1 = bf16[640,128]{1,0:T(8,128)(2,1)} custom-call(f32[640,128]{1,0:T(8,128)S(1)} %shard_map.73.own_ref, bf16[640,128]{1,0:T(8,128)(2,1)S(1)} %collective-permute-done.2.low_ref, bf16[640,128]{1,0:T(8,128)(2,1)S(1)} %collective-permute-done.3.high_ref), custom_call_target="tpu_custom_call" | custom-call | tf_op jit(solution)/shard_map/merge/pallas_call | solution.py:378
  40.7 5.9 %all-to-all-start.1 = ((bf16[8,80,128]{2,1,0:T(8,128)(2,1)}), bf16[8,80,128]{2,1,0:T(8,128)(2,1)S(1)}, u32[]{:S(2)}, u32[]{:S(2)}) async-start(bf16[8,80,128]{2,1,0:T(8,128)(2,1)} %bitcast.1), calls=%async_computation.1 | async-start | bytes 327680 | tf_op jit(solution)/shard_map/all_to_all | solution.py:387
  46.5 0.2 state.1
  46.7 5.4 %all-to-all-done.1.system_ref = bf16[8,80,128]{2,1,0:T(8,128)(2,1)S(1)} async-done(((bf16[8,80,128]{2,1,0:T(8,128)(2,1)}), bf16[8,80,128]{2,1,0:T(8,128)(2,1)S(1)}, u32[]{:S(2)}, u32[]{:S(2)}) %all-to-all-start.1) | async-done | bytes 163872 | tf_op jit(solution)/shard_map/all_to_all | solution.py:387
  52.1 2.3 %finish.1 = bf16[640,128]{1,0:T(8,128)(2,1)S(1)} custom-call(bf16[8,80,128]{2,1,0:T(8,128)(2,1)S(1)} %all-to-all-done.1.system_ref, bf16[80,1024]{1,0:T(8,128)(2,1)S(1)} %get-tuple-element.17.dev_ref, f32[8,128]{1,0:T(8,128)S(1)} %get-tuple-element.18.mean_ref), custom_call_target="tpu_custom_call" | custom-call | tf_op jit(solution)/shard_map/finish/pallas_call | solution.py:400
  54.4 9.3 %all_to_all.15.part_ref = bf16[8,10,8,128]{3,2,1,0:T(8,128)(2,1)S(1)} all-to-all(bf16[8,10,8,128]{3,2,1,0:T(8,128)(2,1)S(1)} %bitcast.5), channel_id=1, replica_groups=mesh['mem'=8,'grid'=32] {'mem'}, dimensions={0} | all-to-all | bytes 327680 | tf_op jit(solution)/shard_map/all_to_all | solution.py:410
  63.7 0.8 %unpack.1 = bf16[10,16,512]{2,1,0:T(8,128)(2,1)} custom-call(bf16[8,10,8,128]{3,2,1,0:T(8,128)(2,1)S(1)} %all_to_all.15.part_ref), custom_call_target="tpu_custom_call" | custom-call | tf_op jit(solution)/shard_map/unpack/pallas_call | solution.py:411
Async XLA Ops:
  2.6 6.1 %copy-start.3 = (s32[16,256]{1,0:T(8,128)S(1)}, s32[16,256]{1,0:T(8,128)}, u32[]{:S(2)}) copy-start(s32[16,256]{1,0:T(8,128)} %mid_ref.1) | copy-start | bytes 49156
  2.6 12.9 %copy-start = (f32[384,128]{1,0:T(8,128)S(1)}, f32[384,128]{1,0:T(8,128)}, u32[]{:S(2)}) copy-start(f32[384,128]{1,0:T(8,128)} %prec_all.1) | copy-start | bytes 589828
  2.6 12.8 %copy-start.1 = (f32[384,128]{1,0:T(8,128)S(1)}, f32[384,128]{1,0:T(8,128)}, u32[]{:S(2)}) copy-start(f32[384,128]{1,0:T(8,128)} %pos_all.1) | copy-start | bytes 589828
  2.6 12.8 %copy-start.2 = (f32[384,128]{1,0:T(8,128)S(1)}, f32[384,128]{1,0:T(8,128)}, u32[]{:S(2)}) copy-start(f32[384,128]{1,0:T(8,128)} %value_all.1) | copy-start | bytes 589828
  2.6 12.8 %copy-start.4 = (s32[384]{0:T(512)S(1)}, s32[384]{0:T(512)}, u32[]{:S(2)}) copy-start(s32[384]{0:T(512)} %len_ref.1) | copy-start | bytes 4612
  2.6 21.7 %all-to-all-start = ((bf16[8,10,56,128]{3,2,1,0:T(8,128)(2,1)}), bf16[8,10,56,128]{3,2,1,0:T(8,128)(2,1)S(1)}, u32[]{:S(2)}, u32[]{:S(2)}) async-start(bf16[8,10,56,128]{3,2,1,0:T(8,128)(2,1)} %pack.1), calls=%async_computation | async-start | bytes 2293760 | tf_op jit(solution)/shard_map/all_to_all | solution.py:323
  8.7 6.6 %collective-permute-start = (s32[16,256]{1,0:T(8,128)S(1)}, s32[16,256]{1,0:T(8,128)S(1)}, u32[]{:S(2)}, u32[]{:S(2)}) collective-permute-start(s32[16,256]{1,0:T(8,128)S(1)} %copy-done.3), channel_id=1, source_target_pairs={{0,1},{1,34},{2,3},{3,36},{4,5},{5,38},{6,7},{7,40},{8,9},{9,42},{... | collective-permute-start | bytes 49160 | tf_op jit(solution)/shard_map/ppermute | solution.py:29
  8.7 6.7 %collective-permute-start.1 = (s32[16,256]{1,0:T(8,128)S(1)}, s32[16,256]{1,0:T(8,128)S(1)}, u32[]{:S(2)}, u32[]{:S(2)}) collective-permute-start(s32[16,256]{1,0:T(8,128)S(1)} %copy-done.3), channel_id=1, source_target_pairs={{0,63},{1,0},{2,33},{3,2},{4,35},{5,4},{6,37},{7,6},{8,39},{9,8},{... | collective-permute-start | bytes 49160 | tf_op jit(solution)/shard_map/ppermute | solution.py:29
  30.8 9.1 %collective-permute-start.2 = (bf16[640,128]{1,0:T(8,128)(2,1)S(1)}, bf16[640,128]{1,0:T(8,128)(2,1)S(1)}, u32[]{:S(2)}, u32[]{:S(2)}) collective-permute-start(bf16[640,128]{1,0:T(8,128)(2,1)S(1)} %shard_map.74), channel_id=1, source_target_pairs={{0,1},{1,34},{2,3},{3,36},{4,5},{5,38},{6,7},{7,40},{8,9},{9,42},{... | collective-permute-start | bytes 491528 | tf_op jit(solution)/shard_map/ppermute | solution.py:29
  30.9 9.0 %collective-permute-start.3 = (bf16[640,128]{1,0:T(8,128)(2,1)S(1)}, bf16[640,128]{1,0:T(8,128)(2,1)S(1)}, u32[]{:S(2)}, u32[]{:S(2)}) collective-permute-start(bf16[640,128]{1,0:T(8,128)(2,1)S(1)} %get-tuple-element.16), channel_id=1, source_target_pairs={{0,63},{1,0},{2,33},{3,2},{4,35},{5,4},{6,37},{7,6},{8,39},{9,8},{... | collective-permute-start | bytes 491528 | tf_op jit(solution)/shard_map/ppermute | solution.py:29
  40.7 11.4 %all-to-all-start.1 = ((bf16[8,80,128]{2,1,0:T(8,128)(2,1)}), bf16[8,80,128]{2,1,0:T(8,128)(2,1)S(1)}, u32[]{:S(2)}, u32[]{:S(2)}) async-start(bf16[8,80,128]{2,1,0:T(8,128)(2,1)} %bitcast.1), calls=%async_computation.1 | async-start | bytes 327680 | tf_op jit(solution)/shard_map/all_to_all | solution.py:387

commit v9 on v8

--- a/solution.py
+++ b/solution.py
@@ -13,6 +13,9 @@
 LANES = 128
 COUNT = 127
 UNIT = 4
+TURN = 18
+ROOM = 256
+SPAN = 16
 
 inflation = 1.1
 
@@ -63,7 +66,7 @@
     state_out.wait()
 
 
-def weight_kernel(nb_total, obs, len_ref, low_ref, mid_ref, high_ref, prec_all, pos_all, value_all, out_ref, aux_ref, list_ref, prec_ref, pos_ref, table_ref, sems):
+def weight_kernel(nb_total, obs, len_ref, low_ref, mid_ref, high_ref, prec_all, pos_all, value_all, out_ref, aux_ref, list_ref, item_ref, prec_ref, pos_ref, table_ref, sems):
     place = lax.axis_index("mem")
     grid_pos = lax.axis_index("grid")
     grid_count = lax.axis_size("grid")
@@ -109,31 +112,43 @@
         relative = distance * (1.0 / LOCR)
         weight = prec_ref[o : o + 1, :] * jnp.exp(-0.5 * relative * relative)
         out_ref[pl.ds(o, blocks, stride=obs), :] = weight
-    out_ref[blocks * obs :, :] = jnp.zeros((8, LANES), jnp.float32)
-    table_ref[...] = jnp.where(slot == COUNT, found, chosen)
+    out_ref[blocks * obs :, :] = jnp.zeros((out_ref.shape[0] - blocks * obs, LANES), jnp.float32)
+    table_ref[0:blocks] = jnp.where(slot == COUNT, found, chosen)
+    table_ref[blocks:] = jnp.full((table_ref.shape[0] - blocks, LANES), obs, jnp.int32)
     copy = pltpu.make_async_copy(table_ref, list_ref, sems.at[3])
     copy.start()
     copy.wait()
-
-
-def accumulate(members, obs, first, blocks, list_ref, d_ref, w_ref, acc_ref):
+    most = -(-obs // UNIT)
+    for group in range(3):
+        at = 0
+        for b in range(group * blocks_dev, (group + 1) * blocks_dev):
+            for k in range(most):
+                item_ref[group, at + k] = b * SPAN + k
+            at = at + lax.shift_right_logical(list_ref[b, COUNT] + UNIT - 1, 2)
+        for k in range(TURN):
+            item_ref[group, at + k] = (group + 1) * blocks_dev * SPAN + most
+        item_ref[group, ROOM - 1] = at
+
+
+def accumulate(members, obs, group, blocks, list_ref, item_ref, d_ref, w_ref, acc_ref):
     rows = d_ref.shape[1]
     acc_ref[...] = jnp.zeros(acc_ref.shape, jnp.float32)
-    longest = list_ref[first, COUNT]
-    for b in range(1, blocks):
-        longest = jnp.maximum(longest, list_ref[first + b, COUNT])
 
     def step(turn, carry):
-        for b in range(blocks):
+        for u in range(TURN):
+            item = item_ref[group, turn * TURN + u]
+            b = lax.shift_right_logical(item, 4)
+            first = lax.bitwise_and(item, SPAN - 1) * UNIT
             full, scaled = [], []
             for k in range(UNIT):
-                o = list_ref[first + b, turn * UNIT + k]
+                o = list_ref[b, first + k]
                 d = d_ref[o]
-                row = w_ref[pl.ds((first + b) * obs + o, 1), :]
+                row = w_ref[pl.ds(b * obs + o, 1), :]
                 w = jnp.broadcast_to(row, (16, LANES)).astype(jnp.bfloat16)
                 full.append(d)
                 scaled.append((d[:members].reshape(members // 16, 16, LANES) * w[None]).reshape(members, LANES))
-            acc_ref[b * members : (b + 1) * members, 0:rows] += lax.dot_general(
+            at = pl.multiple_of((b - group * blocks) * members, 16)
+            acc_ref[pl.ds(at, members), 0:rows] += lax.dot_general(
                 jnp.concatenate(scaled, axis=1),
                 jnp.concatenate(full, axis=1),
                 (((1,), (1,)), ((), ())),
@@ -141,7 +156,7 @@
             )
         return carry
 
-    lax.fori_loop(0, (longest + UNIT - 1) // UNIT, step, 0)
+    lax.fori_loop(0, (item_ref[group, ROOM - 1] + TURN - 1) // TURN, step, 0)
 
 
 def packed_system(members, blocks, acc_ref, out_ref):
@@ -157,7 +172,7 @@
         out_ref[b * half : (b + 1) * half, :] = value.astype(out_ref.dtype)
 
 
-def low_kernel(members, obs, blocks, list_ref, prior_ref, aux_ref, w_ref, d_ref, low_ref, dev_ref, acc_ref):
+def low_kernel(members, obs, blocks, list_ref, item_ref, prior_ref, aux_ref, w_ref, d_ref, low_ref, dev_ref, acc_ref):
     rows = d_ref.shape[1]
     total = prior_ref[0, 0:obs].astype(jnp.float32)
     for i in range(1, members):
@@ -176,12 +191,12 @@
     for o in range(obs):
         d_ref[o] = dev_ref[pl.ds(o, rows, stride=obs), :].astype(jnp.bfloat16)
     d_ref[obs] = jnp.zeros((rows, LANES), jnp.bfloat16)
-    accumulate(members, obs, 0, blocks, list_ref, d_ref, w_ref, acc_ref)
+    accumulate(members, obs, 0, blocks, list_ref, item_ref, d_ref, w_ref, acc_ref)
     packed_system(members, blocks, acc_ref, low_ref)
 
 
-def next_kernel(members, obs, first, blocks, list_ref, d_ref, w_ref, out_ref, acc_ref):
-    accumulate(members, obs, first, blocks, list_ref, d_ref, w_ref, acc_ref)
+def next_kernel(members, obs, group, blocks, list_ref, item_ref, d_ref, w_ref, out_ref, acc_ref):
+    accumulate(members, obs, group, blocks, list_ref, item_ref, d_ref, w_ref, acc_ref)
     packed_system(members, blocks, acc_ref, out_ref)
 
 
@@ -291,6 +306,7 @@
     nb_total = blocks_dev * grid_count
     vmem = pl.BlockSpec(memory_space=pltpu.VMEM)
     anywhere = pl.BlockSpec(memory_space=pl.ANY)
+    scalars = pl.BlockSpec(memory_space=pltpu.SMEM)
 
     pieces = ens_state.shape[2] // LANES
 
@@ -326,19 +342,20 @@
     from_high = shift(pair_block, -1)
 
     blocks = 3 * blocks_dev
-    weights, aux, lists = pl.pallas_call(
+    weights, aux, lists, items = pl.pallas_call(
         functools.partial(weight_kernel, float(nb_total), obs),
         out_shape=(
-            pltpu.VMEM((blocks * obs + 8, LANES), jnp.float32),
+            pltpu.VMEM(((blocks + 1) * obs + 8, LANES), jnp.float32),
             pltpu.VMEM((2 * obs, LANES), jnp.float32),
-            pltpu.SMEM((blocks, LANES), jnp.int32),
+            pltpu.SMEM((blocks + 8, LANES), jnp.int32),
+            pltpu.SMEM((3, ROOM), jnp.int32),
         ),
         in_specs=[pl.BlockSpec(memory_space=pltpu.SMEM), vmem, vmem, vmem, anywhere, anywhere, anywhere],
-        out_specs=(vmem, vmem, pl.BlockSpec(memory_space=pltpu.SMEM)),
+        out_specs=(vmem, vmem, scalars, scalars),
         scratch_shapes=[
             pltpu.VMEM((obs, LANES), jnp.float32),
             pltpu.VMEM((obs, LANES), jnp.float32),
-            pltpu.VMEM((blocks, LANES), jnp.int32),
+            pltpu.VMEM((blocks + 8, LANES), jnp.int32),
             pltpu.SemaphoreType.DMA((4,)),
         ],
         compiler_params=pltpu.CompilerParams(vmem_limit_bytes=16 * 2**20),
@@ -346,35 +363,34 @@
     )(obs_len, near(from_low), pair_block, near(from_high), obs_prec, obs_pos, obs_value)
 
     rows = -(-(members + 2) // 16) * 16
-    scalars = pl.BlockSpec(memory_space=pltpu.SMEM)
     system = pltpu.VMEM((blocks_dev * half, LANES), jnp.bfloat16)
     d_all, to_low = pl.pallas_call(
         functools.partial(low_kernel, members, obs, blocks_dev),
         out_shape=(pltpu.VMEM((obs + 1, rows, LANES), jnp.bfloat16), system),
-        in_specs=[scalars, vmem, vmem, vmem],
+        in_specs=[scalars, scalars, vmem, vmem, vmem],
         out_specs=(vmem, vmem),
         scratch_shapes=[
             pltpu.VMEM((rows * obs, LANES), jnp.float32),
-            pltpu.VMEM((blocks_dev * members, LANES), jnp.float32),
+            pltpu.VMEM(((blocks_dev + 1) * members, LANES), jnp.float32),
         ],
         compiler_params=pltpu.CompilerParams(vmem_limit_bytes=16 * 2**20),
         name="low",
-    )(scalar(lists), near(prior), near(aux), near(weights))
+    )(scalar(lists), scalar(items), near(prior), near(aux), near(weights))
     from_high = shift(to_low, -1)
 
-    def later(first, dtype):
+    def later(group, dtype):
         return pl.pallas_call(
-            functools.partial(next_kernel, members, obs, first, blocks_dev),
+            functools.partial(next_kernel, members, obs, group, blocks_dev),
             out_shape=pltpu.VMEM((blocks_dev * half, LANES), dtype),
-            in_specs=[scalars, vmem, vmem],
+            in_specs=[scalars, scalars, vmem, vmem],
             out_specs=vmem,
-            scratch_shapes=[pltpu.VMEM((blocks_dev * members, LANES), jnp.float32)],
+            scratch_shapes=[pltpu.VMEM(((blocks_dev + 1) * members, LANES), jnp.float32)],
             compiler_params=pltpu.CompilerParams(vmem_limit_bytes=16 * 2**20),
-        )(scalar(lists), near(d_all), near(weights))
-
-    to_high = later(2 * blocks_dev, jnp.bfloat16)
+        )(scalar(lists), scalar(items), near(d_all), near(weights))
+
+    to_high = later(2, jnp.bfloat16)
     from_low = shift(to_high, 1)
-    own = later(blocks_dev, jnp.float32)
+    own = later(1, jnp.float32)
     partial = pl.pallas_call(
         merge_kernel,
         out_shape=pltpu.VMEM((blocks_dev * half, LANES), jnp.bfloat16),

time: 64.8 us -> 63.5 us (0.980)
  the two profiles are of different devices: /device:TPU:2 before, /device:TPU:1 now
where the time goes in v9:
time: 63.5 us; the launch traced here: 63.2 us
  waiting for transfers between devices  19.1 us (30%)
  Pallas kernels  18.8 us (30%)
  starting transfers between devices  16.9 us (27%)
  blocking collectives  8.18 us (13%)
    ppermute x4, waiting for transfers between devices, shift(): return lax.ppermute(value, ('mem', 'grid'), pairs)  10 us
    all_to_all x1, blocking collectives, per_device(): lax.all_to_all(analysis, 'mem', split_axis=0, concat_axis=0, tiled=True)  8.18 us
    ppermute x4, starting transfers between devices, shift(): return lax.ppermute(value, ('mem', 'grid'), pairs)  7.45 us
    all_to_all x1, waiting for transfers between devices, per_device(): lax.all_to_all(partial, 'mem', split_axis=0, concat_axis=0, tiled=True)  6.21 us
    all_to_all x1, starting transfers between devices, per_device(): lax.all_to_all(packed, 'mem', split_axis=0, concat_axis=0, tiled=True)  6.08 us
    pallas_call x2, Pallas kernels, later(): pl.pallas_call(functools.partial(next_kernel, members, obs, group, blocks...  4.62 us
    pallas_call x1, Pallas kernels, per_device(): pl.pallas_call(functools.partial(weight_kernel, float(nb_total), obs), ou...  4.46 us
    all_to_all x1, starting transfers between devices, per_device(): lax.all_to_all(partial, 'mem', split_axis=0, concat_axis=0, tiled=True)  3.38 us
  transfers between devices with their start and end apart: 6, of which 5 were waited for; matrix products, arithmetic and copies ran while one was open for 0% of the time, Pallas kernels for 11%

profile of v9, /device:TPU:1, one launch (start us, length us, event | category | flops | bytes accessed | tf_op | source)
XLA Modules:
  0.0 63.2 jit_solution(13982352249967579178)
XLA Ops:
  0.0 2.6 %pack.1 = bf16[8,10,56,128]{3,2,1,0:T(8,128)(2,1)} custom-call(bf16[10,384,128]{2,1,0:T(8,128)(2,1)} %src_ref.1, bf16[10,16,512]{2,1,0:T(8,128)(2,1)} %state_all.1), custom_call_target="tpu_custom_call" | custom-call | tf_op jit(solution)/shard_map/pack/pallas_call | solution.py:324
  2.6 0.0 copy-start.3
  2.6 0.0 copy-start
  2.6 0.0 copy-start.1
  2.6 0.0 copy-start.2
  2.6 0.0 copy-start.4
  2.6 6.1 %all-to-all-start = ((bf16[8,10,56,128]{3,2,1,0:T(8,128)(2,1)}), bf16[8,10,56,128]{3,2,1,0:T(8,128)(2,1)S(1)}, u32[]{:S(2)}, u32[]{:S(2)}) async-start(bf16[8,10,56,128]{3,2,1,0:T(8,128)(2,1)} %pack.1), calls=%async_computation | async-start | bytes 2293760 | tf_op jit(solution)/shard_map/all_to_all | solution.py:339
  8.7 0.0 copy-done.3
  8.7 3.8 %collective-permute-start = (s32[16,256]{1,0:T(8,128)S(1)}, s32[16,256]{1,0:T(8,128)S(1)}, u32[]{:S(2)}, u32[]{:S(2)}) collective-permute-start(s32[16,256]{1,0:T(8,128)S(1)} %copy-done.3), channel_id=1, source_target_pairs={{0,1},{1,34},{2,3},{3,36},{4,5},{5,38},{6,7},{7,40},{8,9},{9,42},{... | collective-permute-start | bytes 49160 | tf_op jit(solution)/shard_map/ppermute | solution.py:32
  12.6 0.0 collective-permute-start.1
  12.6 0.9 %collective-permute-done.low_ref = s32[16,256]{1,0:T(8,128)S(1)} collective-permute-done((s32[16,256]{1,0:T(8,128)S(1)}, s32[16,256]{1,0:T(8,128)S(1)}, u32[]{:S(2)}, u32[]{:S(2)}) %collective-permute-start) | collective-permute-done | bytes 16416 | tf_op jit(solution)/shard_map/ppermute | solution.py:32
  13.4 3.8 %collective-permute-done.1.high_ref = s32[16,256]{1,0:T(8,128)S(1)} collective-permute-done((s32[16,256]{1,0:T(8,128)S(1)}, s32[16,256]{1,0:T(8,128)S(1)}, u32[]{:S(2)}, u32[]{:S(2)}) %collective-permute-start.1) | collective-permute-done | bytes 16416 | tf_op jit(solution)/shard_map/ppermute | solution.py:32
  17.2 0.0 copy-done
  17.2 0.0 copy-done.1
  17.2 0.0 copy-done.2
  17.2 0.0 copy-done.4
  17.2 4.5 %weights.1 = (f32[2360,128]{1,0:T(8,128)S(1)}, f32[96,128]{1,0:T(8,128)S(1)}, s32[56,128]{1,0:T(8,128)S(4)}, s32[3,256]{1,0:T(4,128)S(4)}) custom-call(s32[384]{0:T(512)S(1)} %copy-done.4, s32[16,256]{1,0:T(8,128)S(1)} %collective-permute-done.low_ref, s32[16,256]{1,0:T(8,128)S(1)} %copy-done.3, s32[16,256]{1,0:T(8,128)S(1)} %collective-permute-done.1.high_ref, ...), custom_call_target="tpu_custom_call" | custom-call | tf_op jit(solution)/shard_map/weights/pallas_call | solution.py:345
  21.7 2.9 %all-to-all-done = bf16[8,10,56,128]{3,2,1,0:T(8,128)(2,1)S(1)} async-done(((bf16[8,10,56,128]{3,2,1,0:T(8,128)(2,1)}), bf16[8,10,56,128]{3,2,1,0:T(8,128)(2,1)S(1)}, u32[]{:S(2)}, u32[]{:S(2)}) %all-to-all-start) | async-done | bytes 1146912 | tf_op jit(solution)/shard_map/all_to_all | solution.py:339
  24.6 3.2 %low.1 = (bf16[49,96,128]{2,1,0:T(8,128)(2,1)S(1)}, bf16[640,128]{1,0:T(8,128)(2,1)S(1)}) custom-call(s32[56,128]{1,0:T(8,128)S(4)} %get-tuple-element.13.list_ref, s32[3,256]{1,0:T(4,128)S(4)} %get-tuple-element.14.item_ref, bf16[80,56,128]{2,1,0:T(8,128)(2,1)S(1)} %bitcast.3, f32[96,128]{1,0:T(8,128)S(1)} %get-tuple-element.15.aux_ref, ...), custom_call_target="tpu_custom_call" | custom-call | tf_op jit(solution)/shard_map/low/pallas_call | solution.py:367
  27.9 2.3 %shard_map.74 = bf16[640,128]{1,0:T(8,128)(2,1)S(1)} custom-call(s32[56,128]{1,0:T(8,128)S(4)} %get-tuple-element.13.list_ref, s32[3,256]{1,0:T(4,128)S(4)} %get-tuple-element.14.item_ref, bf16[49,96,128]{2,1,0:T(8,128)(2,1)S(1)} %get-tuple-element.17.d_ref, f32[2360,128]{1,0:T(8,128)S(1)} %get-tuple-element.16.w_ref), custom_call_target="tpu_custom_call" | custom-call | tf_op jit(solution)/shard_map/pallas_call | solution.py:382
  30.1 3.6 %collective-permute-start.2 = (bf16[640,128]{1,0:T(8,128)(2,1)S(1)}, bf16[640,128]{1,0:T(8,128)(2,1)S(1)}, u32[]{:S(2)}, u32[]{:S(2)}) collective-permute-start(bf16[640,128]{1,0:T(8,128)(2,1)S(1)} %shard_map.74), channel_id=1, source_target_pairs={{0,1},{1,34},{2,3},{3,36},{4,5},{5,38},{6,7},{7,40},{8,9},{9,42},{... | collective-permute-start | bytes 491528 | tf_op jit(solution)/shard_map/ppermute | solution.py:32
  33.7 0.0 collective-permute-start.3
  33.7 2.4 %shard_map.73.own_ref = f32[640,128]{1,0:T(8,128)S(1)} custom-call(s32[56,128]{1,0:T(8,128)S(4)} %get-tuple-element.13.list_ref, s32[3,256]{1,0:T(4,128)S(4)} %get-tuple-element.14.item_ref, bf16[49,96,128]{2,1,0:T(8,128)(2,1)S(1)} %get-tuple-element.17.d_ref, f32[2360,128]{1,0:T(8,128)S(1)} %get-tuple-element.16.w_ref), custom_call_target="tpu_custom_call" | custom-call | tf_op jit(solution)/shard_map/pallas_call | solution.py:382
  36.1 0.0 collective-permute-done.2.low_ref
  36.1 5.3 %collective-permute-done.3.high_ref = bf16[640,128]{1,0:T(8,128)(2,1)S(1)} collective-permute-done((bf16[640,128]{1,0:T(8,128)(2,1)S(1)}, bf16[640,128]{1,0:T(8,128)(2,1)S(1)}, u32[]{:S(2)}, u32[]{:S(2)}) %collective-permute-start.3) | collective-permute-done | bytes 163872 | tf_op jit(solution)/shard_map/ppermute | solution.py:32
  41.5 0.7 %merge.1 = bf16[640,128]{1,0:T(8,128)(2,1)} custom-call(f32[640,128]{1,0:T(8,128)S(1)} %shard_map.73.own_ref, bf16[640,128]{1,0:T(8,128)(2,1)S(1)} %collective-permute-done.2.low_ref, bf16[640,128]{1,0:T(8,128)(2,1)S(1)} %collective-permute-done.3.high_ref), custom_call_target="tpu_custom_call" | custom-call | tf_op jit(solution)/shard_map/merge/pallas_call | solution.py:394
  42.2 3.4 %all-to-all-start.1 = ((bf16[8,80,128]{2,1,0:T(8,128)(2,1)}), bf16[8,80,128]{2,1,0:T(8,128)(2,1)S(1)}, u32[]{:S(2)}, u32[]{:S(2)}) async-start(bf16[8,80,128]{2,1,0:T(8,128)(2,1)} %bitcast.1), calls=%async_computation.1 | async-start | bytes 327680 | tf_op jit(solution)/shard_map/all_to_all | solution.py:403
  45.6 0.2 state.1
  45.7 6.2 %all-to-all-done.1.system_ref = bf16[8,80,128]{2,1,0:T(8,128)(2,1)S(1)} async-done(((bf16[8,80,128]{2,1,0:T(8,128)(2,1)}), bf16[8,80,128]{2,1,0:T(8,128)(2,1)S(1)}, u32[]{:S(2)}, u32[]{:S(2)}) %all-to-all-start.1) | async-done | bytes 163872 | tf_op jit(solution)/shard_map/all_to_all | solution.py:403
  51.9 2.3 %finish.1 = bf16[640,128]{1,0:T(8,128)(2,1)S(1)} custom-call(bf16[8,80,128]{2,1,0:T(8,128)(2,1)S(1)} %all-to-all-done.1.system_ref, bf16[80,1024]{1,0:T(8,128)(2,1)S(1)} %get-tuple-element.19.dev_ref, f32[8,128]{1,0:T(8,128)S(1)} %get-tuple-element.20.mean_ref), custom_call_target="tpu_custom_call" | custom-call | tf_op jit(solution)/shard_map/finish/pallas_call | solution.py:416
  54.3 8.2 %all_to_all.15.part_ref = bf16[8,10,8,128]{3,2,1,0:T(8,128)(2,1)S(1)} all-to-all(bf16[8,10,8,128]{3,2,1,0:T(8,128)(2,1)S(1)} %bitcast.5), channel_id=1, replica_groups=mesh['mem'=8,'grid'=32] {'mem'}, dimensions={0} | all-to-all | bytes 327680 | tf_op jit(solution)/shard_map/all_to_all | solution.py:426
  62.5 0.8 %unpack.1 = bf16[10,16,512]{2,1,0:T(8,128)(2,1)} custom-call(bf16[8,10,8,128]{3,2,1,0:T(8,128)(2,1)S(1)} %all_to_all.15.part_ref), custom_call_target="tpu_custom_call" | custom-call | tf_op jit(solution)/shard_map/unpack/pallas_call | solution.py:427
Async XLA Ops:
  2.6 6.1 %copy-start.3 = (s32[16,256]{1,0:T(8,128)S(1)}, s32[16,256]{1,0:T(8,128)}, u32[]{:S(2)}) copy-start(s32[16,256]{1,0:T(8,128)} %mid_ref.1) | copy-start | bytes 49156
  2.6 14.7 %copy-start = (f32[384,128]{1,0:T(8,128)S(1)}, f32[384,128]{1,0:T(8,128)}, u32[]{:S(2)}) copy-start(f32[384,128]{1,0:T(8,128)} %prec_all.1) | copy-start | bytes 589828
  2.6 14.6 %copy-start.1 = (f32[384,128]{1,0:T(8,128)S(1)}, f32[384,128]{1,0:T(8,128)}, u32[]{:S(2)}) copy-start(f32[384,128]{1,0:T(8,128)} %pos_all.1) | copy-start | bytes 589828
  2.6 14.6 %copy-start.2 = (f32[384,128]{1,0:T(8,128)S(1)}, f32[384,128]{1,0:T(8,128)}, u32[]{:S(2)}) copy-start(f32[384,128]{1,0:T(8,128)} %value_all.1) | copy-start | bytes 589828
  2.6 14.6 %copy-start.4 = (s32[384]{0:T(512)S(1)}, s32[384]{0:T(512)}, u32[]{:S(2)}) copy-start(s32[384]{0:T(512)} %len_ref.1) | copy-start | bytes 4612
  2.6 22.0 %all-to-all-start = ((bf16[8,10,56,128]{3,2,1,0:T(8,128)(2,1)}), bf16[8,10,56,128]{3,2,1,0:T(8,128)(2,1)S(1)}, u32[]{:S(2)}, u32[]{:S(2)}) async-start(bf16[8,10,56,128]{3,2,1,0:T(8,128)(2,1)} %pack.1), calls=%async_computation | async-start | bytes 2293760 | tf_op jit(solution)/shard_map/all_to_all | solution.py:339
  8.7 4.7 %collective-permute-start = (s32[16,256]{1,0:T(8,128)S(1)}, s32[16,256]{1,0:T(8,128)S(1)}, u32[]{:S(2)}, u32[]{:S(2)}) collective-permute-start(s32[16,256]{1,0:T(8,128)S(1)} %copy-done.3), channel_id=1, source_target_pairs={{0,1},{1,34},{2,3},{3,36},{4,5},{5,38},{6,7},{7,40},{8,9},{9,42},{... | collective-permute-start | bytes 49160 | tf_op jit(solution)/shard_map/ppermute | solution.py:32
  12.6 4.7 %collective-permute-start.1 = (s32[16,256]{1,0:T(8,128)S(1)}, s32[16,256]{1,0:T(8,128)S(1)}, u32[]{:S(2)}, u32[]{:S(2)}) collective-permute-start(s32[16,256]{1,0:T(8,128)S(1)} %copy-done.3), channel_id=1, source_target_pairs={{0,63},{1,0},{2,33},{3,2},{4,35},{5,4},{6,37},{7,6},{8,39},{9,8},{... | collective-permute-start | bytes 49160 | tf_op jit(solution)/shard_map/ppermute | solution.py:32
  30.1 6.0 %collective-permute-start.2 = (bf16[640,128]{1,0:T(8,128)(2,1)S(1)}, bf16[640,128]{1,0:T(8,128)(2,1)S(1)}, u32[]{:S(2)}, u32[]{:S(2)}) collective-permute-start(bf16[640,128]{1,0:T(8,128)(2,1)S(1)} %shard_map.74), channel_id=1, source_target_pairs={{0,1},{1,34},{2,3},{3,36},{4,5},{5,38},{6,7},{7,40},{8,9},{9,42},{... | collective-permute-start | bytes 491528 | tf_op jit(solution)/shard_map/ppermute | solution.py:32
  33.7 7.7 %collective-permute-start.3 = (bf16[640,128]{1,0:T(8,128)(2,1)S(1)}, bf16[640,128]{1,0:T(8,128)(2,1)S(1)}, u32[]{:S(2)}, u32[]{:S(2)}) collective-permute-start(bf16[640,128]{1,0:T(8,128)(2,1)S(1)} %get-tuple-element.18), channel_id=1, source_target_pairs={{0,63},{1,0},{2,33},{3,2},{4,35},{5,4},{6,37},{7,6},{8,39},{9,8},{... | collective-permute-start | bytes 491528 | tf_op jit(solution)/shard_map/ppermute | solution.py:32
  42.2 9.8 %all-to-all-start.1 = ((bf16[8,80,128]{2,1,0:T(8,128)(2,1)}), bf16[8,80,128]{2,1,0:T(8,128)(2,1)S(1)}, u32[]{:S(2)}, u32[]{:S(2)}) async-start(bf16[8,80,128]{2,1,0:T(8,128)(2,1)} %bitcast.1), calls=%async_computation.1 | async-start | bytes 327680 | tf_op jit(solution)/shard_map/all_to_all | solution.py:403

commit v10 on v9

--- a/solution.py
+++ b/solution.py
@@ -20,15 +20,17 @@
 inflation = 1.1
 
 
-def shift(value, step):
+def swap(value, crossing):
     mem_count = lax.axis_size("mem")
     grid_count = lax.axis_size("grid")
     pairs = []
     for m in range(mem_count):
         for g in range(grid_count):
-            crossing = g % 2 == (1 if step > 0 else 0)
-            other = m ^ 1 if crossing and mem_count % 2 == 0 else m
-            pairs.append((m * grid_count + g, other * grid_count + (g + step) % grid_count))
+            if crossing:
+                other = m ^ 1, (g + 1 if g % 2 else g - 1) % grid_count
+            else:
+                other = m, g ^ 1
+            pairs.append((m * grid_count + g, other[0] * grid_count + other[1]))
     return lax.ppermute(value, ("mem", "grid"), pairs)
 
 
@@ -66,7 +68,7 @@
     state_out.wait()
 
 
-def weight_kernel(nb_total, obs, len_ref, low_ref, mid_ref, high_ref, prec_all, pos_all, value_all, out_ref, aux_ref, list_ref, item_ref, prec_ref, pos_ref, table_ref, sems):
+def weight_kernel(nb_total, obs, len_ref, cross_ref, mid_ref, chip_ref, prec_all, pos_all, value_all, out_ref, aux_ref, list_ref, item_ref, prec_ref, pos_ref, table_ref, sems):
     place = lax.axis_index("mem")
     grid_pos = lax.axis_index("grid")
     grid_count = lax.axis_size("grid")
@@ -87,7 +89,10 @@
     lane = lax.broadcasted_iota(jnp.int32, (obs, LANES), 1)
     aux_ref[0:obs, :] = jnp.where(lane < count, 1.0, 0.0)
     base = grid_pos * obs_blocks + place * obs
-    pairs = jnp.concatenate([low_ref[...], mid_ref[...], high_ref[...]], axis=0) - base
+    even = jnp.broadcast_to(lax.rem(grid_pos, 2), mid_ref.shape) == 0
+    low = jnp.where(even, cross_ref[...], chip_ref[...])
+    high = jnp.where(even, chip_ref[...], cross_ref[...])
+    pairs = jnp.concatenate([low, mid_ref[...], high], axis=0) - base
     index = lax.broadcasted_iota(jnp.int32, (blocks_dev, LANES), 0)
     centers = jnp.concatenate(
         [
@@ -172,7 +177,7 @@
         out_ref[b * half : (b + 1) * half, :] = value.astype(out_ref.dtype)
 
 
-def low_kernel(members, obs, blocks, list_ref, item_ref, prior_ref, aux_ref, w_ref, d_ref, low_ref, dev_ref, acc_ref):
+def cross_kernel(members, obs, blocks, list_ref, item_ref, prior_ref, aux_ref, w_ref, d_ref, out_ref, dev_ref, acc_ref):
     rows = d_ref.shape[1]
     total = prior_ref[0, 0:obs].astype(jnp.float32)
     for i in range(1, members):
@@ -191,11 +196,13 @@
     for o in range(obs):
         d_ref[o] = dev_ref[pl.ds(o, rows, stride=obs), :].astype(jnp.bfloat16)
     d_ref[obs] = jnp.zeros((rows, LANES), jnp.bfloat16)
-    accumulate(members, obs, 0, blocks, list_ref, item_ref, d_ref, w_ref, acc_ref)
-    packed_system(members, blocks, acc_ref, low_ref)
-
-
-def next_kernel(members, obs, group, blocks, list_ref, item_ref, d_ref, w_ref, out_ref, acc_ref):
+    group = 2 * lax.rem(lax.axis_index("grid"), 2)
+    accumulate(members, obs, group, blocks, list_ref, item_ref, d_ref, w_ref, acc_ref)
+    packed_system(members, blocks, acc_ref, out_ref)
+
+
+def next_kernel(members, obs, own, blocks, list_ref, item_ref, d_ref, w_ref, out_ref, acc_ref):
+    group = 1 if own else 2 - 2 * lax.rem(lax.axis_index("grid"), 2)
     accumulate(members, obs, group, blocks, list_ref, item_ref, d_ref, w_ref, acc_ref)
     packed_system(members, blocks, acc_ref, out_ref)
 
@@ -338,8 +345,8 @@
     )(far(obs_prior), far(ens_state))
     prior = lax.all_to_all(packed, "mem", split_axis=0, concat_axis=0, tiled=True)
     prior = prior.reshape(members, obs + extra, LANES)
-    from_low = shift(pair_block, 1)
-    from_high = shift(pair_block, -1)
+    pairs_cross = swap(pair_block, True)
+    pairs_chip = swap(pair_block, False)
 
     blocks = 3 * blocks_dev
     weights, aux, lists, items = pl.pallas_call(
@@ -360,12 +367,12 @@
         ],
         compiler_params=pltpu.CompilerParams(vmem_limit_bytes=16 * 2**20),
         name="weights",
-    )(obs_len, near(from_low), pair_block, near(from_high), obs_prec, obs_pos, obs_value)
+    )(obs_len, near(pairs_cross), pair_block, near(pairs_chip), obs_prec, obs_pos, obs_value)
 
     rows = -(-(members + 2) // 16) * 16
     system = pltpu.VMEM((blocks_dev * half, LANES), jnp.bfloat16)
-    d_all, to_low = pl.pallas_call(
-        functools.partial(low_kernel, members, obs, blocks_dev),
+    d_all, to_cross = pl.pallas_call(
+        functools.partial(cross_kernel, members, obs, blocks_dev),
         out_shape=(pltpu.VMEM((obs + 1, rows, LANES), jnp.bfloat16), system),
         in_specs=[scalars, scalars, vmem, vmem, vmem],
         out_specs=(vmem, vmem),
@@ -374,13 +381,13 @@
             pltpu.VMEM(((blocks_dev + 1) * members, LANES), jnp.float32),
         ],
         compiler_params=pltpu.CompilerParams(vmem_limit_bytes=16 * 2**20),
-        name="low",
+        name="cross",
     )(scalar(lists), scalar(items), near(prior), near(aux), near(weights))
-    from_high = shift(to_low, -1)
-
-    def later(group, dtype):
+    from_cross = swap(to_cross, True)
+
+    def later(own, dtype):
         return pl.pallas_call(
-            functools.partial(next_kernel, members, obs, group, blocks_dev),
+            functools.partial(next_kernel, members, obs, own, blocks_dev),
             out_shape=pltpu.VMEM((blocks_dev * half, LANES), dtype),
             in_specs=[scalars, scalars, vmem, vmem],
             out_specs=vmem,
@@ -388,9 +395,9 @@
             compiler_params=pltpu.CompilerParams(vmem_limit_bytes=16 * 2**20),
         )(scalar(lists), scalar(items), near(d_all), near(weights))
 
-    to_high = later(2, jnp.bfloat16)
-    from_low = shift(to_high, 1)
-    own = later(1, jnp.float32)
+    to_chip = later(False, jnp.bfloat16)
+    from_chip = swap(to_chip, False)
+    own = later(True, jnp.float32)
     partial = pl.pallas_call(
         merge_kernel,
         out_shape=pltpu.VMEM((blocks_dev * half, LANES), jnp.bfloat16),
@@ -398,7 +405,7 @@
         out_specs=vmem,
         compiler_params=pltpu.CompilerParams(vmem_limit_bytes=16 * 2**20),
         name="merge",
-    )(near(own), near(from_low), near(from_high))
+    )(near(own), near(from_cross), near(from_chip))
     partial = partial.reshape(mem_count, owned * half, LANES)
     swapped = lax.all_to_all(partial, "mem", split_axis=0, concat_axis=0, tiled=True)
     deviation, mean = pl.pallas_call(

time: 63.5 us -> 64 us (level)
  the two profiles are of different devices: /device:TPU:1 before, /device:TPU:2 now
where the time goes in v10:
time: 64 us; the launch traced here: 63.7 us
  starting transfers between devices  23.3 us (36%)
  Pallas kernels  19 us (30%)
  waiting for transfers between devices  11.9 us (19%)
  blocking collectives  9.27 us (14%)
    ppermute x4, starting transfers between devices, swap(): return lax.ppermute(value, ('mem', 'grid'), pairs)  12.7 us
    all_to_all x1, blocking collectives, per_device(): lax.all_to_all(analysis, 'mem', split_axis=0, concat_axis=0, tiled=True)  9.27 us
    all_to_all x1, starting transfers between devices, per_device(): lax.all_to_all(packed, 'mem', split_axis=0, concat_axis=0, tiled=True)  6.07 us
    all_to_all x1, waiting for transfers between devices, per_device(): lax.all_to_all(partial, 'mem', split_axis=0, concat_axis=0, tiled=True)  5.45 us
    pallas_call x2, Pallas kernels, later(): pl.pallas_call(functools.partial(next_kernel, members, obs, own, blocks_d...  4.65 us
    all_to_all x1, starting transfers between devices, per_device(): lax.all_to_all(partial, 'mem', split_axis=0, concat_axis=0, tiled=True)  4.52 us
    pallas_call x1, Pallas kernels, per_device(): pl.pallas_call(functools.partial(weight_kernel, float(nb_total), obs), ou...  4.46 us
    all_to_all x1, waiting for transfers between devices, per_device(): lax.all_to_all(packed, 'mem', split_axis=0, concat_axis=0, tiled=True)  4.44 us
  transfers between devices with their start and end apart: 6, of which 4 were waited for; matrix products, arithmetic and copies ran while one was open for 0% of the time, Pallas kernels for 11%

profile of v10, /device:TPU:2, one launch (start us, length us, event | category | flops | bytes accessed | tf_op | source)
XLA Modules:
  0.0 63.7 jit_solution(191947321969127901)
XLA Ops:
  0.0 2.6 %pack.1 = bf16[8,10,56,128]{3,2,1,0:T(8,128)(2,1)} custom-call(bf16[10,384,128]{2,1,0:T(8,128)(2,1)} %src_ref.1, bf16[10,16,512]{2,1,0:T(8,128)(2,1)} %state_all.1), custom_call_target="tpu_custom_call" | custom-call | tf_op jit(solution)/shard_map/pack/pallas_call | solution.py:331
  2.6 0.0 copy-start.3
  2.6 0.0 copy-start
  2.6 0.0 copy-start.1
  2.6 0.0 copy-start.2
  2.6 0.0 copy-start.4
  2.6 6.1 %all-to-all-start = ((bf16[8,10,56,128]{3,2,1,0:T(8,128)(2,1)}), bf16[8,10,56,128]{3,2,1,0:T(8,128)(2,1)S(1)}, u32[]{:S(2)}, u32[]{:S(2)}) async-start(bf16[8,10,56,128]{3,2,1,0:T(8,128)(2,1)} %pack.1), calls=%async_computation | async-start | bytes 2293760 | tf_op jit(solution)/shard_map/all_to_all | solution.py:346
  8.7 0.0 copy-done.3
  8.7 5.2 %collective-permute-start = (s32[16,256]{1,0:T(8,128)S(1)}, s32[16,256]{1,0:T(8,128)S(1)}, u32[]{:S(2)}, u32[]{:S(2)}) collective-permute-start(s32[16,256]{1,0:T(8,128)S(1)} %copy-done.3), channel_id=1, source_target_pairs={{0,63},{1,34},{2,33},{3,36},{4,35},{5,38},{6,37},{7,40},{8,39},{9,... | collective-permute-start | bytes 49160 | tf_op jit(solution)/shard_map/ppermute | solution.py:34
  13.9 0.0 collective-permute-start.1
  13.9 1.4 %collective-permute-done.cross_ref = s32[16,256]{1,0:T(8,128)S(1)} collective-permute-done((s32[16,256]{1,0:T(8,128)S(1)}, s32[16,256]{1,0:T(8,128)S(1)}, u32[]{:S(2)}, u32[]{:S(2)}) %collective-permute-start) | collective-permute-done | bytes 16416 | tf_op jit(solution)/shard_map/ppermute | solution.py:34
  15.4 0.0 collective-permute-done.1.chip_ref
  15.4 0.0 copy-done
  15.4 0.0 copy-done.1
  15.4 0.0 copy-done.2
  15.4 0.0 copy-done.4
  15.4 4.5 %weights.1 = (f32[2360,128]{1,0:T(8,128)S(1)}, f32[96,128]{1,0:T(8,128)S(1)}, s32[56,128]{1,0:T(8,128)S(4)}, s32[3,256]{1,0:T(4,128)S(4)}) custom-call(s32[384]{0:T(512)S(1)} %copy-done.4, s32[16,256]{1,0:T(8,128)S(1)} %collective-permute-done.cross_ref, s32[16,256]{1,0:T(8,128)S(1)} %copy-done.3, s32[16,256]{1,0:T(8,128)S(1)} %collective-permute-done.1.chip_ref, ...), custom_call_target="tpu_custom_call" | custom-call | tf_op jit(solution)/shard_map/weights/pallas_call | solution.py:352
  19.8 4.4 %all-to-all-done = bf16[8,10,56,128]{3,2,1,0:T(8,128)(2,1)S(1)} async-done(((bf16[8,10,56,128]{3,2,1,0:T(8,128)(2,1)}), bf16[8,10,56,128]{3,2,1,0:T(8,128)(2,1)S(1)}, u32[]{:S(2)}, u32[]{:S(2)}) %all-to-all-start) | async-done | bytes 1146912 | tf_op jit(solution)/shard_map/all_to_all | solution.py:346
  24.3 3.4 %cross.1 = (bf16[49,96,128]{2,1,0:T(8,128)(2,1)S(1)}, bf16[640,128]{1,0:T(8,128)(2,1)S(1)}) custom-call(s32[56,128]{1,0:T(8,128)S(4)} %get-tuple-element.13.list_ref, s32[3,256]{1,0:T(4,128)S(4)} %get-tuple-element.14.item_ref, bf16[80,56,128]{2,1,0:T(8,128)(2,1)S(1)} %bitcast.3, f32[96,128]{1,0:T(8,128)S(1)} %get-tuple-element.15.aux_ref, ...), custom_call_target="tpu_custom_call" | custom-call | tf_op jit(solution)/shard_map/cross/pallas_call | solution.py:374
  27.7 2.3 %shard_map.74 = bf16[640,128]{1,0:T(8,128)(2,1)S(1)} custom-call(s32[56,128]{1,0:T(8,128)S(4)} %get-tuple-element.13.list_ref, s32[3,256]{1,0:T(4,128)S(4)} %get-tuple-element.14.item_ref, bf16[49,96,128]{2,1,0:T(8,128)(2,1)S(1)} %get-tuple-element.17.d_ref, f32[2360,128]{1,0:T(8,128)S(1)} %get-tuple-element.16.w_ref), custom_call_target="tpu_custom_call" | custom-call | tf_op jit(solution)/shard_map/pallas_call | solution.py:389
  30.0 0.1 collective-permute-start.3
  30.1 7.4 %collective-permute-start.2 = (bf16[640,128]{1,0:T(8,128)(2,1)S(1)}, bf16[640,128]{1,0:T(8,128)(2,1)S(1)}, u32[]{:S(2)}, u32[]{:S(2)}) collective-permute-start(bf16[640,128]{1,0:T(8,128)(2,1)S(1)} %get-tuple-element.18), channel_id=1, source_target_pairs={{0,63},{1,34},{2,33},{3,36},{4,35},{5,38},{6,37},{7,40},{8,39},{9,... | collective-permute-start | bytes 491528 | tf_op jit(solution)/shard_map/ppermute | solution.py:34
  37.5 2.4 %shard_map.73.own_ref = f32[640,128]{1,0:T(8,128)S(1)} custom-call(s32[56,128]{1,0:T(8,128)S(4)} %get-tuple-element.13.list_ref, s32[3,256]{1,0:T(4,128)S(4)} %get-tuple-element.14.item_ref, bf16[49,96,128]{2,1,0:T(8,128)(2,1)S(1)} %get-tuple-element.17.d_ref, f32[2360,128]{1,0:T(8,128)S(1)} %get-tuple-element.16.w_ref), custom_call_target="tpu_custom_call" | custom-call | tf_op jit(solution)/shard_map/pallas_call | solution.py:389
  39.9 0.0 collective-permute-done.3.high_ref
  39.9 0.6 collective-permute-done.2.low_ref
  40.5 0.7 %merge.1 = bf16[640,128]{1,0:T(8,128)(2,1)} custom-call(f32[640,128]{1,0:T(8,128)S(1)} %shard_map.73.own_ref, bf16[640,128]{1,0:T(8,128)(2,1)S(1)} %collective-permute-done.2.low_ref, bf16[640,128]{1,0:T(8,128)(2,1)S(1)} %collective-permute-done.3.high_ref), custom_call_target="tpu_custom_call" | custom-call | tf_op jit(solution)/shard_map/merge/pallas_call | solution.py:401
  41.2 4.5 %all-to-all-start.1 = ((bf16[8,80,128]{2,1,0:T(8,128)(2,1)}), bf16[8,80,128]{2,1,0:T(8,128)(2,1)S(1)}, u32[]{:S(2)}, u32[]{:S(2)}) async-start(bf16[8,80,128]{2,1,0:T(8,128)(2,1)} %bitcast.1), calls=%async_computation.1 | async-start | bytes 327680 | tf_op jit(solution)/shard_map/all_to_all | solution.py:410
  45.7 0.2 state.1
  45.9 5.4 %all-to-all-done.1.system_ref = bf16[8,80,128]{2,1,0:T(8,128)(2,1)S(1)} async-done(((bf16[8,80,128]{2,1,0:T(8,128)(2,1)}), bf16[8,80,128]{2,1,0:T(8,128)(2,1)S(1)}, u32[]{:S(2)}, u32[]{:S(2)}) %all-to-all-start.1) | async-done | bytes 163872 | tf_op jit(solution)/shard_map/all_to_all | solution.py:410
  51.3 2.3 %finish.1 = bf16[640,128]{1,0:T(8,128)(2,1)S(1)} custom-call(bf16[8,80,128]{2,1,0:T(8,128)(2,1)S(1)} %all-to-all-done.1.system_ref, bf16[80,1024]{1,0:T(8,128)(2,1)S(1)} %get-tuple-element.19.dev_ref, f32[8,128]{1,0:T(8,128)S(1)} %get-tuple-element.20.mean_ref), custom_call_target="tpu_custom_call" | custom-call | tf_op jit(solution)/shard_map/finish/pallas_call | solution.py:423
  53.7 9.3 %all_to_all.15.part_ref = bf16[8,10,8,128]{3,2,1,0:T(8,128)(2,1)S(1)} all-to-all(bf16[8,10,8,128]{3,2,1,0:T(8,128)(2,1)S(1)} %bitcast.5), channel_id=1, replica_groups=mesh['mem'=8,'grid'=32] {'mem'}, dimensions={0} | all-to-all | bytes 327680 | tf_op jit(solution)/shard_map/all_to_all | solution.py:433
  63.0 0.8 %unpack.1 = bf16[10,16,512]{2,1,0:T(8,128)(2,1)} custom-call(bf16[8,10,8,128]{3,2,1,0:T(8,128)(2,1)S(1)} %all_to_all.15.part_ref), custom_call_target="tpu_custom_call" | custom-call | tf_op jit(solution)/shard_map/unpack/pallas_call | solution.py:434
Async XLA Ops:
  2.6 6.1 %copy-start.3 = (s32[16,256]{1,0:T(8,128)S(1)}, s32[16,256]{1,0:T(8,128)}, u32[]{:S(2)}) copy-start(s32[16,256]{1,0:T(8,128)} %mid_ref.1) | copy-start | bytes 49156
  2.6 12.8 %copy-start = (f32[384,128]{1,0:T(8,128)S(1)}, f32[384,128]{1,0:T(8,128)}, u32[]{:S(2)}) copy-start(f32[384,128]{1,0:T(8,128)} %prec_all.1) | copy-start | bytes 589828
  2.6 12.8 %copy-start.1 = (f32[384,128]{1,0:T(8,128)S(1)}, f32[384,128]{1,0:T(8,128)}, u32[]{:S(2)}) copy-start(f32[384,128]{1,0:T(8,128)} %pos_all.1) | copy-start | bytes 589828
  2.6 12.8 %copy-start.2 = (f32[384,128]{1,0:T(8,128)S(1)}, f32[384,128]{1,0:T(8,128)}, u32[]{:S(2)}) copy-start(f32[384,128]{1,0:T(8,128)} %value_all.1) | copy-start | bytes 589828
  2.6 12.8 %copy-start.4 = (s32[384]{0:T(512)S(1)}, s32[384]{0:T(512)}, u32[]{:S(2)}) copy-start(s32[384]{0:T(512)} %len_ref.1) | copy-start | bytes 4612
  2.6 21.7 %all-to-all-start = ((bf16[8,10,56,128]{3,2,1,0:T(8,128)(2,1)}), bf16[8,10,56,128]{3,2,1,0:T(8,128)(2,1)S(1)}, u32[]{:S(2)}, u32[]{:S(2)}) async-start(bf16[8,10,56,128]{3,2,1,0:T(8,128)(2,1)} %pack.1), calls=%async_computation | async-start | bytes 2293760 | tf_op jit(solution)/shard_map/all_to_all | solution.py:346
  8.7 6.7 %collective-permute-start = (s32[16,256]{1,0:T(8,128)S(1)}, s32[16,256]{1,0:T(8,128)S(1)}, u32[]{:S(2)}, u32[]{:S(2)}) collective-permute-start(s32[16,256]{1,0:T(8,128)S(1)} %copy-done.3), channel_id=1, source_target_pairs={{0,63},{1,34},{2,33},{3,36},{4,35},{5,38},{6,37},{7,40},{8,39},{9,... | collective-permute-start | bytes 49160 | tf_op jit(solution)/shard_map/ppermute | solution.py:34
  13.9 1.4 %collective-permute-start.1 = (s32[16,256]{1,0:T(8,128)S(1)}, s32[16,256]{1,0:T(8,128)S(1)}, u32[]{:S(2)}, u32[]{:S(2)}) collective-permute-start(s32[16,256]{1,0:T(8,128)S(1)} %copy-done.3), channel_id=1, source_target_pairs={{0,1},{1,0},{2,3},{3,2},{4,5},{5,4},{6,7},{7,6},{8,9},{9,8},{10,11... | collective-permute-start | bytes 49160 | tf_op jit(solution)/shard_map/ppermute | solution.py:34
  30.0 9.9 %collective-permute-start.3 = (bf16[640,128]{1,0:T(8,128)(2,1)S(1)}, bf16[640,128]{1,0:T(8,128)(2,1)S(1)}, u32[]{:S(2)}, u32[]{:S(2)}) collective-permute-start(bf16[640,128]{1,0:T(8,128)(2,1)S(1)} %shard_map.74), channel_id=1, source_target_pairs={{0,1},{1,0},{2,3},{3,2},{4,5},{5,4},{6,7},{7,6},{8,9},{9,8},{10,11... | collective-permute-start | bytes 491528 | tf_op jit(solution)/shard_map/ppermute | solution.py:34
  30.1 10.4 %collective-permute-start.2 = (bf16[640,128]{1,0:T(8,128)(2,1)S(1)}, bf16[640,128]{1,0:T(8,128)(2,1)S(1)}, u32[]{:S(2)}, u32[]{:S(2)}) collective-permute-start(bf16[640,128]{1,0:T(8,128)(2,1)S(1)} %get-tuple-element.18), channel_id=1, source_target_pairs={{0,63},{1,34},{2,33},{3,36},{4,35},{5,38},{6,37},{7,40},{8,39},{9,... | collective-permute-start | bytes 491528 | tf_op jit(solution)/shard_map/ppermute | solution.py:34
  41.2 10.1 %all-to-all-start.1 = ((bf16[8,80,128]{2,1,0:T(8,128)(2,1)}), bf16[8,80,128]{2,1,0:T(8,128)(2,1)S(1)}, u32[]{:S(2)}, u32[]{:S(2)}) async-start(bf16[8,80,128]{2,1,0:T(8,128)(2,1)} %bitcast.1), calls=%async_computation.1 | async-start | bytes 327680 | tf_op jit(solution)/shard_map/all_to_all | solution.py:410

commit v11 on v10

--- a/solution.py
+++ b/solution.py
@@ -13,9 +13,10 @@
 LANES = 128
 COUNT = 127
 UNIT = 4
-TURN = 18
+TURN = 28
 ROOM = 256
 SPAN = 16
+PITCH = 49
 
 inflation = 1.1
 
@@ -185,16 +186,16 @@
     mean = total / members
     valid = aux_ref[0:obs, :] > 0.0
     for i in range(members):
-        dev_ref[i * obs : (i + 1) * obs, :] = jnp.where(
+        dev_ref[i * PITCH : i * PITCH + obs, :] = jnp.where(
             valid, prior_ref[i, 0:obs].astype(jnp.float32) - mean, 0.0
         )
     departure = jnp.where(valid, aux_ref[obs : 2 * obs, :] - mean, 0.0)
     high = departure.astype(jnp.bfloat16).astype(jnp.float32)
-    dev_ref[members * obs : (members + 1) * obs, :] = high
-    dev_ref[(members + 1) * obs : (members + 2) * obs, :] = departure - high
-    dev_ref[(members + 2) * obs :, :] = jnp.zeros(((rows - members - 2) * obs, LANES), jnp.float32)
+    dev_ref[members * PITCH : members * PITCH + obs, :] = high
+    dev_ref[(members + 1) * PITCH : (members + 1) * PITCH + obs, :] = departure - high
+    dev_ref[(members + 2) * PITCH :, :] = jnp.zeros(((rows - members - 2) * PITCH, LANES), jnp.float32)
     for o in range(obs):
-        d_ref[o] = dev_ref[pl.ds(o, rows, stride=obs), :].astype(jnp.bfloat16)
+        d_ref[o] = dev_ref[pl.ds(o, rows, stride=PITCH), :].astype(jnp.bfloat16)
     d_ref[obs] = jnp.zeros((rows, LANES), jnp.bfloat16)
     group = 2 * lax.rem(lax.axis_index("grid"), 2)
     accumulate(members, obs, group, blocks, list_ref, item_ref, d_ref, w_ref, acc_ref)
@@ -261,9 +262,13 @@
         sums = jnp.sum(jnp.abs(system), axis=1, keepdims=True)
         bound.append(jnp.max(sums, axis=0, keepdims=True))
         y_iter.append(system / bound[r])
-        f_top = part[:, members : members + 1] + part[:, members + 1 : members + 2]
-        f_low = part[:, members + 2 : members + 3] + part[:, members + 3 : members + 4]
-        force.append(jnp.concatenate([f_top, f_low], axis=0))
+        turned = jnp.transpose(square)
+        sums_hl = turned[members : members + 8] + pltpu.roll(turned[members : members + 8], 7, 0)
+        low = jnp.broadcast_to(sums_hl[2:3], (8, LANES))
+        row = jnp.broadcast_to(sums_hl[0:1], (8, LANES))
+        lane8 = lax.broadcasted_iota(jnp.int32, (8, LANES), 1)
+        row = jnp.where(lane8 < half, row, pltpu.roll(low, half, 1))
+        force.append(row[:, :members])
     for sweep in range(NSIT):
         if sweep == 0:
             factor = [1.5 * identity - 0.5 * y for y in y_iter]
@@ -273,13 +278,14 @@
             z_next = [dot(f, z) for f, z in zip(factor, z_iter)]
         if sweep + 1 < NSIT:
             y_iter = [dot(y, f) for y, f in zip(y_iter, factor)]
+        else:
+            before = [dot(row, z) for row, z in zip(force, z_iter)]
+            before = [dot(row, f) for row, f in zip(before, factor)]
         z_iter = z_next
     for r in range(owned):
-        root = z_iter[r] / jnp.sqrt(bound[r])
-        first = dot(root, jnp.broadcast_to(force[r], (members, LANES)))
-        shiftu = dot(root, first)[:, :1]
-        transform = math.sqrt(members - 1) * root + shiftu
-        turned = jnp.transpose(transform).astype(jnp.bfloat16)
+        weight = dot(before[r], z_iter[r])[0:1] / bound[r]
+        turned = math.sqrt(members - 1) * (z_iter[r] / jnp.sqrt(bound[r])) + weight
+        turned = turned.astype(jnp.bfloat16)
         for k in range(r, rows_out, owned):
             moved = jnp.dot(
                 turned, dev_ref[:, k * LANES : (k + 1) * LANES], preferred_element_type=jnp.float32
@@ -377,7 +383,7 @@
         in_specs=[scalars, scalars, vmem, vmem, vmem],
         out_specs=(vmem, vmem),
         scratch_shapes=[
-            pltpu.VMEM((rows * obs, LANES), jnp.float32),
+            pltpu.VMEM((rows * PITCH, LANES), jnp.float32),
             pltpu.VMEM(((blocks_dev + 1) * members, LANES), jnp.float32),
         ],
         compiler_params=pltpu.CompilerParams(vmem_limit_bytes=16 * 2**20),

time: 64 us -> 62.9 us (0.983)
  Pallas kernels: 19 us -> 17.7 us
    pallas_call x1, Pallas kernels: 3.4 us -> 2.61 us  [per_device(): pl.pallas_call(functools.partial(cross_kernel, members, obs, blocks_dev),...]
where the time goes in v11:
time: 62.9 us; the launch traced here: 62.6 us
  starting transfers between devices  23.5 us (37%)
  Pallas kernels  17.7 us (28%)
  waiting for transfers between devices  11.9 us (19%)
  blocking collectives  9.27 us (15%)
    ppermute x4, starting transfers between devices, swap(): return lax.ppermute(value, ('mem', 'grid'), pairs)  12.5 us
    all_to_all x1, blocking collectives, per_device(): lax.all_to_all(analysis, 'mem', split_axis=0, concat_axis=0, tiled=True)  9.27 us
    all_to_all x1, starting transfers between devices, per_device(): lax.all_to_all(packed, 'mem', split_axis=0, concat_axis=0, tiled=True)  6.07 us
    all_to_all x1, waiting for transfers between devices, per_device(): lax.all_to_all(partial, 'mem', split_axis=0, concat_axis=0, tiled=True)  5.45 us
    all_to_all x1, starting transfers between devices, per_device(): lax.all_to_all(partial, 'mem', split_axis=0, concat_axis=0, tiled=True)  4.9 us
    pallas_call x1, Pallas kernels, per_device(): pl.pallas_call(functools.partial(weight_kernel, float(nb_total), obs), ou...  4.52 us
    pallas_call x2, Pallas kernels, later(): pl.pallas_call(functools.partial(next_kernel, members, obs, own, blocks_d...  4.52 us
    all_to_all x1, waiting for transfers between devices, per_device(): lax.all_to_all(packed, 'mem', split_axis=0, concat_axis=0, tiled=True)  4.38 us
  transfers between devices with their start and end apart: 6, of which 4 were waited for; matrix products, arithmetic and copies ran while one was open for 0% of the time, Pallas kernels for 11%

profile of v11, /device:TPU:2, one launch (start us, length us, event | category | flops | bytes accessed | tf_op | source)
XLA Modules:
  0.0 62.6 jit_solution(16585374868513871961)
XLA Ops:
  0.0 2.6 %pack.1 = bf16[8,10,56,128]{3,2,1,0:T(8,128)(2,1)} custom-call(bf16[10,384,128]{2,1,0:T(8,128)(2,1)} %src_ref.1, bf16[10,16,512]{2,1,0:T(8,128)(2,1)} %state_all.1), custom_call_target="tpu_custom_call" | custom-call | tf_op jit(solution)/shard_map/pack/pallas_call | solution.py:337
  2.6 0.0 copy-start.3
  2.6 0.0 copy-start
  2.6 0.0 copy-start.1
  2.6 0.0 copy-start.2
  2.6 0.0 copy-start.4
  2.6 6.1 %all-to-all-start = ((bf16[8,10,56,128]{3,2,1,0:T(8,128)(2,1)}), bf16[8,10,56,128]{3,2,1,0:T(8,128)(2,1)S(1)}, u32[]{:S(2)}, u32[]{:S(2)}) async-start(bf16[8,10,56,128]{3,2,1,0:T(8,128)(2,1)} %pack.1), calls=%async_computation | async-start | bytes 2293760 | tf_op jit(solution)/shard_map/all_to_all | solution.py:352
  8.7 0.0 copy-done.3
  8.7 5.2 %collective-permute-start = (s32[16,256]{1,0:T(8,128)S(1)}, s32[16,256]{1,0:T(8,128)S(1)}, u32[]{:S(2)}, u32[]{:S(2)}) collective-permute-start(s32[16,256]{1,0:T(8,128)S(1)} %copy-done.3), channel_id=1, source_target_pairs={{0,63},{1,34},{2,33},{3,36},{4,35},{5,38},{6,37},{7,40},{8,39},{9,... | collective-permute-start | bytes 49160 | tf_op jit(solution)/shard_map/ppermute | solution.py:35
  13.9 0.0 collective-permute-start.1
  13.9 1.4 %collective-permute-done.cross_ref = s32[16,256]{1,0:T(8,128)S(1)} collective-permute-done((s32[16,256]{1,0:T(8,128)S(1)}, s32[16,256]{1,0:T(8,128)S(1)}, u32[]{:S(2)}, u32[]{:S(2)}) %collective-permute-start) | collective-permute-done | bytes 16416 | tf_op jit(solution)/shard_map/ppermute | solution.py:35
  15.4 0.0 collective-permute-done.1.chip_ref
  15.4 0.0 copy-done
  15.4 0.0 copy-done.1
  15.4 0.0 copy-done.2
  15.4 0.0 copy-done.4
  15.4 4.5 %weights.1 = (f32[2360,128]{1,0:T(8,128)S(1)}, f32[96,128]{1,0:T(8,128)S(1)}, s32[56,128]{1,0:T(8,128)S(4)}, s32[3,256]{1,0:T(4,128)S(4)}) custom-call(s32[384]{0:T(512)S(1)} %copy-done.4, s32[16,256]{1,0:T(8,128)S(1)} %collective-permute-done.cross_ref, s32[16,256]{1,0:T(8,128)S(1)} %copy-done.3, s32[16,256]{1,0:T(8,128)S(1)} %collective-permute-done.1.chip_ref, ...), custom_call_target="tpu_custom_call" | custom-call | tf_op jit(solution)/shard_map/weights/pallas_call | solution.py:358
  19.9 4.4 %all-to-all-done = bf16[8,10,56,128]{3,2,1,0:T(8,128)(2,1)S(1)} async-done(((bf16[8,10,56,128]{3,2,1,0:T(8,128)(2,1)}), bf16[8,10,56,128]{3,2,1,0:T(8,128)(2,1)S(1)}, u32[]{:S(2)}, u32[]{:S(2)}) %all-to-all-start) | async-done | bytes 1146912 | tf_op jit(solution)/shard_map/all_to_all | solution.py:352
  24.3 2.6 %cross.1 = (bf16[49,96,128]{2,1,0:T(8,128)(2,1)S(1)}, bf16[640,128]{1,0:T(8,128)(2,1)S(1)}) custom-call(s32[56,128]{1,0:T(8,128)S(4)} %get-tuple-element.13.list_ref, s32[3,256]{1,0:T(4,128)S(4)} %get-tuple-element.14.item_ref, bf16[80,56,128]{2,1,0:T(8,128)(2,1)S(1)} %bitcast.3, f32[96,128]{1,0:T(8,128)S(1)} %get-tuple-element.15.aux_ref, ...), custom_call_target="tpu_custom_call" | custom-call | tf_op jit(solution)/shard_map/cross/pallas_call | solution.py:380
  26.9 2.2 %shard_map.74 = bf16[640,128]{1,0:T(8,128)(2,1)S(1)} custom-call(s32[56,128]{1,0:T(8,128)S(4)} %get-tuple-element.13.list_ref, s32[3,256]{1,0:T(4,128)S(4)} %get-tuple-element.14.item_ref, bf16[49,96,128]{2,1,0:T(8,128)(2,1)S(1)} %get-tuple-element.17.d_ref, f32[2360,128]{1,0:T(8,128)S(1)} %get-tuple-element.16.w_ref), custom_call_target="tpu_custom_call" | custom-call | tf_op jit(solution)/shard_map/pallas_call | solution.py:395
  29.1 0.1 collective-permute-start.3
  29.2 7.2 %collective-permute-start.2 = (bf16[640,128]{1,0:T(8,128)(2,1)S(1)}, bf16[640,128]{1,0:T(8,128)(2,1)S(1)}, u32[]{:S(2)}, u32[]{:S(2)}) collective-permute-start(bf16[640,128]{1,0:T(8,128)(2,1)S(1)} %get-tuple-element.18), channel_id=1, source_target_pairs={{0,63},{1,34},{2,33},{3,36},{4,35},{5,38},{6,37},{7,40},{8,39},{9,... | collective-permute-start | bytes 491528 | tf_op jit(solution)/shard_map/ppermute | solution.py:35
  36.4 2.3 %shard_map.73.own_ref = f32[640,128]{1,0:T(8,128)S(1)} custom-call(s32[56,128]{1,0:T(8,128)S(4)} %get-tuple-element.13.list_ref, s32[3,256]{1,0:T(4,128)S(4)} %get-tuple-element.14.item_ref, bf16[49,96,128]{2,1,0:T(8,128)(2,1)S(1)} %get-tuple-element.17.d_ref, f32[2360,128]{1,0:T(8,128)S(1)} %get-tuple-element.16.w_ref), custom_call_target="tpu_custom_call" | custom-call | tf_op jit(solution)/shard_map/pallas_call | solution.py:395
  38.8 0.0 collective-permute-done.3.high_ref
  38.8 0.7 %collective-permute-done.2.low_ref = bf16[640,128]{1,0:T(8,128)(2,1)S(1)} collective-permute-done((bf16[640,128]{1,0:T(8,128)(2,1)S(1)}, bf16[640,128]{1,0:T(8,128)(2,1)S(1)}, u32[]{:S(2)}, u32[]{:S(2)}) %collective-permute-start.2) | collective-permute-done | bytes 163872 | tf_op jit(solution)/shard_map/ppermute | solution.py:35
  39.4 0.7 %merge.1 = bf16[640,128]{1,0:T(8,128)(2,1)} custom-call(f32[640,128]{1,0:T(8,128)S(1)} %shard_map.73.own_ref, bf16[640,128]{1,0:T(8,128)(2,1)S(1)} %collective-permute-done.2.low_ref, bf16[640,128]{1,0:T(8,128)(2,1)S(1)} %collective-permute-done.3.high_ref), custom_call_target="tpu_custom_call" | custom-call | tf_op jit(solution)/shard_map/merge/pallas_call | solution.py:407
  40.2 4.9 %all-to-all-start.1 = ((bf16[8,80,128]{2,1,0:T(8,128)(2,1)}), bf16[8,80,128]{2,1,0:T(8,128)(2,1)S(1)}, u32[]{:S(2)}, u32[]{:S(2)}) async-start(bf16[8,80,128]{2,1,0:T(8,128)(2,1)} %bitcast.1), calls=%async_computation.1 | async-start | bytes 327680 | tf_op jit(solution)/shard_map/all_to_all | solution.py:416
  45.1 0.2 state.1
  45.2 5.4 %all-to-all-done.1.system_ref = bf16[8,80,128]{2,1,0:T(8,128)(2,1)S(1)} async-done(((bf16[8,80,128]{2,1,0:T(8,128)(2,1)}), bf16[8,80,128]{2,1,0:T(8,128)(2,1)S(1)}, u32[]{:S(2)}, u32[]{:S(2)}) %all-to-all-start.1) | async-done | bytes 163872 | tf_op jit(solution)/shard_map/all_to_all | solution.py:416
  50.7 1.9 %finish.1 = bf16[640,128]{1,0:T(8,128)(2,1)S(1)} custom-call(bf16[8,80,128]{2,1,0:T(8,128)(2,1)S(1)} %all-to-all-done.1.system_ref, bf16[80,1024]{1,0:T(8,128)(2,1)S(1)} %get-tuple-element.19.dev_ref, f32[8,128]{1,0:T(8,128)S(1)} %get-tuple-element.20.mean_ref), custom_call_target="tpu_custom_call" | custom-call | tf_op jit(solution)/shard_map/finish/pallas_call | solution.py:429
  52.6 9.3 %all_to_all.15.part_ref = bf16[8,10,8,128]{3,2,1,0:T(8,128)(2,1)S(1)} all-to-all(bf16[8,10,8,128]{3,2,1,0:T(8,128)(2,1)S(1)} %bitcast.5), channel_id=1, replica_groups=mesh['mem'=8,'grid'=32] {'mem'}, dimensions={0} | all-to-all | bytes 327680 | tf_op jit(solution)/shard_map/all_to_all | solution.py:439
  61.8 0.8 %unpack.1 = bf16[10,16,512]{2,1,0:T(8,128)(2,1)} custom-call(bf16[8,10,8,128]{3,2,1,0:T(8,128)(2,1)S(1)} %all_to_all.15.part_ref), custom_call_target="tpu_custom_call" | custom-call | tf_op jit(solution)/shard_map/unpack/pallas_call | solution.py:440
Async XLA Ops:
  2.6 6.1 %copy-start.3 = (s32[16,256]{1,0:T(8,128)S(1)}, s32[16,256]{1,0:T(8,128)}, u32[]{:S(2)}) copy-start(s32[16,256]{1,0:T(8,128)} %mid_ref.1) | copy-start | bytes 49156
  2.6 12.8 %copy-start = (f32[384,128]{1,0:T(8,128)S(1)}, f32[384,128]{1,0:T(8,128)}, u32[]{:S(2)}) copy-start(f32[384,128]{1,0:T(8,128)} %prec_all.1) | copy-start | bytes 589828
  2.6 12.8 %copy-start.1 = (f32[384,128]{1,0:T(8,128)S(1)}, f32[384,128]{1,0:T(8,128)}, u32[]{:S(2)}) copy-start(f32[384,128]{1,0:T(8,128)} %pos_all.1) | copy-start | bytes 589828
  2.6 12.8 %copy-start.2 = (f32[384,128]{1,0:T(8,128)S(1)}, f32[384,128]{1,0:T(8,128)}, u32[]{:S(2)}) copy-start(f32[384,128]{1,0:T(8,128)} %value_all.1) | copy-start | bytes 589828
  2.6 12.8 %copy-start.4 = (s32[384]{0:T(512)S(1)}, s32[384]{0:T(512)}, u32[]{:S(2)}) copy-start(s32[384]{0:T(512)} %len_ref.1) | copy-start | bytes 4612
  2.6 21.7 %all-to-all-start = ((bf16[8,10,56,128]{3,2,1,0:T(8,128)(2,1)}), bf16[8,10,56,128]{3,2,1,0:T(8,128)(2,1)S(1)}, u32[]{:S(2)}, u32[]{:S(2)}) async-start(bf16[8,10,56,128]{3,2,1,0:T(8,128)(2,1)} %pack.1), calls=%async_computation | async-start | bytes 2293760 | tf_op jit(solution)/shard_map/all_to_all | solution.py:352
  8.7 6.7 %collective-permute-start = (s32[16,256]{1,0:T(8,128)S(1)}, s32[16,256]{1,0:T(8,128)S(1)}, u32[]{:S(2)}, u32[]{:S(2)}) collective-permute-start(s32[16,256]{1,0:T(8,128)S(1)} %copy-done.3), channel_id=1, source_target_pairs={{0,63},{1,34},{2,33},{3,36},{4,35},{5,38},{6,37},{7,40},{8,39},{9,... | collective-permute-start | bytes 49160 | tf_op jit(solution)/shard_map/ppermute | solution.py:35
  13.9 1.4 %collective-permute-start.1 = (s32[16,256]{1,0:T(8,128)S(1)}, s32[16,256]{1,0:T(8,128)S(1)}, u32[]{:S(2)}, u32[]{:S(2)}) collective-permute-start(s32[16,256]{1,0:T(8,128)S(1)} %copy-done.3), channel_id=1, source_target_pairs={{0,1},{1,0},{2,3},{3,2},{4,5},{5,4},{6,7},{7,6},{8,9},{9,8},{10,11... | collective-permute-start | bytes 49160 | tf_op jit(solution)/shard_map/ppermute | solution.py:35
  29.1 9.6 %collective-permute-start.3 = (bf16[640,128]{1,0:T(8,128)(2,1)S(1)}, bf16[640,128]{1,0:T(8,128)(2,1)S(1)}, u32[]{:S(2)}, u32[]{:S(2)}) collective-permute-start(bf16[640,128]{1,0:T(8,128)(2,1)S(1)} %shard_map.74), channel_id=1, source_target_pairs={{0,1},{1,0},{2,3},{3,2},{4,5},{5,4},{6,7},{7,6},{8,9},{9,8},{10,11... | collective-permute-start | bytes 491528 | tf_op jit(solution)/shard_map/ppermute | solution.py:35
  29.2 10.2 %collective-permute-start.2 = (bf16[640,128]{1,0:T(8,128)(2,1)S(1)}, bf16[640,128]{1,0:T(8,128)(2,1)S(1)}, u32[]{:S(2)}, u32[]{:S(2)}) collective-permute-start(bf16[640,128]{1,0:T(8,128)(2,1)S(1)} %get-tuple-element.18), channel_id=1, source_target_pairs={{0,63},{1,34},{2,33},{3,36},{4,35},{5,38},{6,37},{7,40},{8,39},{9,... | collective-permute-start | bytes 491528 | tf_op jit(solution)/shard_map/ppermute | solution.py:35
  40.2 10.5 %all-to-all-start.1 = ((bf16[8,80,128]{2,1,0:T(8,128)(2,1)}), bf16[8,80,128]{2,1,0:T(8,128)(2,1)S(1)}, u32[]{:S(2)}, u32[]{:S(2)}) async-start(bf16[8,80,128]{2,1,0:T(8,128)(2,1)} %bitcast.1), calls=%async_computation.1 | async-start | bytes 327680 | tf_op jit(solution)/shard_map/all_to_all | solution.py:416

commit v12 on v11

--- a/solution.py
+++ b/solution.py
@@ -178,7 +178,7 @@
         out_ref[b * half : (b + 1) * half, :] = value.astype(out_ref.dtype)
 
 
-def cross_kernel(members, obs, blocks, list_ref, item_ref, prior_ref, aux_ref, w_ref, d_ref, out_ref, dev_ref, acc_ref):
+def cross_kernel(members, obs, blocks, list_ref, item_ref, prior_ref, aux_ref, w_ref, d_ref, out_ref, early_ref, dev_ref, acc_ref):
     rows = d_ref.shape[1]
     total = prior_ref[0, 0:obs].astype(jnp.float32)
     for i in range(1, members):
@@ -197,14 +197,33 @@
     for o in range(obs):
         d_ref[o] = dev_ref[pl.ds(o, rows, stride=PITCH), :].astype(jnp.bfloat16)
     d_ref[obs] = jnp.zeros((rows, LANES), jnp.bfloat16)
-    group = 2 * lax.rem(lax.axis_index("grid"), 2)
+    place = lax.axis_index("grid")
+    group = 2 * lax.rem(place, 2)
     accumulate(members, obs, group, blocks, list_ref, item_ref, d_ref, w_ref, acc_ref)
     packed_system(members, blocks, acc_ref, out_ref)
 
-
-def next_kernel(members, obs, own, blocks, list_ref, item_ref, d_ref, w_ref, out_ref, acc_ref):
-    group = 1 if own else 2 - 2 * lax.rem(lax.axis_index("grid"), 2)
-    accumulate(members, obs, group, blocks, list_ref, item_ref, d_ref, w_ref, acc_ref)
+    @pl.when(place == 0)
+    def _():
+        accumulate(members, obs, 2 - group, blocks, list_ref, item_ref, d_ref, w_ref, acc_ref)
+        packed_system(members, blocks, acc_ref, early_ref)
+
+
+def chip_kernel(members, obs, blocks, list_ref, item_ref, d_ref, w_ref, early_ref, out_ref, acc_ref):
+    place = lax.axis_index("grid")
+
+    @pl.when(place == 0)
+    def _():
+        out_ref[...] = early_ref[...]
+
+    @pl.when(place != 0)
+    def _():
+        group = 2 - 2 * lax.rem(place, 2)
+        accumulate(members, obs, group, blocks, list_ref, item_ref, d_ref, w_ref, acc_ref)
+        packed_system(members, blocks, acc_ref, out_ref)
+
+
+def own_kernel(members, obs, blocks, list_ref, item_ref, d_ref, w_ref, out_ref, acc_ref):
+    accumulate(members, obs, 1, blocks, list_ref, item_ref, d_ref, w_ref, acc_ref)
     packed_system(members, blocks, acc_ref, out_ref)
 
 
@@ -377,11 +396,11 @@
 
     rows = -(-(members + 2) // 16) * 16
     system = pltpu.VMEM((blocks_dev * half, LANES), jnp.bfloat16)
-    d_all, to_cross = pl.pallas_call(
+    d_all, to_cross, early = pl.pallas_call(
         functools.partial(cross_kernel, members, obs, blocks_dev),
-        out_shape=(pltpu.VMEM((obs + 1, rows, LANES), jnp.bfloat16), system),
+        out_shape=(pltpu.VMEM((obs + 1, rows, LANES), jnp.bfloat16), system, system),
         in_specs=[scalars, scalars, vmem, vmem, vmem],
-        out_specs=(vmem, vmem),
+        out_specs=(vmem, vmem, vmem),
         scratch_shapes=[
             pltpu.VMEM((rows * PITCH, LANES), jnp.float32),
             pltpu.VMEM(((blocks_dev + 1) * members, LANES), jnp.float32),
@@ -391,19 +410,19 @@
     )(scalar(lists), scalar(items), near(prior), near(aux), near(weights))
     from_cross = swap(to_cross, True)
 
-    def later(own, dtype):
+    def later(kernel, more, dtype):
         return pl.pallas_call(
-            functools.partial(next_kernel, members, obs, own, blocks_dev),
+            functools.partial(kernel, members, obs, blocks_dev),
             out_shape=pltpu.VMEM((blocks_dev * half, LANES), dtype),
-            in_specs=[scalars, scalars, vmem, vmem],
+            in_specs=[scalars, scalars, vmem, vmem] + [vmem] * len(more),
             out_specs=vmem,
             scratch_shapes=[pltpu.VMEM(((blocks_dev + 1) * members, LANES), jnp.float32)],
             compiler_params=pltpu.CompilerParams(vmem_limit_bytes=16 * 2**20),
-        )(scalar(lists), scalar(items), near(d_all), near(weights))
-
-    to_chip = later(False, jnp.bfloat16)
+        )(scalar(lists), scalar(items), near(d_all), near(weights), *(near(value) for value in more))
+
+    to_chip = later(chip_kernel, (early,), jnp.bfloat16)
     from_chip = swap(to_chip, False)
-    own = later(True, jnp.float32)
+    own = later(own_kernel, (), jnp.float32)
     partial = pl.pallas_call(
         merge_kernel,
         out_shape=pltpu.VMEM((blocks_dev * half, LANES), jnp.bfloat16),
@@ -457,6 +476,4 @@
         P("grid", None),
         P("grid", None),
     )
-    return jax.shard_map(
-        per_device, mesh=mesh, in_specs=placed, out_specs=P("mem", "grid", None), check_vma=False
-    )
+    return jax.shard_map(per_device, mesh=mesh, in_specs=placed, out_specs=P("mem", "grid", None), check_vma=False)

time: 62.9 us -> 62.8 us (level)
    pallas_call x2, Pallas kernels: 4.52 us -> 2.34 us  [later(): pl.pallas_call(functools.partial(kernel, members, obs, blocks_dev), out_s...]
    pallas_call x1, Pallas kernels: 2.61 us -> 4.79 us  [per_device(): pl.pallas_call(functools.partial(cross_kernel, members, obs, blocks_dev),...]
where the time goes in v12:
time: 62.8 us; the launch traced here: 62.5 us
  starting transfers between devices  23.4 us (37%)
  Pallas kernels  17.7 us (28%)
  waiting for transfers between devices  11.9 us (19%)
  blocking collectives  9.27 us (15%)
    ppermute x4, starting transfers between devices, swap(): return lax.ppermute(value, ('mem', 'grid'), pairs)  12.6 us
    all_to_all x1, blocking collectives, per_device(): lax.all_to_all(analysis, 'mem', split_axis=0, concat_axis=0, tiled=True)  9.27 us
    all_to_all x1, starting transfers between devices, per_device(): lax.all_to_all(packed, 'mem', split_axis=0, concat_axis=0, tiled=True)  6.07 us
    all_to_all x1, waiting for transfers between devices, per_device(): lax.all_to_all(partial, 'mem', split_axis=0, concat_axis=0, tiled=True)  5.45 us
    pallas_call x1, Pallas kernels, per_device(): pl.pallas_call(functools.partial(cross_kernel, members, obs, blocks_dev),...  4.79 us
    all_to_all x1, starting transfers between devices, per_device(): lax.all_to_all(partial, 'mem', split_axis=0, concat_axis=0, tiled=True)  4.72 us
    pallas_call x1, Pallas kernels, per_device(): pl.pallas_call(functools.partial(weight_kernel, float(nb_total), obs), ou...  4.52 us
    all_to_all x1, waiting for transfers between devices, per_device(): lax.all_to_all(packed, 'mem', split_axis=0, concat_axis=0, tiled=True)  4.38 us
  transfers between devices with their start and end apart: 6, of which 4 were waited for; matrix products, arithmetic and copies ran while one was open for 0% of the time, Pallas kernels for 11%

profile of v12, /device:TPU:2, one launch (start us, length us, event | category | flops | bytes accessed | tf_op | source)
XLA Modules:
  0.0 62.5 jit_solution(14430790250820603033)
XLA Ops:
  0.0 2.6 %pack.1 = bf16[8,10,56,128]{3,2,1,0:T(8,128)(2,1)} custom-call(bf16[10,384,128]{2,1,0:T(8,128)(2,1)} %src_ref.1, bf16[10,16,512]{2,1,0:T(8,128)(2,1)} %state_all.1), custom_call_target="tpu_custom_call" | custom-call | tf_op jit(solution)/shard_map/pack/pallas_call | solution.py:356
  2.6 0.0 copy-start.3
  2.6 0.0 copy-start
  2.6 0.0 copy-start.1
  2.6 0.0 copy-start.2
  2.6 0.0 copy-start.4
  2.6 6.1 %all-to-all-start = ((bf16[8,10,56,128]{3,2,1,0:T(8,128)(2,1)}), bf16[8,10,56,128]{3,2,1,0:T(8,128)(2,1)S(1)}, u32[]{:S(2)}, u32[]{:S(2)}) async-start(bf16[8,10,56,128]{3,2,1,0:T(8,128)(2,1)} %pack.1), calls=%async_computation | async-start | bytes 2293760 | tf_op jit(solution)/shard_map/all_to_all | solution.py:371
  8.7 0.0 copy-done.3
  8.7 5.2 %collective-permute-start = (s32[16,256]{1,0:T(8,128)S(1)}, s32[16,256]{1,0:T(8,128)S(1)}, u32[]{:S(2)}, u32[]{:S(2)}) collective-permute-start(s32[16,256]{1,0:T(8,128)S(1)} %copy-done.3), channel_id=1, source_target_pairs={{0,63},{1,34},{2,33},{3,36},{4,35},{5,38},{6,37},{7,40},{8,39},{9,... | collective-permute-start | bytes 49160 | tf_op jit(solution)/shard_map/ppermute | solution.py:35
  13.9 0.0 collective-permute-start.1
  13.9 1.4 %collective-permute-done.cross_ref = s32[16,256]{1,0:T(8,128)S(1)} collective-permute-done((s32[16,256]{1,0:T(8,128)S(1)}, s32[16,256]{1,0:T(8,128)S(1)}, u32[]{:S(2)}, u32[]{:S(2)}) %collective-permute-start) | collective-permute-done | bytes 16416 | tf_op jit(solution)/shard_map/ppermute | solution.py:35
  15.4 0.0 collective-permute-done.1.chip_ref
  15.4 0.0 copy-done
  15.4 0.0 copy-done.1
  15.4 0.0 copy-done.2
  15.4 0.0 copy-done.4
  15.4 4.5 %weights.1 = (f32[2360,128]{1,0:T(8,128)S(1)}, f32[96,128]{1,0:T(8,128)S(1)}, s32[56,128]{1,0:T(8,128)S(4)}, s32[3,256]{1,0:T(4,128)S(4)}) custom-call(s32[384]{0:T(512)S(1)} %copy-done.4, s32[16,256]{1,0:T(8,128)S(1)} %collective-permute-done.cross_ref, s32[16,256]{1,0:T(8,128)S(1)} %copy-done.3, s32[16,256]{1,0:T(8,128)S(1)} %collective-permute-done.1.chip_ref, ...), custom_call_target="tpu_custom_call" | custom-call | tf_op jit(solution)/shard_map/weights/pallas_call | solution.py:377
  19.9 4.4 %all-to-all-done = bf16[8,10,56,128]{3,2,1,0:T(8,128)(2,1)S(1)} async-done(((bf16[8,10,56,128]{3,2,1,0:T(8,128)(2,1)}), bf16[8,10,56,128]{3,2,1,0:T(8,128)(2,1)S(1)}, u32[]{:S(2)}, u32[]{:S(2)}) %all-to-all-start) | async-done | bytes 1146912 | tf_op jit(solution)/shard_map/all_to_all | solution.py:371
  24.3 4.8 %cross.1 = (bf16[49,96,128]{2,1,0:T(8,128)(2,1)S(1)}, bf16[640,128]{1,0:T(8,128)(2,1)S(1)}, bf16[640,128]{1,0:T(8,128)(2,1)S(1)}) custom-call(s32[56,128]{1,0:T(8,128)S(4)} %get-tuple-element.14.list_ref, s32[3,256]{1,0:T(4,128)S(4)} %get-tuple-element.15.item_ref, bf16[80,56,128]{2,1,0:T(8,128)(2,1)S(1)} %bitcast.3, ...), custom_call_target="tpu_custom_call" | custom-call | tf_op jit(solution)/shard_map/cross/pallas_call | solution.py:399
  29.1 0.1 collective-permute-start.3
  29.2 7.3 %collective-permute-start.2 = (bf16[640,128]{1,0:T(8,128)(2,1)S(1)}, bf16[640,128]{1,0:T(8,128)(2,1)S(1)}, u32[]{:S(2)}, u32[]{:S(2)}) collective-permute-start(bf16[640,128]{1,0:T(8,128)(2,1)S(1)} %get-tuple-element.19), channel_id=1, source_target_pairs={{0,63},{1,34},{2,33},{3,36},{4,35},{5,38},{6,37},{7,40},{8,39},{9,... | collective-permute-start | bytes 491528 | tf_op jit(solution)/shard_map/ppermute | solution.py:35
  36.5 2.3 %shard_map.73.own_ref = f32[640,128]{1,0:T(8,128)S(1)} custom-call(s32[56,128]{1,0:T(8,128)S(4)} %get-tuple-element.14.list_ref, s32[3,256]{1,0:T(4,128)S(4)} %get-tuple-element.15.item_ref, bf16[49,96,128]{2,1,0:T(8,128)(2,1)S(1)} %get-tuple-element.18.d_ref, f32[2360,128]{1,0:T(8,128)S(1)} %get-tuple-element.17.w_ref), custom_call_target="tpu_custom_call" | custom-call | tf_op jit(solution)/shard_map/pallas_call | solution.py:414
  38.8 0.0 collective-permute-done.3.high_ref
  38.8 0.7 %collective-permute-done.2.low_ref = bf16[640,128]{1,0:T(8,128)(2,1)S(1)} collective-permute-done((bf16[640,128]{1,0:T(8,128)(2,1)S(1)}, bf16[640,128]{1,0:T(8,128)(2,1)S(1)}, u32[]{:S(2)}, u32[]{:S(2)}) %collective-permute-start.2) | collective-permute-done | bytes 163872 | tf_op jit(solution)/shard_map/ppermute | solution.py:35
  39.5 0.7 %merge.1 = bf16[640,128]{1,0:T(8,128)(2,1)} custom-call(f32[640,128]{1,0:T(8,128)S(1)} %shard_map.73.own_ref, bf16[640,128]{1,0:T(8,128)(2,1)S(1)} %collective-permute-done.2.low_ref, bf16[640,128]{1,0:T(8,128)(2,1)S(1)} %collective-permute-done.3.high_ref), custom_call_target="tpu_custom_call" | custom-call | tf_op jit(solution)/shard_map/merge/pallas_call | solution.py:426
  40.2 4.7 %all-to-all-start.1 = ((bf16[8,80,128]{2,1,0:T(8,128)(2,1)}), bf16[8,80,128]{2,1,0:T(8,128)(2,1)S(1)}, u32[]{:S(2)}, u32[]{:S(2)}) async-start(bf16[8,80,128]{2,1,0:T(8,128)(2,1)} %bitcast.1), calls=%async_computation.1 | async-start | bytes 327680 | tf_op jit(solution)/shard_map/all_to_all | solution.py:435
  45.0 0.2 state.1
  45.1 5.4 %all-to-all-done.1.system_ref = bf16[8,80,128]{2,1,0:T(8,128)(2,1)S(1)} async-done(((bf16[8,80,128]{2,1,0:T(8,128)(2,1)}), bf16[8,80,128]{2,1,0:T(8,128)(2,1)S(1)}, u32[]{:S(2)}, u32[]{:S(2)}) %all-to-all-start.1) | async-done | bytes 163872 | tf_op jit(solution)/shard_map/all_to_all | solution.py:435
  50.6 1.9 %finish.1 = bf16[640,128]{1,0:T(8,128)(2,1)S(1)} custom-call(bf16[8,80,128]{2,1,0:T(8,128)(2,1)S(1)} %all-to-all-done.1.system_ref, bf16[80,1024]{1,0:T(8,128)(2,1)S(1)} %get-tuple-element.21.dev_ref, f32[8,128]{1,0:T(8,128)S(1)} %get-tuple-element.22.mean_ref), custom_call_target="tpu_custom_call" | custom-call | tf_op jit(solution)/shard_map/finish/pallas_call | solution.py:448
  52.5 9.3 %all_to_all.15.part_ref = bf16[8,10,8,128]{3,2,1,0:T(8,128)(2,1)S(1)} all-to-all(bf16[8,10,8,128]{3,2,1,0:T(8,128)(2,1)S(1)} %bitcast.5), channel_id=1, replica_groups=mesh['mem'=8,'grid'=32] {'mem'}, dimensions={0} | all-to-all | bytes 327680 | tf_op jit(solution)/shard_map/all_to_all | solution.py:458
  61.7 0.8 %unpack.1 = bf16[10,16,512]{2,1,0:T(8,128)(2,1)} custom-call(bf16[8,10,8,128]{3,2,1,0:T(8,128)(2,1)S(1)} %all_to_all.15.part_ref), custom_call_target="tpu_custom_call" | custom-call | tf_op jit(solution)/shard_map/unpack/pallas_call | solution.py:459
  (1 shorter events, 0.0 us)
Async XLA Ops:
  2.6 6.1 %copy-start.3 = (s32[16,256]{1,0:T(8,128)S(1)}, s32[16,256]{1,0:T(8,128)}, u32[]{:S(2)}) copy-start(s32[16,256]{1,0:T(8,128)} %mid_ref.1) | copy-start | bytes 49156
  2.6 12.8 %copy-start = (f32[384,128]{1,0:T(8,128)S(1)}, f32[384,128]{1,0:T(8,128)}, u32[]{:S(2)}) copy-start(f32[384,128]{1,0:T(8,128)} %prec_all.1) | copy-start | bytes 589828
  2.6 12.8 %copy-start.1 = (f32[384,128]{1,0:T(8,128)S(1)}, f32[384,128]{1,0:T(8,128)}, u32[]{:S(2)}) copy-start(f32[384,128]{1,0:T(8,128)} %pos_all.1) | copy-start | bytes 589828
  2.6 12.8 %copy-start.2 = (f32[384,128]{1,0:T(8,128)S(1)}, f32[384,128]{1,0:T(8,128)}, u32[]{:S(2)}) copy-start(f32[384,128]{1,0:T(8,128)} %value_all.1) | copy-start | bytes 589828
  2.6 12.8 %copy-start.4 = (s32[384]{0:T(512)S(1)}, s32[384]{0:T(512)}, u32[]{:S(2)}) copy-start(s32[384]{0:T(512)} %len_ref.1) | copy-start | bytes 4612
  2.6 21.7 %all-to-all-start = ((bf16[8,10,56,128]{3,2,1,0:T(8,128)(2,1)}), bf16[8,10,56,128]{3,2,1,0:T(8,128)(2,1)S(1)}, u32[]{:S(2)}, u32[]{:S(2)}) async-start(bf16[8,10,56,128]{3,2,1,0:T(8,128)(2,1)} %pack.1), calls=%async_computation | async-start | bytes 2293760 | tf_op jit(solution)/shard_map/all_to_all | solution.py:371
  8.7 6.7 %collective-permute-start = (s32[16,256]{1,0:T(8,128)S(1)}, s32[16,256]{1,0:T(8,128)S(1)}, u32[]{:S(2)}, u32[]{:S(2)}) collective-permute-start(s32[16,256]{1,0:T(8,128)S(1)} %copy-done.3), channel_id=1, source_target_pairs={{0,63},{1,34},{2,33},{3,36},{4,35},{5,38},{6,37},{7,40},{8,39},{9,... | collective-permute-start | bytes 49160 | tf_op jit(solution)/shard_map/ppermute | solution.py:35
  13.9 1.4 %collective-permute-start.1 = (s32[16,256]{1,0:T(8,128)S(1)}, s32[16,256]{1,0:T(8,128)S(1)}, u32[]{:S(2)}, u32[]{:S(2)}) collective-permute-start(s32[16,256]{1,0:T(8,128)S(1)} %copy-done.3), channel_id=1, source_target_pairs={{0,1},{1,0},{2,3},{3,2},{4,5},{5,4},{6,7},{7,6},{8,9},{9,8},{10,11... | collective-permute-start | bytes 49160 | tf_op jit(solution)/shard_map/ppermute | solution.py:35
  29.1 9.7 %collective-permute-start.3 = (bf16[640,128]{1,0:T(8,128)(2,1)S(1)}, bf16[640,128]{1,0:T(8,128)(2,1)S(1)}, u32[]{:S(2)}, u32[]{:S(2)}) collective-permute-start(bf16[640,128]{1,0:T(8,128)(2,1)S(1)} %shard_map.74), channel_id=1, source_target_pairs={{0,1},{1,0},{2,3},{3,2},{4,5},{5,4},{6,7},{7,6},{8,9},{9,8},{10,11... | collective-permute-start | bytes 491528 | tf_op jit(solution)/shard_map/ppermute | solution.py:35
  29.2 10.3 %collective-permute-start.2 = (bf16[640,128]{1,0:T(8,128)(2,1)S(1)}, bf16[640,128]{1,0:T(8,128)(2,1)S(1)}, u32[]{:S(2)}, u32[]{:S(2)}) collective-permute-start(bf16[640,128]{1,0:T(8,128)(2,1)S(1)} %get-tuple-element.19), channel_id=1, source_target_pairs={{0,63},{1,34},{2,33},{3,36},{4,35},{5,38},{6,37},{7,40},{8,39},{9,... | collective-permute-start | bytes 491528 | tf_op jit(solution)/shard_map/ppermute | solution.py:35
  40.2 10.3 %all-to-all-start.1 = ((bf16[8,80,128]{2,1,0:T(8,128)(2,1)}), bf16[8,80,128]{2,1,0:T(8,128)(2,1)S(1)}, u32[]{:S(2)}, u32[]{:S(2)}) async-start(bf16[8,80,128]{2,1,0:T(8,128)(2,1)} %bitcast.1), calls=%async_computation.1 | async-start | bytes 327680 | tf_op jit(solution)/shard_map/all_to_all | solution.py:435

commit v13 on v12

--- a/solution.py
+++ b/solution.py
@@ -136,6 +136,11 @@
         item_ref[group, ROOM - 1] = at
 
 
+def early_chip(place):
+    last = lax.axis_size("grid") - 1
+    return (place == 0) | ((lax.rem(place, 2) == 1) & (place != last))
+
+
 def accumulate(members, obs, group, blocks, list_ref, item_ref, d_ref, w_ref, acc_ref):
     rows = d_ref.shape[1]
     acc_ref[...] = jnp.zeros(acc_ref.shape, jnp.float32)
@@ -202,7 +207,7 @@
     accumulate(members, obs, group, blocks, list_ref, item_ref, d_ref, w_ref, acc_ref)
     packed_system(members, blocks, acc_ref, out_ref)
 
-    @pl.when(place == 0)
+    @pl.when(early_chip(place))
     def _():
         accumulate(members, obs, 2 - group, blocks, list_ref, item_ref, d_ref, w_ref, acc_ref)
         packed_system(members, blocks, acc_ref, early_ref)
@@ -211,11 +216,11 @@
 def chip_kernel(members, obs, blocks, list_ref, item_ref, d_ref, w_ref, early_ref, out_ref, acc_ref):
     place = lax.axis_index("grid")
 
-    @pl.when(place == 0)
+    @pl.when(early_chip(place))
     def _():
         out_ref[...] = early_ref[...]
 
-    @pl.when(place != 0)
+    @pl.when(jnp.logical_not(early_chip(place)))
     def _():
         group = 2 - 2 * lax.rem(place, 2)
         accumulate(members, obs, group, blocks, list_ref, item_ref, d_ref, w_ref, acc_ref)

time: 62.8 us -> 62.8 us (level)
  no operation moved by 1% of the time
where the time goes in v13:
time: 62.8 us; the launch traced here: 62.5 us
  starting transfers between devices  23.4 us (37%)
  Pallas kernels  17.7 us (28%)
  waiting for transfers between devices  12 us (19%)
  blocking collectives  9.27 us (15%)
    ppermute x4, starting transfers between devices, swap(): return lax.ppermute(value, ('mem', 'grid'), pairs)  12.5 us
    all_to_all x1, blocking collectives, per_device(): lax.all_to_all(analysis, 'mem', split_axis=0, concat_axis=0, tiled=True)  9.27 us
    all_to_all x1, starting transfers between devices, per_device(): lax.all_to_all(packed, 'mem', split_axis=0, concat_axis=0, tiled=True)  6.07 us
    all_to_all x1, waiting for transfers between devices, per_device(): lax.all_to_all(partial, 'mem', split_axis=0, concat_axis=0, tiled=True)  5.45 us
    all_to_all x1, starting transfers between devices, per_device(): lax.all_to_all(partial, 'mem', split_axis=0, concat_axis=0, tiled=True)  4.84 us
    pallas_call x1, Pallas kernels, per_device(): pl.pallas_call(functools.partial(cross_kernel, members, obs, blocks_dev),...  4.79 us
    pallas_call x1, Pallas kernels, per_device(): pl.pallas_call(functools.partial(weight_kernel, float(nb_total), obs), ou...  4.52 us
    all_to_all x1, waiting for transfers between devices, per_device(): lax.all_to_all(packed, 'mem', split_axis=0, concat_axis=0, tiled=True)  4.38 us
  transfers between devices with their start and end apart: 6, of which 4 were waited for; matrix products, arithmetic and copies ran while one was open for 0% of the time, Pallas kernels for 11%

profile of v13, /device:TPU:2, one launch (start us, length us, event | category | flops | bytes accessed | tf_op | source)
XLA Modules:
  0.0 62.5 jit_solution(16317262000209871153)
XLA Ops:
  0.0 2.6 %pack.1 = bf16[8,10,56,128]{3,2,1,0:T(8,128)(2,1)} custom-call(bf16[10,384,128]{2,1,0:T(8,128)(2,1)} %src_ref.1, bf16[10,16,512]{2,1,0:T(8,128)(2,1)} %state_all.1), custom_call_target="tpu_custom_call" | custom-call | tf_op jit(solution)/shard_map/pack/pallas_call | solution.py:361
  2.6 0.0 copy-start.3
  2.6 0.0 copy-start
  2.6 0.0 copy-start.1
  2.6 0.0 copy-start.2
  2.6 0.0 copy-start.4
  2.6 6.1 %all-to-all-start = ((bf16[8,10,56,128]{3,2,1,0:T(8,128)(2,1)}), bf16[8,10,56,128]{3,2,1,0:T(8,128)(2,1)S(1)}, u32[]{:S(2)}, u32[]{:S(2)}) async-start(bf16[8,10,56,128]{3,2,1,0:T(8,128)(2,1)} %pack.1), calls=%async_computation | async-start | bytes 2293760 | tf_op jit(solution)/shard_map/all_to_all | solution.py:376
  8.7 0.0 copy-done.3
  8.7 5.2 %collective-permute-start = (s32[16,256]{1,0:T(8,128)S(1)}, s32[16,256]{1,0:T(8,128)S(1)}, u32[]{:S(2)}, u32[]{:S(2)}) collective-permute-start(s32[16,256]{1,0:T(8,128)S(1)} %copy-done.3), channel_id=1, source_target_pairs={{0,63},{1,34},{2,33},{3,36},{4,35},{5,38},{6,37},{7,40},{8,39},{9,... | collective-permute-start | bytes 49160 | tf_op jit(solution)/shard_map/ppermute | solution.py:35
  13.9 0.0 collective-permute-start.1
  13.9 1.4 %collective-permute-done.cross_ref = s32[16,256]{1,0:T(8,128)S(1)} collective-permute-done((s32[16,256]{1,0:T(8,128)S(1)}, s32[16,256]{1,0:T(8,128)S(1)}, u32[]{:S(2)}, u32[]{:S(2)}) %collective-permute-start) | collective-permute-done | bytes 16416 | tf_op jit(solution)/shard_map/ppermute | solution.py:35
  15.4 0.0 collective-permute-done.1.chip_ref
  15.4 0.0 copy-done
  15.4 0.0 copy-done.1
  15.4 0.0 copy-done.2
  15.4 0.0 copy-done.4
  15.4 4.5 %weights.1 = (f32[2360,128]{1,0:T(8,128)S(1)}, f32[96,128]{1,0:T(8,128)S(1)}, s32[56,128]{1,0:T(8,128)S(4)}, s32[3,256]{1,0:T(4,128)S(4)}) custom-call(s32[384]{0:T(512)S(1)} %copy-done.4, s32[16,256]{1,0:T(8,128)S(1)} %collective-permute-done.cross_ref, s32[16,256]{1,0:T(8,128)S(1)} %copy-done.3, s32[16,256]{1,0:T(8,128)S(1)} %collective-permute-done.1.chip_ref, ...), custom_call_target="tpu_custom_call" | custom-call | tf_op jit(solution)/shard_map/weights/pallas_call | solution.py:382
  19.9 4.4 %all-to-all-done = bf16[8,10,56,128]{3,2,1,0:T(8,128)(2,1)S(1)} async-done(((bf16[8,10,56,128]{3,2,1,0:T(8,128)(2,1)}), bf16[8,10,56,128]{3,2,1,0:T(8,128)(2,1)S(1)}, u32[]{:S(2)}, u32[]{:S(2)}) %all-to-all-start) | async-done | bytes 1146912 | tf_op jit(solution)/shard_map/all_to_all | solution.py:376
  24.3 4.8 %cross.1 = (bf16[49,96,128]{2,1,0:T(8,128)(2,1)S(1)}, bf16[640,128]{1,0:T(8,128)(2,1)S(1)}, bf16[640,128]{1,0:T(8,128)(2,1)S(1)}) custom-call(s32[56,128]{1,0:T(8,128)S(4)} %get-tuple-element.14.list_ref, s32[3,256]{1,0:T(4,128)S(4)} %get-tuple-element.15.item_ref, bf16[80,56,128]{2,1,0:T(8,128)(2,1)S(1)} %bitcast.3, ...), custom_call_target="tpu_custom_call" | custom-call | tf_op jit(solution)/shard_map/cross/pallas_call | solution.py:404
  29.1 0.1 collective-permute-start.3
  29.2 7.2 %collective-permute-start.2 = (bf16[640,128]{1,0:T(8,128)(2,1)S(1)}, bf16[640,128]{1,0:T(8,128)(2,1)S(1)}, u32[]{:S(2)}, u32[]{:S(2)}) collective-permute-start(bf16[640,128]{1,0:T(8,128)(2,1)S(1)} %get-tuple-element.19), channel_id=1, source_target_pairs={{0,63},{1,34},{2,33},{3,36},{4,35},{5,38},{6,37},{7,40},{8,39},{9,... | collective-permute-start | bytes 491528 | tf_op jit(solution)/shard_map/ppermute | solution.py:35
  36.4 2.3 %shard_map.73.own_ref = f32[640,128]{1,0:T(8,128)S(1)} custom-call(s32[56,128]{1,0:T(8,128)S(4)} %get-tuple-element.14.list_ref, s32[3,256]{1,0:T(4,128)S(4)} %get-tuple-element.15.item_ref, bf16[49,96,128]{2,1,0:T(8,128)(2,1)S(1)} %get-tuple-element.18.d_ref, f32[2360,128]{1,0:T(8,128)S(1)} %get-tuple-element.17.w_ref), custom_call_target="tpu_custom_call" | custom-call | tf_op jit(solution)/shard_map/pallas_call | solution.py:419
  38.7 0.0 collective-permute-done.3.high_ref
  38.8 0.7 %collective-permute-done.2.low_ref = bf16[640,128]{1,0:T(8,128)(2,1)S(1)} collective-permute-done((bf16[640,128]{1,0:T(8,128)(2,1)S(1)}, bf16[640,128]{1,0:T(8,128)(2,1)S(1)}, u32[]{:S(2)}, u32[]{:S(2)}) %collective-permute-start.2) | collective-permute-done | bytes 163872 | tf_op jit(solution)/shard_map/ppermute | solution.py:35
  39.4 0.7 %merge.1 = bf16[640,128]{1,0:T(8,128)(2,1)} custom-call(f32[640,128]{1,0:T(8,128)S(1)} %shard_map.73.own_ref, bf16[640,128]{1,0:T(8,128)(2,1)S(1)} %collective-permute-done.2.low_ref, bf16[640,128]{1,0:T(8,128)(2,1)S(1)} %collective-permute-done.3.high_ref), custom_call_target="tpu_custom_call" | custom-call | tf_op jit(solution)/shard_map/merge/pallas_call | solution.py:431
  40.2 4.8 %all-to-all-start.1 = ((bf16[8,80,128]{2,1,0:T(8,128)(2,1)}), bf16[8,80,128]{2,1,0:T(8,128)(2,1)S(1)}, u32[]{:S(2)}, u32[]{:S(2)}) async-start(bf16[8,80,128]{2,1,0:T(8,128)(2,1)} %bitcast.1), calls=%async_computation.1 | async-start | bytes 327680 | tf_op jit(solution)/shard_map/all_to_all | solution.py:440
  45.0 0.2 state.1
  45.2 5.4 %all-to-all-done.1.system_ref = bf16[8,80,128]{2,1,0:T(8,128)(2,1)S(1)} async-done(((bf16[8,80,128]{2,1,0:T(8,128)(2,1)}), bf16[8,80,128]{2,1,0:T(8,128)(2,1)S(1)}, u32[]{:S(2)}, u32[]{:S(2)}) %all-to-all-start.1) | async-done | bytes 163872 | tf_op jit(solution)/shard_map/all_to_all | solution.py:440
  50.6 1.9 %finish.1 = bf16[640,128]{1,0:T(8,128)(2,1)S(1)} custom-call(bf16[8,80,128]{2,1,0:T(8,128)(2,1)S(1)} %all-to-all-done.1.system_ref, bf16[80,1024]{1,0:T(8,128)(2,1)S(1)} %get-tuple-element.21.dev_ref, f32[8,128]{1,0:T(8,128)S(1)} %get-tuple-element.22.mean_ref), custom_call_target="tpu_custom_call" | custom-call | tf_op jit(solution)/shard_map/finish/pallas_call | solution.py:453
  52.5 9.3 %all_to_all.15.part_ref = bf16[8,10,8,128]{3,2,1,0:T(8,128)(2,1)S(1)} all-to-all(bf16[8,10,8,128]{3,2,1,0:T(8,128)(2,1)S(1)} %bitcast.5), channel_id=1, replica_groups=mesh['mem'=8,'grid'=32] {'mem'}, dimensions={0} | all-to-all | bytes 327680 | tf_op jit(solution)/shard_map/all_to_all | solution.py:463
  61.8 0.8 %unpack.1 = bf16[10,16,512]{2,1,0:T(8,128)(2,1)} custom-call(bf16[8,10,8,128]{3,2,1,0:T(8,128)(2,1)S(1)} %all_to_all.15.part_ref), custom_call_target="tpu_custom_call" | custom-call | tf_op jit(solution)/shard_map/unpack/pallas_call | solution.py:464
  (1 shorter events, 0.0 us)
Async XLA Ops:
  2.6 6.1 %copy-start.3 = (s32[16,256]{1,0:T(8,128)S(1)}, s32[16,256]{1,0:T(8,128)}, u32[]{:S(2)}) copy-start(s32[16,256]{1,0:T(8,128)} %mid_ref.1) | copy-start | bytes 49156
  2.6 12.8 %copy-start = (f32[384,128]{1,0:T(8,128)S(1)}, f32[384,128]{1,0:T(8,128)}, u32[]{:S(2)}) copy-start(f32[384,128]{1,0:T(8,128)} %prec_all.1) | copy-start | bytes 589828
  2.6 12.8 %copy-start.1 = (f32[384,128]{1,0:T(8,128)S(1)}, f32[384,128]{1,0:T(8,128)}, u32[]{:S(2)}) copy-start(f32[384,128]{1,0:T(8,128)} %pos_all.1) | copy-start | bytes 589828
  2.6 12.8 %copy-start.2 = (f32[384,128]{1,0:T(8,128)S(1)}, f32[384,128]{1,0:T(8,128)}, u32[]{:S(2)}) copy-start(f32[384,128]{1,0:T(8,128)} %value_all.1) | copy-start | bytes 589828
  2.6 12.8 %copy-start.4 = (s32[384]{0:T(512)S(1)}, s32[384]{0:T(512)}, u32[]{:S(2)}) copy-start(s32[384]{0:T(512)} %len_ref.1) | copy-start | bytes 4612
  2.6 21.7 %all-to-all-start = ((bf16[8,10,56,128]{3,2,1,0:T(8,128)(2,1)}), bf16[8,10,56,128]{3,2,1,0:T(8,128)(2,1)S(1)}, u32[]{:S(2)}, u32[]{:S(2)}) async-start(bf16[8,10,56,128]{3,2,1,0:T(8,128)(2,1)} %pack.1), calls=%async_computation | async-start | bytes 2293760 | tf_op jit(solution)/shard_map/all_to_all | solution.py:376
  8.7 6.7 %collective-permute-start = (s32[16,256]{1,0:T(8,128)S(1)}, s32[16,256]{1,0:T(8,128)S(1)}, u32[]{:S(2)}, u32[]{:S(2)}) collective-permute-start(s32[16,256]{1,0:T(8,128)S(1)} %copy-done.3), channel_id=1, source_target_pairs={{0,63},{1,34},{2,33},{3,36},{4,35},{5,38},{6,37},{7,40},{8,39},{9,... | collective-permute-start | bytes 49160 | tf_op jit(solution)/shard_map/ppermute | solution.py:35
  13.9 1.4 %collective-permute-start.1 = (s32[16,256]{1,0:T(8,128)S(1)}, s32[16,256]{1,0:T(8,128)S(1)}, u32[]{:S(2)}, u32[]{:S(2)}) collective-permute-start(s32[16,256]{1,0:T(8,128)S(1)} %copy-done.3), channel_id=1, source_target_pairs={{0,1},{1,0},{2,3},{3,2},{4,5},{5,4},{6,7},{7,6},{8,9},{9,8},{10,11... | collective-permute-start | bytes 49160 | tf_op jit(solution)/shard_map/ppermute | solution.py:35
  29.1 9.6 %collective-permute-start.3 = (bf16[640,128]{1,0:T(8,128)(2,1)S(1)}, bf16[640,128]{1,0:T(8,128)(2,1)S(1)}, u32[]{:S(2)}, u32[]{:S(2)}) collective-permute-start(bf16[640,128]{1,0:T(8,128)(2,1)S(1)} %shard_map.74), channel_id=1, source_target_pairs={{0,1},{1,0},{2,3},{3,2},{4,5},{5,4},{6,7},{7,6},{8,9},{9,8},{10,11... | collective-permute-start | bytes 491528 | tf_op jit(solution)/shard_map/ppermute | solution.py:35
  29.2 10.2 %collective-permute-start.2 = (bf16[640,128]{1,0:T(8,128)(2,1)S(1)}, bf16[640,128]{1,0:T(8,128)(2,1)S(1)}, u32[]{:S(2)}, u32[]{:S(2)}) collective-permute-start(bf16[640,128]{1,0:T(8,128)(2,1)S(1)} %get-tuple-element.19), channel_id=1, source_target_pairs={{0,63},{1,34},{2,33},{3,36},{4,35},{5,38},{6,37},{7,40},{8,39},{9,... | collective-permute-start | bytes 491528 | tf_op jit(solution)/shard_map/ppermute | solution.py:35
  40.2 10.5 %all-to-all-start.1 = ((bf16[8,80,128]{2,1,0:T(8,128)(2,1)}), bf16[8,80,128]{2,1,0:T(8,128)(2,1)S(1)}, u32[]{:S(2)}, u32[]{:S(2)}) async-start(bf16[8,80,128]{2,1,0:T(8,128)(2,1)} %bitcast.1), calls=%async_computation.1 | async-start | bytes 327680 | tf_op jit(solution)/shard_map/all_to_all | solution.py:440

commit v14 on v13

--- a/solution.py
+++ b/solution.py
@@ -138,7 +138,7 @@
 
 def early_chip(place):
     last = lax.axis_size("grid") - 1
-    return (place == 0) | ((lax.rem(place, 2) == 1) & (place != last))
+    return place != last
 
 
 def accumulate(members, obs, group, blocks, list_ref, item_ref, d_ref, w_ref, acc_ref):
@@ -198,7 +198,7 @@
     high = departure.astype(jnp.bfloat16).astype(jnp.float32)
     dev_ref[members * PITCH : members * PITCH + obs, :] = high
     dev_ref[(members + 1) * PITCH : (members + 1) * PITCH + obs, :] = departure - high
-    dev_ref[(members + 2) * PITCH :, :] = jnp.zeros(((rows - members - 2) * PITCH, LANES), jnp.float32)
+    dev_ref[(members + 2) * PITCH :, :] = jnp.zeros((dev_ref.shape[0] - (members + 2) * PITCH, LANES), jnp.float32)
     for o in range(obs):
         d_ref[o] = dev_ref[pl.ds(o, rows, stride=PITCH), :].astype(jnp.bfloat16)
     d_ref[obs] = jnp.zeros((rows, LANES), jnp.bfloat16)
@@ -315,7 +315,7 @@
                 turned, dev_ref[:, k * LANES : (k + 1) * LANES], preferred_element_type=jnp.float32
             )
             wide_ref[pl.ds(k, members, stride=rows_out), :] = mean_ref[k : k + 1, :] + moved
-    out_ref[...] = wide_ref[...].astype(jnp.bfloat16)
+    out_ref[...] = wide_ref[0 : out_ref.shape[0], :].astype(jnp.bfloat16)
 
 
 def unpack_kernel(owned, part_ref, out_ref):
@@ -407,7 +407,7 @@
         in_specs=[scalars, scalars, vmem, vmem, vmem],
         out_specs=(vmem, vmem, vmem),
         scratch_shapes=[
-            pltpu.VMEM((rows * PITCH, LANES), jnp.float32),
+            pltpu.VMEM((rows * PITCH + 56, LANES), jnp.float32),
             pltpu.VMEM(((blocks_dev + 1) * members, LANES), jnp.float32),
         ],
         compiler_params=pltpu.CompilerParams(vmem_limit_bytes=16 * 2**20),
@@ -446,7 +446,7 @@
         ),
         in_specs=[vmem],
         out_specs=(vmem, vmem),
-        scratch_shapes=[pltpu.VMEM((members * extra, LANES), jnp.float32)],
+        scratch_shapes=[pltpu.VMEM((members * extra + extra, LANES), jnp.float32)],
         compiler_params=pltpu.CompilerParams(vmem_limit_bytes=16 * 2**20),
         name="state",
     )(near(prior))
@@ -455,7 +455,7 @@
         out_shape=pltpu.VMEM((members * extra, LANES), jnp.bfloat16),
         in_specs=[vmem, vmem, vmem],
         out_specs=vmem,
-        scratch_shapes=[pltpu.VMEM((members * extra, LANES), jnp.float32)],
+        scratch_shapes=[pltpu.VMEM((members * extra + extra, LANES), jnp.float32)],
         compiler_params=pltpu.CompilerParams(vmem_limit_bytes=16 * 2**20),
         name="finish",
     )(near(swapped), near(deviation), near(mean))

time: 62.8 us -> 62.8 us (level)
  no operation moved by 1% of the time
where the time goes in v14:
time: 62.8 us; the launch traced here: 62.5 us
  starting transfers between devices  23.3 us (37%)
  Pallas kernels  17.8 us (28%)
  waiting for transfers between devices  12 us (19%)
  blocking collectives  9.27 us (15%)
    ppermute x4, starting transfers between devices, swap(): return lax.ppermute(value, ('mem', 'grid'), pairs)  12.5 us
    all_to_all x1, blocking collectives, per_device(): lax.all_to_all(analysis, 'mem', split_axis=0, concat_axis=0, tiled=True)  9.27 us
    all_to_all x1, starting transfers between devices, per_device(): lax.all_to_all(packed, 'mem', split_axis=0, concat_axis=0, tiled=True)  6.07 us
    all_to_all x1, waiting for transfers between devices, per_device(): lax.all_to_all(partial, 'mem', split_axis=0, concat_axis=0, tiled=True)  5.45 us
    pallas_call x1, Pallas kernels, per_device(): pl.pallas_call(functools.partial(cross_kernel, members, obs, blocks_dev),...  4.94 us
    all_to_all x1, starting transfers between devices, per_device(): lax.all_to_all(partial, 'mem', split_axis=0, concat_axis=0, tiled=True)  4.78 us
    pallas_call x1, Pallas kernels, per_device(): pl.pallas_call(functools.partial(weight_kernel, float(nb_total), obs), ou...  4.52 us
    all_to_all x1, waiting for transfers between devices, per_device(): lax.all_to_all(packed, 'mem', split_axis=0, concat_axis=0, tiled=True)  4.38 us
  transfers between devices with their start and end apart: 6, of which 4 were waited for; matrix products, arithmetic and copies ran while one was open for 0% of the time, Pallas kernels for 11%

profile of v14, /device:TPU:2, one launch (start us, length us, event | category | flops | bytes accessed | tf_op | source)
XLA Modules:
  0.0 62.5 jit_solution(1354721552229844760)
XLA Ops:
  0.0 2.6 %pack.1 = bf16[8,10,56,128]{3,2,1,0:T(8,128)(2,1)} custom-call(bf16[10,384,128]{2,1,0:T(8,128)(2,1)} %src_ref.1, bf16[10,16,512]{2,1,0:T(8,128)(2,1)} %state_all.1), custom_call_target="tpu_custom_call" | custom-call | tf_op jit(solution)/shard_map/pack/pallas_call | solution.py:361
  2.6 0.0 copy-start.3
  2.6 0.0 copy-start
  2.6 0.0 copy-start.1
  2.6 0.0 copy-start.2
  2.6 0.0 copy-start.4
  2.6 6.1 %all-to-all-start = ((bf16[8,10,56,128]{3,2,1,0:T(8,128)(2,1)}), bf16[8,10,56,128]{3,2,1,0:T(8,128)(2,1)S(1)}, u32[]{:S(2)}, u32[]{:S(2)}) async-start(bf16[8,10,56,128]{3,2,1,0:T(8,128)(2,1)} %pack.1), calls=%async_computation | async-start | bytes 2293760 | tf_op jit(solution)/shard_map/all_to_all | solution.py:376
  8.7 0.0 copy-done.3
  8.7 5.2 %collective-permute-start = (s32[16,256]{1,0:T(8,128)S(1)}, s32[16,256]{1,0:T(8,128)S(1)}, u32[]{:S(2)}, u32[]{:S(2)}) collective-permute-start(s32[16,256]{1,0:T(8,128)S(1)} %copy-done.3), channel_id=1, source_target_pairs={{0,63},{1,34},{2,33},{3,36},{4,35},{5,38},{6,37},{7,40},{8,39},{9,... | collective-permute-start | bytes 49160 | tf_op jit(solution)/shard_map/ppermute | solution.py:35
  13.9 0.0 collective-permute-start.1
  13.9 1.4 %collective-permute-done.cross_ref = s32[16,256]{1,0:T(8,128)S(1)} collective-permute-done((s32[16,256]{1,0:T(8,128)S(1)}, s32[16,256]{1,0:T(8,128)S(1)}, u32[]{:S(2)}, u32[]{:S(2)}) %collective-permute-start) | collective-permute-done | bytes 16416 | tf_op jit(solution)/shard_map/ppermute | solution.py:35
  15.4 0.0 collective-permute-done.1.chip_ref
  15.4 0.0 copy-done
  15.4 0.0 copy-done.1
  15.4 0.0 copy-done.2
  15.4 0.0 copy-done.4
  15.4 4.5 %weights.1 = (f32[2360,128]{1,0:T(8,128)S(1)}, f32[96,128]{1,0:T(8,128)S(1)}, s32[56,128]{1,0:T(8,128)S(4)}, s32[3,256]{1,0:T(4,128)S(4)}) custom-call(s32[384]{0:T(512)S(1)} %copy-done.4, s32[16,256]{1,0:T(8,128)S(1)} %collective-permute-done.cross_ref, s32[16,256]{1,0:T(8,128)S(1)} %copy-done.3, s32[16,256]{1,0:T(8,128)S(1)} %collective-permute-done.1.chip_ref, ...), custom_call_target="tpu_custom_call" | custom-call | tf_op jit(solution)/shard_map/weights/pallas_call | solution.py:382
  19.9 4.4 %all-to-all-done = bf16[8,10,56,128]{3,2,1,0:T(8,128)(2,1)S(1)} async-done(((bf16[8,10,56,128]{3,2,1,0:T(8,128)(2,1)}), bf16[8,10,56,128]{3,2,1,0:T(8,128)(2,1)S(1)}, u32[]{:S(2)}, u32[]{:S(2)}) %all-to-all-start) | async-done | bytes 1146912 | tf_op jit(solution)/shard_map/all_to_all | solution.py:376
  24.3 4.9 %cross.1 = (bf16[49,96,128]{2,1,0:T(8,128)(2,1)S(1)}, bf16[640,128]{1,0:T(8,128)(2,1)S(1)}, bf16[640,128]{1,0:T(8,128)(2,1)S(1)}) custom-call(s32[56,128]{1,0:T(8,128)S(4)} %get-tuple-element.14.list_ref, s32[3,256]{1,0:T(4,128)S(4)} %get-tuple-element.15.item_ref, bf16[80,56,128]{2,1,0:T(8,128)(2,1)S(1)} %bitcast.3, ...), custom_call_target="tpu_custom_call" | custom-call | tf_op jit(solution)/shard_map/cross/pallas_call | solution.py:404
  29.3 0.1 collective-permute-start.3
  29.4 7.2 %collective-permute-start.2 = (bf16[640,128]{1,0:T(8,128)(2,1)S(1)}, bf16[640,128]{1,0:T(8,128)(2,1)S(1)}, u32[]{:S(2)}, u32[]{:S(2)}) collective-permute-start(bf16[640,128]{1,0:T(8,128)(2,1)S(1)} %get-tuple-element.19), channel_id=1, source_target_pairs={{0,63},{1,34},{2,33},{3,36},{4,35},{5,38},{6,37},{7,40},{8,39},{9,... | collective-permute-start | bytes 491528 | tf_op jit(solution)/shard_map/ppermute | solution.py:35
  36.5 2.3 %shard_map.73.own_ref = f32[640,128]{1,0:T(8,128)S(1)} custom-call(s32[56,128]{1,0:T(8,128)S(4)} %get-tuple-element.14.list_ref, s32[3,256]{1,0:T(4,128)S(4)} %get-tuple-element.15.item_ref, bf16[49,96,128]{2,1,0:T(8,128)(2,1)S(1)} %get-tuple-element.18.d_ref, f32[2360,128]{1,0:T(8,128)S(1)} %get-tuple-element.17.w_ref), custom_call_target="tpu_custom_call" | custom-call | tf_op jit(solution)/shard_map/pallas_call | solution.py:419
  38.8 0.0 collective-permute-done.3.high_ref
  38.8 0.7 %collective-permute-done.2.low_ref = bf16[640,128]{1,0:T(8,128)(2,1)S(1)} collective-permute-done((bf16[640,128]{1,0:T(8,128)(2,1)S(1)}, bf16[640,128]{1,0:T(8,128)(2,1)S(1)}, u32[]{:S(2)}, u32[]{:S(2)}) %collective-permute-start.2) | collective-permute-done | bytes 163872 | tf_op jit(solution)/shard_map/ppermute | solution.py:35
  39.5 0.7 %merge.1 = bf16[640,128]{1,0:T(8,128)(2,1)} custom-call(f32[640,128]{1,0:T(8,128)S(1)} %shard_map.73.own_ref, bf16[640,128]{1,0:T(8,128)(2,1)S(1)} %collective-permute-done.2.low_ref, bf16[640,128]{1,0:T(8,128)(2,1)S(1)} %collective-permute-done.3.high_ref), custom_call_target="tpu_custom_call" | custom-call | tf_op jit(solution)/shard_map/merge/pallas_call | solution.py:431
  40.2 4.8 %all-to-all-start.1 = ((bf16[8,80,128]{2,1,0:T(8,128)(2,1)}), bf16[8,80,128]{2,1,0:T(8,128)(2,1)S(1)}, u32[]{:S(2)}, u32[]{:S(2)}) async-start(bf16[8,80,128]{2,1,0:T(8,128)(2,1)} %bitcast.1), calls=%async_computation.1 | async-start | bytes 327680 | tf_op jit(solution)/shard_map/all_to_all | solution.py:440
  45.0 0.2 state.1
  45.2 5.4 %all-to-all-done.1.system_ref = bf16[8,80,128]{2,1,0:T(8,128)(2,1)S(1)} async-done(((bf16[8,80,128]{2,1,0:T(8,128)(2,1)}), bf16[8,80,128]{2,1,0:T(8,128)(2,1)S(1)}, u32[]{:S(2)}, u32[]{:S(2)}) %all-to-all-start.1) | async-done | bytes 163872 | tf_op jit(solution)/shard_map/all_to_all | solution.py:440
  50.6 1.9 %finish.1 = bf16[640,128]{1,0:T(8,128)(2,1)S(1)} custom-call(bf16[8,80,128]{2,1,0:T(8,128)(2,1)S(1)} %all-to-all-done.1.system_ref, bf16[80,1024]{1,0:T(8,128)(2,1)S(1)} %get-tuple-element.21.dev_ref, f32[8,128]{1,0:T(8,128)S(1)} %get-tuple-element.22.mean_ref), custom_call_target="tpu_custom_call" | custom-call | tf_op jit(solution)/shard_map/finish/pallas_call | solution.py:453
  52.5 9.3 %all_to_all.15.part_ref = bf16[8,10,8,128]{3,2,1,0:T(8,128)(2,1)S(1)} all-to-all(bf16[8,10,8,128]{3,2,1,0:T(8,128)(2,1)S(1)} %bitcast.5), channel_id=1, replica_groups=mesh['mem'=8,'grid'=32] {'mem'}, dimensions={0} | all-to-all | bytes 327680 | tf_op jit(solution)/shard_map/all_to_all | solution.py:463
  61.8 0.8 %unpack.1 = bf16[10,16,512]{2,1,0:T(8,128)(2,1)} custom-call(bf16[8,10,8,128]{3,2,1,0:T(8,128)(2,1)S(1)} %all_to_all.15.part_ref), custom_call_target="tpu_custom_call" | custom-call | tf_op jit(solution)/shard_map/unpack/pallas_call | solution.py:464
  (1 shorter events, 0.0 us)
Async XLA Ops:
  2.6 6.1 %copy-start.3 = (s32[16,256]{1,0:T(8,128)S(1)}, s32[16,256]{1,0:T(8,128)}, u32[]{:S(2)}) copy-start(s32[16,256]{1,0:T(8,128)} %mid_ref.1) | copy-start | bytes 49156
  2.6 12.8 %copy-start = (f32[384,128]{1,0:T(8,128)S(1)}, f32[384,128]{1,0:T(8,128)}, u32[]{:S(2)}) copy-start(f32[384,128]{1,0:T(8,128)} %prec_all.1) | copy-start | bytes 589828
  2.6 12.8 %copy-start.1 = (f32[384,128]{1,0:T(8,128)S(1)}, f32[384,128]{1,0:T(8,128)}, u32[]{:S(2)}) copy-start(f32[384,128]{1,0:T(8,128)} %pos_all.1) | copy-start | bytes 589828
  2.6 12.8 %copy-start.2 = (f32[384,128]{1,0:T(8,128)S(1)}, f32[384,128]{1,0:T(8,128)}, u32[]{:S(2)}) copy-start(f32[384,128]{1,0:T(8,128)} %value_all.1) | copy-start | bytes 589828
  2.6 12.8 %copy-start.4 = (s32[384]{0:T(512)S(1)}, s32[384]{0:T(512)}, u32[]{:S(2)}) copy-start(s32[384]{0:T(512)} %len_ref.1) | copy-start | bytes 4612
  2.6 21.7 %all-to-all-start = ((bf16[8,10,56,128]{3,2,1,0:T(8,128)(2,1)}), bf16[8,10,56,128]{3,2,1,0:T(8,128)(2,1)S(1)}, u32[]{:S(2)}, u32[]{:S(2)}) async-start(bf16[8,10,56,128]{3,2,1,0:T(8,128)(2,1)} %pack.1), calls=%async_computation | async-start | bytes 2293760 | tf_op jit(solution)/shard_map/all_to_all | solution.py:376
  8.7 6.7 %collective-permute-start = (s32[16,256]{1,0:T(8,128)S(1)}, s32[16,256]{1,0:T(8,128)S(1)}, u32[]{:S(2)}, u32[]{:S(2)}) collective-permute-start(s32[16,256]{1,0:T(8,128)S(1)} %copy-done.3), channel_id=1, source_target_pairs={{0,63},{1,34},{2,33},{3,36},{4,35},{5,38},{6,37},{7,40},{8,39},{9,... | collective-permute-start | bytes 49160 | tf_op jit(solution)/shard_map/ppermute | solution.py:35
  13.9 1.4 %collective-permute-start.1 = (s32[16,256]{1,0:T(8,128)S(1)}, s32[16,256]{1,0:T(8,128)S(1)}, u32[]{:S(2)}, u32[]{:S(2)}) collective-permute-start(s32[16,256]{1,0:T(8,128)S(1)} %copy-done.3), channel_id=1, source_target_pairs={{0,1},{1,0},{2,3},{3,2},{4,5},{5,4},{6,7},{7,6},{8,9},{9,8},{10,11... | collective-permute-start | bytes 49160 | tf_op jit(solution)/shard_map/ppermute | solution.py:35
  29.3 9.6 %collective-permute-start.3 = (bf16[640,128]{1,0:T(8,128)(2,1)S(1)}, bf16[640,128]{1,0:T(8,128)(2,1)S(1)}, u32[]{:S(2)}, u32[]{:S(2)}) collective-permute-start(bf16[640,128]{1,0:T(8,128)(2,1)S(1)} %shard_map.74), channel_id=1, source_target_pairs={{0,1},{1,0},{2,3},{3,2},{4,5},{5,4},{6,7},{7,6},{8,9},{9,8},{10,11... | collective-permute-start | bytes 491528 | tf_op jit(solution)/shard_map/ppermute | solution.py:35
  29.4 10.2 %collective-permute-start.2 = (bf16[640,128]{1,0:T(8,128)(2,1)S(1)}, bf16[640,128]{1,0:T(8,128)(2,1)S(1)}, u32[]{:S(2)}, u32[]{:S(2)}) collective-permute-start(bf16[640,128]{1,0:T(8,128)(2,1)S(1)} %get-tuple-element.19), channel_id=1, source_target_pairs={{0,63},{1,34},{2,33},{3,36},{4,35},{5,38},{6,37},{7,40},{8,39},{9,... | collective-permute-start | bytes 491528 | tf_op jit(solution)/shard_map/ppermute | solution.py:35
  40.2 10.4 %all-to-all-start.1 = ((bf16[8,80,128]{2,1,0:T(8,128)(2,1)}), bf16[8,80,128]{2,1,0:T(8,128)(2,1)S(1)}, u32[]{:S(2)}, u32[]{:S(2)}) async-start(bf16[8,80,128]{2,1,0:T(8,128)(2,1)} %bitcast.1), calls=%async_computation.1 | async-start | bytes 327680 | tf_op jit(solution)/shard_map/all_to_all | solution.py:440
